TPU v7x, 32 devices: a whole 2x2x4 slice. The times are simulated.
32 devices in a mesh: leaf: 8 (over z, x), panel: 4 (over y, core).
Axes of the slice: x: 2, y: 2, z: 4, core: 2. Of those that a mesh axis runs over, the one named last changes fastest.
Arguments:
- adjoint_rhs: float32 [8, 64, 3840], P('leaf', None, 'panel'), may hold values from -6 to 6
- panel_tiles: bfloat16 [8, 2048, 8704], P('leaf', 'panel'), may hold values from -0.0625 to 0.0625
- diag_inverse: bfloat16 [8, 3840, 2048], P('leaf', 'panel'), may hold values from -0.125 to 0.125
- front_sizes: int32 [15], replicated, may hold values from 512 to 2048
Outputs:
- solution: float32 [8, 4, 64, 2048], P('leaf', None, None, 'panel')
All inputs are finite; a program needn't handle non-finite values.
Results may differ from a plain program's by a relative error of at most 0.0051.
Values sent between devices are 32-bit elements; how exact they have to be, the bound alone decides.
No kernel may reach another device: no remote copies, remote signals or barrier semaphores. Data moves between devices by JAX's collectives and lax.ppermute only.
A program may use at most 128 MiB of HBM per device.

v0:
```python
import jax
import jax.numpy as jnp
from jax import lax
from jax.sharding import PartitionSpec as P


def swapped(block, axis, stride):
    count = lax.axis_size(axis)
    route = []
    for low in range(count):
        high = low | 1 << stride
        if high != low and high < count:
            route += [(low, high), (high, low)]
    return lax.ppermute(block, axis, route)


def per_device(adjoint_rhs, panel_tiles, diag_inverse, front_sizes):
    leaf_count = lax.axis_size("leaf")
    panel_count = lax.axis_size("panel")
    levels = leaf_count.bit_length()
    leaf_pos = lax.axis_index("leaf")
    panel_pos = lax.axis_index("panel")
    sep_rows = diag_inverse.shape[2]
    strip = panel_tiles.shape[1]
    columns = jnp.arange(sep_rows)
    solved = []
    results = []
    for height in range(levels):
        group_size = leaf_count >> height
        col_width = sep_rows // group_size
        share = col_width // panel_count
        col_start = sum((upper * (sep_rows // (leaf_count >> upper)) for upper in range(height)))
        row_start = sum(
            (sep_rows // (leaf_count >> upper) // panel_count for upper in range(height))
        )
        front_pos = leaf_pos // group_size
        member = leaf_pos % group_size
        right = adjoint_rhs[0, :, row_start : row_start + share]
        if height > 0:
            strips = jnp.stack([solved[upper] for upper in range(height)], axis=1)
            region = panel_tiles[0, :, col_start : col_start + height * col_width].reshape(
                strip, height, col_width
            )
            partial_value = jnp.einsum(
                "nar,raw->nw", strips, region, preferred_element_type=jnp.float32
            )
            shares = lax.psum_scatter(partial_value, "panel", scatter_dimension=1, tiled=True)
            resid = right - shares
        else:
            resid = right
        front_id = (1 << height) - 1 + front_pos
        live_size = jnp.sum(jnp.where(jnp.arange(front_sizes.shape[0]) == front_id, front_sizes, 0))
        global_rows = member * col_width + panel_pos * share + jnp.arange(share)
        resid_low = jnp.where(global_rows[None, :] < live_size, resid, 0.0).astype(jnp.bfloat16)
        block = diag_inverse[0, row_start : row_start + share, :].astype(jnp.float32)
        below = columns[None, :] <= global_rows[:, None]
        factor = (
            jnp.where(below, block, 0.0)
            + (columns[None, :] == global_rows[:, None]).astype(jnp.float32)
        ).astype(jnp.bfloat16)
        terms = jnp.dot(resid_low, factor, preferred_element_type=jnp.float32)
        mine = lax.psum_scatter(terms, "panel", scatter_dimension=1, tiled=True)
        for bit in range(levels - 1 - height):
            mine = mine + swapped(mine, "leaf", bit)
        rows_now = mine.astype(jnp.bfloat16)
        solved.append(rows_now)
        results.append(mine)
    return jnp.stack(results, axis=0)[None]


def solution(mesh):
    in_specs = (P("leaf", None, "panel"), P("leaf", "panel", None), P("leaf", "panel", None), P())
    out_specs = P("leaf", None, None, "panel")
    return jax.shard_map(
        per_device, mesh=mesh, in_specs=in_specs, out_specs=out_specs, check_vma=False
    )
```

profile of v0, /device:TPU:0, one launch (start us, length us, event | category | flops | bytes accessed | tf_op | source)
XLA Modules:
  0.0 236.3 jit_solution(1629834679634465325)
XLA Ops:
  6.5 0.0 reduce-scatter.8.cloned.1.call-start
  6.5 1.3 fusion.60
  7.9 0.7 broadcast_compare_fusion.3
  8.5 2.1 fusion.25
  10.7 0.0 reduce-scatter.8.cloned.1.call-update
  10.7 0.0 reduce-scatter.10.cloned.1.call-start
  10.7 24.5 %reduce-scatter.8.cloned.1.call-done = f32[64,512]{1,0:T(8,128)} async-done(((f32[64,2048]{1,0:T(8,128)}), f32[64,512]{1,0:T(8,128)}) %reduce-scatter.8.cloned.1.call-update) | async-done | bytes 131088 | tf_op jit(solution)/shard_map/reduce_scatter | solution.py:62
  35.2 1.5 collective-permute-start
  36.7 3.8 %collective-permute-done = f32[64,512]{1,0:T(8,128)S(1)} collective-permute-done((f32[64,512]{1,0:T(8,128)}, f32[64,512]{1,0:T(8,128)S(1)}, u32[]{:S(2)}, u32[]{:S(2)}) %collective-permute-start) | collective-permute-done | bytes 131104 | tf_op jit(solution)/shard_map/ppermute | solution.py:14
  40.5 0.9 add.134
  41.4 1.6 collective-permute-start.1
  43.0 3.5 %collective-permute-done.1 = f32[64,512]{1,0:T(8,128)S(1)} collective-permute-done((f32[64,512]{1,0:T(8,128)S(1)}, f32[64,512]{1,0:T(8,128)S(1)}, u32[]{:S(2)}, u32[]{:S(2)}) %collective-permute-start.1) | collective-permute-done | bytes 131104 | tf_op jit(solution)/shard_map/ppermute | solution.py:14
  46.5 2.5 %collective-permute-start.2 = (f32[64,512]{1,0:T(8,128)S(1)}, f32[64,512]{1,0:T(8,128)S(1)}, u32[]{:S(2)}, u32[]{:S(2)}) collective-permute-start(f32[64,512]{1,0:T(8,128)S(1)} %add.135), channel_id=1, source_target_pairs={{0,16},{16,0},{4,20},{20,4},{8,24},{24,8},{12,28},{28,12},{1,17},{... | collective-permute-start | bytes 393224 | tf_op jit(solution)/shard_map/ppermute | solution.py:14
  49.0 4.8 %collective-permute-done.2 = f32[64,512]{1,0:T(8,128)S(1)} collective-permute-done((f32[64,512]{1,0:T(8,128)S(1)}, f32[64,512]{1,0:T(8,128)S(1)}, u32[]{:S(2)}, u32[]{:S(2)}) %collective-permute-start.2) | collective-permute-done | bytes 131104 | tf_op jit(solution)/shard_map/ppermute | solution.py:14
  53.8 0.0 slice-start
  53.8 2.1 fusion.18
  55.9 0.0 reduce-scatter.10.cloned.1.call-update
  55.9 0.0 reduce-scatter.12.cloned.1.call-start
  56.0 0.6 broadcast_compare_fusion.2
  56.6 19.1 %reduce-scatter.10.cloned.1.call-done = f32[64,128]{1,0:T(8,128)} async-done(((f32[64,512]{1,0:T(8,128)}), f32[64,128]{1,0:T(8,128)}) %reduce-scatter.10.cloned.1.call-update) | async-done | bytes 32784 | tf_op jit(solution)/shard_map/reduce_scatter | solution.py:47
  75.7 2.4 %fusion.15 = f32[64,2048]{1,0:T(8,128)} fusion(bf16[1,960,2048]{2,1,0:T(8,128)(2,1)} %param.6, s32[128]{0:T(128)S(1)} %iota_add_fusion.2, f32[64,128]{1,0:T(8,128)} %reduce-scatter.10.cloned.1.call-done, f32[1,64,960]{2,1,0:T(8,128)} %param.4, pred[128]{0:T(512)(128)(4,1)S(1)} %broadcast_compare_fusion.2), kind=kOutput, calls=%fused_computation.21 | convolution fusion | flops 35414016 | bytes 1114752 | tf_op jit(solution)/shard_map/dot_general | solution.py:61
  78.1 0.0 reduce-scatter.12.cloned.1.call-update
  78.1 0.0 reduce-scatter.14.cloned.1.call-start
  78.1 21.8 %reduce-scatter.12.cloned.1.call-done = f32[64,512]{1,0:T(8,128)} async-done(((f32[64,2048]{1,0:T(8,128)}), f32[64,512]{1,0:T(8,128)}) %reduce-scatter.12.cloned.1.call-update) | async-done | bytes 131088 | tf_op jit(solution)/shard_map/reduce_scatter | solution.py:62
  99.9 1.5 collective-permute-start.3
  101.4 3.8 %collective-permute-done.3 = f32[64,512]{1,0:T(8,128)S(1)} collective-permute-done((f32[64,512]{1,0:T(8,128)}, f32[64,512]{1,0:T(8,128)S(1)}, u32[]{:S(2)}, u32[]{:S(2)}) %collective-permute-start.3) | collective-permute-done | bytes 131104 | tf_op jit(solution)/shard_map/ppermute | solution.py:14
  105.2 0.9 add.143
  106.2 1.5 collective-permute-start.4
  107.7 0.0 slice-done
  107.7 0.0 copy-start.1
  107.7 2.7 %reshape_squeeze.7 = bf16[512,2,1024]{2,1,0:T(2,128)(2,1)} reshape(bf16[1,512,2048]{2,1,0:T(8,128)(2,1)S(1)} %slice-done) | data formatting | bytes 4194304 | tf_op jit(solution)/shard_map/reshape;squeeze | solution.py:41
  110.4 0.8 collective-permute-done.4
  111.2 3.1 %fusion.8 = f32[64,1024]{1,0:T(8,128)} fusion(bf16[512,2,1024]{2,1,0:T(2,128)(2,1)} %reshape_squeeze.7, bf16[64,1,512]{2,0,1:T(8,128)(2,1)S(1)} %get-tuple-element.12, bf16[64,1,512]{2,0,1:T(8,128)(2,1)S(1)} %bitcast.66), kind=kOutput, calls=%fused_computation.14 | convolution fusion | flops 134283264 | bytes 2490368 | tf_op jit(solution)/shard_map/nar,raw->nw/dot_general | solution.py:44
  114.3 0.0 reduce-scatter.14.cloned.1.call-update
  114.3 0.0 reduce-scatter.16.cloned.1.call-start
  114.4 0.6 broadcast_compare_fusion.1
  114.9 19.6 %reduce-scatter.14.cloned.1.call-done = f32[64,256]{1,0:T(8,128)} async-done(((f32[64,1024]{1,0:T(8,128)}), f32[64,256]{1,0:T(8,128)}) %reduce-scatter.14.cloned.1.call-update) | async-done | bytes 65552 | tf_op jit(solution)/shard_map/reduce_scatter | solution.py:47
  134.5 0.0 copy-done.1
  134.5 2.8 %fusion.13 = f32[64,2048]{1,0:T(8,128)} fusion(bf16[1,960,2048]{2,1,0:T(8,128)(2,1)} %param.6, s32[256]{0:T(256)S(1)} %iota_add_fusion.1, f32[64,256]{1,0:T(8,128)} %reduce-scatter.14.cloned.1.call-done, f32[1,64,960]{2,1,0:T(8,128)S(1)} %copy-done.1, pred[256]{0:T(512)(128)(4,1)S(1)} %broadcast_compare_fusion.1), kind=kOutput, calls=%fused_computation.20 | convolution fusion | flops 70828032 | bytes 1705472 | tf_op jit(solution)/shard_map/dot_general | solution.py:61
  137.3 0.0 reduce-scatter.16.cloned.1.call-update
  137.3 0.0 reduce-scatter.18.cloned.1.call-start
  137.4 21.8 %reduce-scatter.16.cloned.1.call-done = f32[64,512]{1,0:T(8,128)} async-done(((f32[64,2048]{1,0:T(8,128)}), f32[64,512]{1,0:T(8,128)}) %reduce-scatter.16.cloned.1.call-update) | async-done | bytes 131088 | tf_op jit(solution)/shard_map/reduce_scatter | solution.py:62
  159.1 1.5 collective-permute-start.5
  160.6 6.2 %slice.42 = bf16[1,512,6144]{2,1,0:T(8,128)(2,1)} slice(bf16[1,512,8704]{2,1,0:T(8,128)(2,1)} %param.5), slice={[0:1], [0:512], [2560:8704]} | slice | bytes 12582912 | tf_op jit(solution)/shard_map/slice | solution.py:41
  166.8 0.0 copy-start
  166.8 8.7 %copy.7 = bf16[1,512,6144]{1,2,0:T(8,128)(2,1)} copy(bf16[1,512,6144]{2,1,0:T(8,128)(2,1)} %slice.42) | data formatting | bytes 12582912
  175.5 0.0 collective-permute-done.5
  175.5 0.0 copy-done
  175.5 5.6 %convolution_bitcast_fusion = f32[64,2048]{1,0:T(8,128)} fusion(bf16[512,3,2048]{0,2,1:T(8,128)(2,1)} %bitcast.65, bf16[64,1,512]{2,0,1:T(8,128)(2,1)S(1)} %get-tuple-element.14, bf16[64,1,512]{2,0,1:T(8,128)(2,1)S(1)} %get-tuple-element.12, bf16[64,1,512]{2,0,1:T(8,128)(2,1)S(1)} %bitcast.67), kind=kOutput, calls=%fused_computation.5 | convolution fusion | flops 402849792 | bytes 7012352 | tf_op jit(solution)/shard_map/nar,raw->nw/dot_general | solution.py:44
  181.1 0.0 reduce-scatter.18.cloned.1.call-update
  181.1 0.0 reduce-scatter.20.cloned.1.call-start
  181.2 0.6 broadcast_compare_fusion
  181.7 20.3 %reduce-scatter.18.cloned.1.call-done = f32[64,512]{1,0:T(8,128)} async-done(((f32[64,2048]{1,0:T(8,128)}), f32[64,512]{1,0:T(8,128)}) %reduce-scatter.18.cloned.1.call-update) | async-done | bytes 131088 | tf_op jit(solution)/shard_map/reduce_scatter | solution.py:47
  202.0 3.8 %fusion.6 = f32[64,2048]{1,0:T(8,128)} fusion(bf16[1,960,2048]{2,1,0:T(8,128)(2,1)} %param.6, s32[512]{0:T(512)S(1)} %iota_add_fusion, f32[64,512]{1,0:T(8,128)} %reduce-scatter.18.cloned.1.call-done, f32[1,64,960]{2,1,0:T(8,128)S(1)} %copy-done.1, pred[512]{0:T(512)(128)(4,1)S(1)} %broadcast_compare_fusion), kind=kOutput, calls=%fused_computation.13 | convolution fusion | flops 141656064 | bytes 2886144 | tf_op jit(solution)/shard_map/dot_general | solution.py:61
  205.9 0.0 reduce-scatter.20.cloned.1.call-update
  205.9 21.8 %reduce-scatter.20.cloned.1.call-done = f32[64,512]{1,0:T(8,128)} async-done(((f32[64,2048]{1,0:T(8,128)}), f32[64,512]{1,0:T(8,128)}) %reduce-scatter.20.cloned.1.call-update) | async-done | bytes 131088 | tf_op jit(solution)/shard_map/reduce_scatter | solution.py:62
  227.7 1.7 maximum_bitcast_fusion
  (8 shorter events, 0.1 us)
Async XLA Ops:
  6.5 28.7 %reduce-scatter.8.cloned.1.call-start = ((), (), s32[]{:S(2)}) async-start(), calls=%async_computation.7 | async-start | bytes 655360 | tf_op jit(solution)/shard_map/reduce_scatter | solution.py:62
  10.7 65.0 %reduce-scatter.10.cloned.1.call-start = ((), (), s32[]{:S(2)}) async-start(), calls=%async_computation.8 | async-start | bytes 163840 | tf_op jit(solution)/shard_map/reduce_scatter | solution.py:47
  35.2 5.3 %collective-permute-start = (f32[64,512]{1,0:T(8,128)}, f32[64,512]{1,0:T(8,128)S(1)}, u32[]{:S(2)}, u32[]{:S(2)}) collective-permute-start(f32[64,512]{1,0:T(8,128)} %reduce-scatter.8.cloned.1.call-done), channel_id=1, source_target_pairs={{0,4},{4,0},{8,12},{12,8},{16,20},{20,16},{24,28},{28,24},{1,5},{5... | collective-permute-start | bytes 393224 | tf_op jit(solution)/shard_map/ppermute | solution.py:14
  41.4 5.0 %collective-permute-start.1 = (f32[64,512]{1,0:T(8,128)S(1)}, f32[64,512]{1,0:T(8,128)S(1)}, u32[]{:S(2)}, u32[]{:S(2)}) collective-permute-start(f32[64,512]{1,0:T(8,128)S(1)} %add.134), channel_id=1, source_target_pairs={{0,8},{8,0},{4,12},{12,4},{16,24},{24,16},{20,28},{28,20},{1,9},{9... | collective-permute-start | bytes 393224 | tf_op jit(solution)/shard_map/ppermute | solution.py:14
  46.5 7.3 %collective-permute-start.2 = (f32[64,512]{1,0:T(8,128)S(1)}, f32[64,512]{1,0:T(8,128)S(1)}, u32[]{:S(2)}, u32[]{:S(2)}) collective-permute-start(f32[64,512]{1,0:T(8,128)S(1)} %add.135), channel_id=1, source_target_pairs={{0,16},{16,0},{4,20},{20,4},{8,24},{24,8},{12,28},{28,12},{1,17},{... | collective-permute-start | bytes 393224 | tf_op jit(solution)/shard_map/ppermute | solution.py:14
  53.8 53.9 %slice-start = ((bf16[1,512,8704]{2,1,0:T(8,128)(2,1)}), bf16[1,512,2048]{2,1,0:T(8,128)(2,1)S(1)}, s32[]{:S(2)}) async-start(bf16[1,512,8704]{2,1,0:T(8,128)(2,1)} %param.5), calls=%async_computation.14 | async-start | bytes 4194304 | tf_op jit(solution)/shard_map/slice | solution.py:41
  55.9 44.0 %reduce-scatter.12.cloned.1.call-start = ((), (), s32[]{:S(2)}) async-start(), calls=%async_computation.9 | async-start | bytes 655360 | tf_op jit(solution)/shard_map/reduce_scatter | solution.py:62
  78.1 56.4 %reduce-scatter.14.cloned.1.call-start = ((), (), s32[]{:S(2)}) async-start(), calls=%async_computation.10 | async-start | bytes 327680 | tf_op jit(solution)/shard_map/reduce_scatter | solution.py:47
  99.9 5.3 %collective-permute-start.3 = (f32[64,512]{1,0:T(8,128)}, f32[64,512]{1,0:T(8,128)S(1)}, u32[]{:S(2)}, u32[]{:S(2)}) collective-permute-start(f32[64,512]{1,0:T(8,128)} %reduce-scatter.12.cloned.1.call-done), channel_id=1, source_target_pairs={{0,4},{4,0},{8,12},{12,8},{16,20},{20,16},{24,28},{28,24},{1,5},{5... | collective-permute-start | bytes 393224 | tf_op jit(solution)/shard_map/ppermute | solution.py:14
  106.2 5.0 %collective-permute-start.4 = (f32[64,512]{1,0:T(8,128)S(1)}, f32[64,512]{1,0:T(8,128)S(1)}, u32[]{:S(2)}, u32[]{:S(2)}) collective-permute-start(f32[64,512]{1,0:T(8,128)S(1)} %add.143), channel_id=1, source_target_pairs={{0,8},{8,0},{4,12},{12,4},{16,24},{24,16},{20,28},{28,20},{1,9},{9... | collective-permute-start | bytes 393224 | tf_op jit(solution)/shard_map/ppermute | solution.py:14
  107.7 26.8 %copy-start.1 = (f32[1,64,960]{2,1,0:T(8,128)S(1)}, f32[1,64,960]{2,1,0:T(8,128)}, u32[]{:S(2)}) copy-start(f32[1,64,960]{2,1,0:T(8,128)} %param.4) | copy-start | bytes 737284
  114.3 44.8 %reduce-scatter.16.cloned.1.call-start = ((), (), s32[]{:S(2)}) async-start(), calls=%async_computation.11 | async-start | bytes 655360 | tf_op jit(solution)/shard_map/reduce_scatter | solution.py:62
  137.3 64.7 %reduce-scatter.18.cloned.1.call-start = ((), (), s32[]{:S(2)}) async-start(), calls=%async_computation.12 | async-start | bytes 655360 | tf_op jit(solution)/shard_map/reduce_scatter | solution.py:47
  159.1 16.4 %collective-permute-start.5 = (f32[64,512]{1,0:T(8,128)}, f32[64,512]{1,0:T(8,128)S(1)}, u32[]{:S(2)}, u32[]{:S(2)}) collective-permute-start(f32[64,512]{1,0:T(8,128)} %reduce-scatter.16.cloned.1.call-done), channel_id=1, source_target_pairs={{0,4},{4,0},{8,12},{12,8},{16,20},{20,16},{24,28},{28,24},{1,5},{5... | collective-permute-start | bytes 393224 | tf_op jit(solution)/shard_map/ppermute | solution.py:14
  166.8 8.7 %copy-start = (f32[64,512]{1,0:T(8,128)S(1)}, f32[64,512]{1,0:T(8,128)}, u32[]{:S(2)}) copy-start(f32[64,512]{1,0:T(8,128)} %reduce-scatter.16.cloned.1.call-done) | copy-start | bytes 393220
  181.1 46.6 %reduce-scatter.20.cloned.1.call-start = ((), (), s32[]{:S(2)}) async-start(), calls=%async_computation.13 | async-start | bytes 655360 | tf_op jit(solution)/shard_map/reduce_scatter | solution.py:62
Sparse Core Ops, SparseCore 0:
  10.8 24.3 reduce-scatter.7
  56.0 19.6 reduce-scatter.9
  78.2 21.6 reduce-scatter.11
  114.4 20.0 reduce-scatter.13
  137.4 21.6 reduce-scatter.15
  181.2 20.7 reduce-scatter.17
  206.0 21.6 reduce-scatter.19
where the time goes:
time: 237 us; the launch traced here: 236 us
  waiting for transfers between devices  166 us (70%)
  matrix products  21.8 us (9%)
  local copies, waits for them, and re-layouts  17.7 us (7%)
  between operations  13.6 us (6%)
  starting transfers between devices  10.2 us (4%)
  other arithmetic  7.41 us (3%)
    reduce_scatter x4, waiting for transfers between devices, per_device(): mine = lax.psum_scatter(terms, 'panel', scatter_dimension=1, tiled=True)  89.8 us
    reduce_scatter x3, waiting for transfers between devices, per_device(): lax.psum_scatter(partial_value, 'panel', scatter_dimension=1, tiled=True)  58.9 us
    ppermute x6, waiting for transfers between devices, swapped(): return lax.ppermute(block, axis, route)  16.7 us
    dot_general x4, matrix products, per_device(): terms = jnp.dot(resid_low, factor, preferred_element_type=jnp.float32)  11.1 us
    dot_general x3, matrix products, per_device(): jnp.einsum('nar,raw->nw', strips, region, preferred_element_type=jnp.floa...  10.7 us
    ppermute x6, starting transfers between devices, swapped(): return lax.ppermute(block, axis, route)  9.97 us
    unnamed x5, local copies, waits for them, and re-layouts  8.71 us
    slice x3, local copies, waits for them, and re-layouts, per_device(): panel_tiles[0, :, col_start:col_start + height * col_width]  6.2 us
  transfers between devices with their start and end apart: 13, of which 12 were waited for; matrix products, arithmetic and copies ran while one was open for 8% of the time, Pallas kernels for 0%

commit v1 on v0

--- a/solution.py
+++ b/solution.py
@@ -6,12 +6,29 @@
 
 def swapped(block, axis, stride):
     count = lax.axis_size(axis)
-    route = []
-    for low in range(count):
-        high = low | 1 << stride
-        if high != low and high < count:
-            route += [(low, high), (high, low)]
-    return lax.ppermute(block, axis, route)
+    return lax.ppermute(block, axis, [(low, low ^ 1 << stride) for low in range(count)])
+
+
+def halved(parts, axis_pos, axis, bit):
+    mine = (axis_pos >> bit) & 1
+    low, high = parts[: len(parts) // 2], parts[len(parts) // 2 :]
+    keep = [jnp.where(mine == 0, a, b) for a, b in zip(low, high)]
+    give = [jnp.where(mine == 0, b, a) for a, b in zip(low, high)]
+    width = keep[0].shape[1]
+    got = swapped(jnp.concatenate(give, axis=1), axis, bit)
+    return [k + got[:, i * width : (i + 1) * width] for i, k in enumerate(keep)]
+
+
+def scattered(partial_sum, axis_pos, axis):
+    count = lax.axis_size(axis)
+    bits = count.bit_length() - 1
+    width = partial_sum.shape[1] // count
+    blocks = [partial_sum[:, i * width : (i + 1) * width] for i in range(count)]
+    order = sorted(range(count), key=lambda i: [(i >> b) & 1 for b in range(bits)])
+    parts = [blocks[i] for i in order]
+    for bit in range(bits):
+        parts = halved(parts, axis_pos, axis, bit)
+    return parts[0]
 
 
 def per_device(adjoint_rhs, panel_tiles, diag_inverse, front_sizes):
@@ -21,7 +38,6 @@
     leaf_pos = lax.axis_index("leaf")
     panel_pos = lax.axis_index("panel")
     sep_rows = diag_inverse.shape[2]
-    strip = panel_tiles.shape[1]
     columns = jnp.arange(sep_rows)
     solved = []
     results = []
@@ -37,15 +53,15 @@
         member = leaf_pos % group_size
         right = adjoint_rhs[0, :, row_start : row_start + share]
         if height > 0:
-            strips = jnp.stack([solved[upper] for upper in range(height)], axis=1)
-            region = panel_tiles[0, :, col_start : col_start + height * col_width].reshape(
-                strip, height, col_width
-            )
-            partial_value = jnp.einsum(
-                "nar,raw->nw", strips, region, preferred_element_type=jnp.float32
-            )
-            shares = lax.psum_scatter(partial_value, "panel", scatter_dimension=1, tiled=True)
-            resid = right - shares
+            partial_value = 0.0
+            for upper in range(height):
+                low = col_start + upper * col_width
+                partial_value = partial_value + jnp.dot(
+                    solved[upper],
+                    panel_tiles[0, :, low : low + col_width],
+                    preferred_element_type=jnp.float32,
+                )
+            resid = right - scattered(partial_value, panel_pos, "panel")
         else:
             resid = right
         front_id = (1 << height) - 1 + front_pos
@@ -59,7 +75,7 @@
             + (columns[None, :] == global_rows[:, None]).astype(jnp.float32)
         ).astype(jnp.bfloat16)
         terms = jnp.dot(resid_low, factor, preferred_element_type=jnp.float32)
-        mine = lax.psum_scatter(terms, "panel", scatter_dimension=1, tiled=True)
+        mine = scattered(terms, panel_pos, "panel")
         for bit in range(levels - 1 - height):
             mine = mine + swapped(mine, "leaf", bit)
         rows_now = mine.astype(jnp.bfloat16)

time: 237 us -> 102 us (0.43)
  waiting for transfers between devices: 166 us -> 52.8 us
  local copies, waits for them, and re-layouts: 17.7 us -> 0.01 us
  starting transfers between devices: 10.2 us -> 24.2 us
  between operations: 13.6 us -> 0.35 us
  matrix products: 21.8 us -> 18.3 us
    reduce_scatter x7 -> x0, waiting for transfers between devices: 149 us -> none  [the longest x4 89.8 us: per_device(): mine = lax.psum_scatter(terms, 'panel', scatter_dimension=1, tiled=True)]
    ppermute x6 -> x20, waiting for transfers between devices: 16.7 us -> 52.8 us  [swapped(): lax.ppermute(block, axis, [(low, low ^ 1 << stride) for low in range(coun...]
    ppermute x6 -> x20, starting transfers between devices: 9.97 us -> 24.2 us  [swapped(): lax.ppermute(block, axis, [(low, low ^ 1 << stride) for low in range(coun...]
    unnamed x5 -> x2, local copies, waits for them, and re-layouts: 8.71 us -> 0.01 us
    slice x3 -> x0, local copies, waits for them, and re-layouts: 6.2 us -> none  [per_device(): panel_tiles[0, :, col_start:col_start + height * col_width]]
    dot_general x4, matrix products: 11.1 us -> 7.82 us  [per_device(): terms = jnp.dot(resid_low, factor, preferred_element_type=jnp.float32)]
    another operation x1 -> x0, local copies, waits for them, and re-layouts: 2.74 us -> none  [per_device(): panel_tiles[0, :, col_start:col_start + height * col_width]]
    dot_general x3 -> x6, matrix products: 10.7 us -> 10.5 us  [per_device(): jnp.dot(solved[upper], panel_tiles[0, :, low:low + col_width], preferred_...]
  transfers between devices with their start and end apart: 13 -> 20, of which waited for: 12 -> 20; matrix products, arithmetic and copies ran while one was open for 8% -> 4% of each run, Pallas kernels for 0% -> 0%
where the time goes in v1:
time: 102 us; the launch traced here: 101 us
  waiting for transfers between devices  52.8 us (52%)
  starting transfers between devices  24.2 us (24%)
  matrix products  18.3 us (18%)
  other arithmetic  5.79 us (6%)
    ppermute x20, waiting for transfers between devices, swapped(): lax.ppermute(block, axis, [(low, low ^ 1 << stride) for low in range(coun...  52.8 us
    ppermute x20, starting transfers between devices, swapped(): lax.ppermute(block, axis, [(low, low ^ 1 << stride) for low in range(coun...  24.2 us
    dot_general x6, matrix products, per_device(): jnp.dot(solved[upper], panel_tiles[0, :, low:low + col_width], preferred_...  10.5 us
    dot_general x4, matrix products, per_device(): terms = jnp.dot(resid_low, factor, preferred_element_type=jnp.float32)  7.82 us
    lt x4, other arithmetic, per_device(): global_rows[None, :] < live_size  2.59 us
  transfers between devices with their start and end apart: 20, of which 20 were waited for; matrix products, arithmetic and copies ran while one was open for 4% of the time, Pallas kernels for 0%

profile of v1, /device:TPU:0, one launch (start us, length us, event | category | flops | bytes accessed | tf_op | source)
XLA Modules:
  0.0 101.5 jit_solution(6545792644506139279)
XLA Ops:
  0.0 0.0 copy-start
  0.0 1.5 %fusion.66 = (s32[]{:T(128)}, s32[]{:T(128)}, s32[]{:T(128)}, s32[]{:T(128)}) fusion(s32[15]{0:T(128)} %param.7, s32[]{:T(128)S(6)} %add_shard_map.7, s32[]{:T(128)S(6)} %add.202, s32[]{:T(128)S(6)} %select_n.264, s32[]{:T(128)S(6)} %add_shard_map.6), kind=kLoop, calls=%fused_computation.135 | loop fusion | flops 176 | bytes 92 | tf_op jit(solution)/shard_map/reduce_sum | solution.py:68
  1.5 0.7 broadcast_compare_fusion.3
  2.1 1.3 %fusion.34 = f32[64,2048]{1,0:T(8,128)S(1)} fusion(bf16[1,960,2048]{2,1,0:T(8,128)(2,1)} %param.6, s32[64]{0:T(128)S(1)} %iota_add_fusion.3, f32[1,64,960]{2,1,0:T(8,128)} %param.4, pred[64]{0:T(512)(128)(4,1)S(1)} %broadcast_compare_fusion.3), kind=kOutput, calls=%fused_computation.46 | convolution fusion | flops 17698816 | bytes 803136 | tf_op jit(solution)/shard_map/dot_general | solution.py:77
  3.6 0.6 collective-permute-start
  4.1 1.2 %collective-permute-done = f32[64,1024]{1,0:T(8,128)S(1)} collective-permute-done((f32[64,1024]{1,0:T(8,128)S(1)}, f32[64,1024]{1,0:T(8,128)S(1)}, u32[]{:S(2)}, u32[]{:S(2)}) %collective-permute-start) | collective-permute-done | bytes 262176 | tf_op jit(solution)/shard_map/ppermute | solution.py:9
  5.3 0.1 broadcast_select_fusion.4
  5.3 2.9 %collective-permute-start.1 = (f32[64,512]{1,0:T(8,128)S(1)}, f32[64,512]{1,0:T(8,128)S(1)}, u32[]{:S(2)}, u32[]{:S(2)}) collective-permute-start(f32[64,512]{1,0:T(8,128)S(1)} %get-tuple-element.27), channel_id=1, source_target_pairs={{0,2},{1,3},{2,0},{3,1},{4,6},{5,7},{6,4},{7,5},{8,10},{9,11},{10,... | collective-permute-start | bytes 393224 | tf_op jit(solution)/shard_map/ppermute | solution.py:9
  8.3 3.8 %collective-permute-done.1 = f32[64,512]{1,0:T(8,128)S(1)} collective-permute-done((f32[64,512]{1,0:T(8,128)S(1)}, f32[64,512]{1,0:T(8,128)S(1)}, u32[]{:S(2)}, u32[]{:S(2)}) %collective-permute-start.1) | collective-permute-done | bytes 131104 | tf_op jit(solution)/shard_map/ppermute | solution.py:9
  12.1 1.8 %collective-permute-start.2 = (f32[64,512]{1,0:T(8,128)S(1)}, f32[64,512]{1,0:T(8,128)S(1)}, u32[]{:S(2)}, u32[]{:S(2)}) collective-permute-start(f32[64,512]{1,0:T(8,128)S(1)} %select_add_fusion.2), channel_id=1, source_target_pairs={{0,4},{4,0},{8,12},{12,8},{16,20},{20,16},{24,28},{28,24},{1,5},{5... | collective-permute-start | bytes 393224 | tf_op jit(solution)/shard_map/ppermute | solution.py:9
  13.9 3.3 %collective-permute-done.2 = f32[64,512]{1,0:T(8,128)S(1)} collective-permute-done((f32[64,512]{1,0:T(8,128)S(1)}, f32[64,512]{1,0:T(8,128)S(1)}, u32[]{:S(2)}, u32[]{:S(2)}) %collective-permute-start.2) | collective-permute-done | bytes 131104 | tf_op jit(solution)/shard_map/ppermute | solution.py:9
  17.2 1.9 %collective-permute-start.3 = (f32[64,512]{1,0:T(8,128)S(1)}, f32[64,512]{1,0:T(8,128)S(1)}, u32[]{:S(2)}, u32[]{:S(2)}) collective-permute-start(f32[64,512]{1,0:T(8,128)S(1)} %add.195), channel_id=1, source_target_pairs={{0,8},{4,12},{8,0},{12,4},{16,24},{20,28},{24,16},{28,20},{1,9},{5... | collective-permute-start | bytes 393224 | tf_op jit(solution)/shard_map/ppermute | solution.py:9
  19.0 3.2 %collective-permute-done.3 = f32[64,512]{1,0:T(8,128)S(1)} collective-permute-done((f32[64,512]{1,0:T(8,128)S(1)}, f32[64,512]{1,0:T(8,128)S(1)}, u32[]{:S(2)}, u32[]{:S(2)}) %collective-permute-start.3) | collective-permute-done | bytes 131104 | tf_op jit(solution)/shard_map/ppermute | solution.py:9
  22.2 3.3 %collective-permute-start.4 = (f32[64,512]{1,0:T(8,128)S(1)}, f32[64,512]{1,0:T(8,128)S(1)}, u32[]{:S(2)}, u32[]{:S(2)}) collective-permute-start(f32[64,512]{1,0:T(8,128)S(1)} %add.196), channel_id=1, source_target_pairs={{0,16},{4,20},{8,24},{12,28},{16,0},{20,4},{24,8},{28,12},{1,17},{... | collective-permute-start | bytes 393224 | tf_op jit(solution)/shard_map/ppermute | solution.py:9
  25.6 4.4 %collective-permute-done.4 = f32[64,512]{1,0:T(8,128)S(1)} collective-permute-done((f32[64,512]{1,0:T(8,128)S(1)}, f32[64,512]{1,0:T(8,128)S(1)}, u32[]{:S(2)}, u32[]{:S(2)}) %collective-permute-start.4) | collective-permute-done | bytes 131104 | tf_op jit(solution)/shard_map/ppermute | solution.py:9
  29.9 1.2 %fusion.27 = f32[64,512]{1,0:T(8,128)S(1)} fusion(bf16[64,512]{1,0:T(8,128)(2,1)S(1)} %get-tuple-element.41, bf16[1,512,8704]{2,1,0:T(8,128)(2,1)} %param.5), kind=kOutput, calls=%fused_computation.36 | convolution fusion | flops 33554432 | bytes 720896 | tf_op jit(solution)/shard_map/dot_general | solution.py:59
  31.2 0.1 collective-permute-start.5
  31.3 1.2 %collective-permute-done.5 = f32[64,256]{1,0:T(8,128)S(1)} collective-permute-done((f32[64,256]{1,0:T(8,128)S(1)}, f32[64,256]{1,0:T(8,128)S(1)}, u32[]{:S(2)}, u32[]{:S(2)}) %collective-permute-start.5) | collective-permute-done | bytes 65568 | tf_op jit(solution)/shard_map/ppermute | solution.py:9
  32.5 1.6 %collective-permute-start.6 = (f32[64,128]{1,0:T(8,128)S(1)}, f32[64,128]{1,0:T(8,128)S(1)}, u32[]{:S(2)}, u32[]{:S(2)}) collective-permute-start(f32[64,128]{1,0:T(8,128)S(1)} %get-tuple-element.24), channel_id=1, source_target_pairs={{0,2},{1,3},{2,0},{3,1},{4,6},{5,7},{6,4},{7,5},{8,10},{9,11},{10,... | collective-permute-start | bytes 98312 | tf_op jit(solution)/shard_map/ppermute | solution.py:9
  34.1 0.6 broadcast_compare_fusion.2
  34.7 1.8 %collective-permute-done.6 = f32[64,128]{1,0:T(8,128)S(1)} collective-permute-done((f32[64,128]{1,0:T(8,128)S(1)}, f32[64,128]{1,0:T(8,128)S(1)}, u32[]{:S(2)}, u32[]{:S(2)}) %collective-permute-start.6) | collective-permute-done | bytes 32800 | tf_op jit(solution)/shard_map/ppermute | solution.py:9
  36.5 0.0 copy-done
  36.5 1.5 %fusion.24 = f32[64,2048]{1,0:T(8,128)S(1)} fusion(bf16[1,960,2048]{2,1,0:T(8,128)(2,1)} %param.6, s32[128]{0:T(128)S(1)} %iota_add_fusion.2, f32[64,128]{1,0:T(8,128)S(1)} %collective-permute-done.6, f32[64,128]{1,0:T(8,128)S(1)} %get-tuple-element.25, f32[64,128]{1,0:T(8,128)S(1)} %get-tuple-element.26, f32[1,64,960]{2,1,0:T(8,128)S(1)} %copy-done, ...), kind=kOutput, calls=%fused_computation.33 | convolution fusion | flops 35430400 | bytes 1180673 | tf_op jit(solution)/shard_map/dot_general | solution.py:77
  38.1 0.1 collective-permute-start.7
  38.2 1.5 %collective-permute-done.7 = f32[64,1024]{1,0:T(8,128)S(1)} collective-permute-done((f32[64,1024]{1,0:T(8,128)S(1)}, f32[64,1024]{1,0:T(8,128)S(1)}, u32[]{:S(2)}, u32[]{:S(2)}) %collective-permute-start.7) | collective-permute-done | bytes 262176 | tf_op jit(solution)/shard_map/ppermute | solution.py:9
  39.7 0.1 broadcast_select_fusion.3
  39.8 1.6 %collective-permute-start.8 = (f32[64,512]{1,0:T(8,128)S(1)}, f32[64,512]{1,0:T(8,128)S(1)}, u32[]{:S(2)}, u32[]{:S(2)}) collective-permute-start(f32[64,512]{1,0:T(8,128)S(1)} %get-tuple-element.21), channel_id=1, source_target_pairs={{0,2},{1,3},{2,0},{3,1},{4,6},{5,7},{6,4},{7,5},{8,10},{9,11},{10,... | collective-permute-start | bytes 393224 | tf_op jit(solution)/shard_map/ppermute | solution.py:9
  41.4 4.0 %collective-permute-done.8 = f32[64,512]{1,0:T(8,128)S(1)} collective-permute-done((f32[64,512]{1,0:T(8,128)S(1)}, f32[64,512]{1,0:T(8,128)S(1)}, u32[]{:S(2)}, u32[]{:S(2)}) %collective-permute-start.8) | collective-permute-done | bytes 131104 | tf_op jit(solution)/shard_map/ppermute | solution.py:9
  45.4 1.6 %collective-permute-start.9 = (f32[64,512]{1,0:T(8,128)S(1)}, f32[64,512]{1,0:T(8,128)S(1)}, u32[]{:S(2)}, u32[]{:S(2)}) collective-permute-start(f32[64,512]{1,0:T(8,128)S(1)} %select_add_fusion.1), channel_id=1, source_target_pairs={{0,4},{4,0},{8,12},{12,8},{16,20},{20,16},{24,28},{28,24},{1,5},{5... | collective-permute-start | bytes 393224 | tf_op jit(solution)/shard_map/ppermute | solution.py:9
  47.0 3.5 %collective-permute-done.9 = f32[64,512]{1,0:T(8,128)S(1)} collective-permute-done((f32[64,512]{1,0:T(8,128)S(1)}, f32[64,512]{1,0:T(8,128)S(1)}, u32[]{:S(2)}, u32[]{:S(2)}) %collective-permute-start.9) | collective-permute-done | bytes 131104 | tf_op jit(solution)/shard_map/ppermute | solution.py:9
  50.5 0.7 collective-permute-start.10
  51.2 4.3 %collective-permute-done.10 = f32[64,512]{1,0:T(8,128)S(1)} collective-permute-done((f32[64,512]{1,0:T(8,128)S(1)}, f32[64,512]{1,0:T(8,128)S(1)}, u32[]{:S(2)}, u32[]{:S(2)}) %collective-permute-start.10) | collective-permute-done | bytes 131104 | tf_op jit(solution)/shard_map/ppermute | solution.py:9
  55.5 1.5 %fusion.17 = f32[64,1024]{1,0:T(8,128)S(1)} fusion(bf16[64,512]{1,0:T(8,128)(2,1)S(1)} %get-tuple-element.43, bf16[1,512,8704]{2,1,0:T(8,128)(2,1)} %param.5), kind=kOutput, calls=%fused_computation.25 | convolution fusion | flops 67108864 | bytes 1376256 | tf_op jit(solution)/shard_map/dot_general | solution.py:59
  57.1 1.5 %convolution_add_fusion.1 = f32[64,1024]{1,0:T(8,128)S(1)} fusion(f32[64,1024]{1,0:T(8,128)S(1)} %fusion.17, bf16[64,512]{1,0:T(8,128)(2,1)S(1)} %get-tuple-element.41, bf16[1,512,8704]{2,1,0:T(8,128)(2,1)} %param.5), kind=kOutput, calls=%fused_computation.21 | convolution fusion | flops 67174400 | bytes 1638400 | tf_op jit(solution)/shard_map/dot_general | solution.py:59
  58.6 0.1 collective-permute-start.11
  58.8 1.3 %collective-permute-done.11 = f32[64,512]{1,0:T(8,128)S(1)} collective-permute-done((f32[64,512]{1,0:T(8,128)S(1)}, f32[64,512]{1,0:T(8,128)S(1)}, u32[]{:S(2)}, u32[]{:S(2)}) %collective-permute-start.11) | collective-permute-done | bytes 131104 | tf_op jit(solution)/shard_map/ppermute | solution.py:9
  60.1 1.6 %collective-permute-start.12 = (f32[64,256]{1,0:T(8,128)S(1)}, f32[64,256]{1,0:T(8,128)S(1)}, u32[]{:S(2)}, u32[]{:S(2)}) collective-permute-start(f32[64,256]{1,0:T(8,128)S(1)} %get-tuple-element.18), channel_id=1, source_target_pairs={{0,2},{1,3},{2,0},{3,1},{4,6},{5,7},{6,4},{7,5},{8,10},{9,11},{10,... | collective-permute-start | bytes 196616 | tf_op jit(solution)/shard_map/ppermute | solution.py:9
  61.7 0.7 broadcast_compare_fusion.1
  62.4 2.0 %collective-permute-done.12 = f32[64,256]{1,0:T(8,128)S(1)} collective-permute-done((f32[64,256]{1,0:T(8,128)S(1)}, f32[64,256]{1,0:T(8,128)S(1)}, u32[]{:S(2)}, u32[]{:S(2)}) %collective-permute-start.12) | collective-permute-done | bytes 65568 | tf_op jit(solution)/shard_map/ppermute | solution.py:9
  64.4 2.0 %fusion.22 = f32[64,2048]{1,0:T(8,128)S(1)} fusion(bf16[1,960,2048]{2,1,0:T(8,128)(2,1)} %param.6, s32[256]{0:T(256)S(1)} %iota_add_fusion.1, f32[64,256]{1,0:T(8,128)S(1)} %collective-permute-done.12, f32[64,256]{1,0:T(8,128)S(1)} %get-tuple-element.19, f32[64,256]{1,0:T(8,128)S(1)} %get-tuple-element.20, f32[1,64,960]{2,1,0:T(8,128)S(1)} %copy-done, ...), kind=kOutput, calls=%fused_computation.32 | convolution fusion | flops 70860800 | bytes 1836545 | tf_op jit(solution)/shard_map/dot_general | solution.py:77
  66.5 0.1 collective-permute-start.13
  66.6 1.5 %collective-permute-done.13 = f32[64,1024]{1,0:T(8,128)S(1)} collective-permute-done((f32[64,1024]{1,0:T(8,128)S(1)}, f32[64,1024]{1,0:T(8,128)S(1)}, u32[]{:S(2)}, u32[]{:S(2)}) %collective-permute-start.13) | collective-permute-done | bytes 262176 | tf_op jit(solution)/shard_map/ppermute | solution.py:9
  68.1 0.1 broadcast_select_fusion.2
  68.2 1.6 %collective-permute-start.14 = (f32[64,512]{1,0:T(8,128)S(1)}, f32[64,512]{1,0:T(8,128)S(1)}, u32[]{:S(2)}, u32[]{:S(2)}) collective-permute-start(f32[64,512]{1,0:T(8,128)S(1)} %get-tuple-element.15), channel_id=1, source_target_pairs={{0,2},{1,3},{2,0},{3,1},{4,6},{5,7},{6,4},{7,5},{8,10},{9,11},{10,... | collective-permute-start | bytes 393224 | tf_op jit(solution)/shard_map/ppermute | solution.py:9
  69.7 4.0 %collective-permute-done.14 = f32[64,512]{1,0:T(8,128)S(1)} collective-permute-done((f32[64,512]{1,0:T(8,128)S(1)}, f32[64,512]{1,0:T(8,128)S(1)}, u32[]{:S(2)}, u32[]{:S(2)}) %collective-permute-start.14) | collective-permute-done | bytes 131104 | tf_op jit(solution)/shard_map/ppermute | solution.py:9
  73.8 1.6 %collective-permute-start.15 = (f32[64,512]{1,0:T(8,128)S(1)}, f32[64,512]{1,0:T(8,128)S(1)}, u32[]{:S(2)}, u32[]{:S(2)}) collective-permute-start(f32[64,512]{1,0:T(8,128)S(1)} %select_add_fusion), channel_id=1, source_target_pairs={{0,4},{4,0},{8,12},{12,8},{16,20},{20,16},{24,28},{28,24},{1,5},{5... | collective-permute-start | bytes 393224 | tf_op jit(solution)/shard_map/ppermute | solution.py:9
  75.3 2.1 %fusion.7 = f32[64,2048]{1,0:T(8,128)S(1)} fusion(bf16[64,512]{1,0:T(8,128)(2,1)S(1)} %get-tuple-element.43, bf16[1,512,8704]{2,1,0:T(8,128)(2,1)} %param.5), kind=kOutput, calls=%fused_computation.12 | convolution fusion | flops 134217728 | bytes 2686976 | tf_op jit(solution)/shard_map/dot_general | solution.py:59
  77.4 1.4 %collective-permute-done.15 = f32[64,512]{1,0:T(8,128)S(1)} collective-permute-done((f32[64,512]{1,0:T(8,128)S(1)}, f32[64,512]{1,0:T(8,128)S(1)}, u32[]{:S(2)}, u32[]{:S(2)}) %collective-permute-start.15) | collective-permute-done | bytes 131104 | tf_op jit(solution)/shard_map/ppermute | solution.py:9
  78.8 2.1 %fusion.5 = f32[64,2048]{1,0:T(8,128)S(1)} fusion(bf16[1,512,8704]{2,1,0:T(8,128)(2,1)} %param.5, f32[64,512]{1,0:T(8,128)S(1)} %select_add_fusion, f32[64,512]{1,0:T(8,128)S(1)} %collective-permute-done.15), kind=kOutput, calls=%fused_computation.10 | convolution fusion | flops 134283264 | bytes 2883584 | tf_op jit(solution)/shard_map/dot_general | solution.py:59
  80.9 2.1 %fusion.2 = f32[64,2048]{1,0:T(8,128)S(1)} fusion(f32[64,2048]{1,0:T(8,128)S(1)} %fusion.5, f32[64,2048]{1,0:T(8,128)S(1)} %fusion.7, bf16[64,512]{1,0:T(8,128)(2,1)S(1)} %get-tuple-element.41, bf16[1,512,8704]{2,1,0:T(8,128)(2,1)} %param.5), kind=kOutput, calls=%fused_computation.6 | convolution fusion | flops 134479872 | bytes 3735552 | tf_op jit(solution)/shard_map/dot_general | solution.py:59
  83.0 0.1 collective-permute-start.16
  83.1 1.5 %collective-permute-done.16 = f32[64,1024]{1,0:T(8,128)S(1)} collective-permute-done((f32[64,1024]{1,0:T(8,128)S(1)}, f32[64,1024]{1,0:T(8,128)S(1)}, u32[]{:S(2)}, u32[]{:S(2)}) %collective-permute-start.16) | collective-permute-done | bytes 262176 | tf_op jit(solution)/shard_map/ppermute | solution.py:9
  84.6 0.1 broadcast_select_fusion.1
  84.7 1.6 %collective-permute-start.17 = (f32[64,512]{1,0:T(8,128)S(1)}, f32[64,512]{1,0:T(8,128)S(1)}, u32[]{:S(2)}, u32[]{:S(2)}) collective-permute-start(f32[64,512]{1,0:T(8,128)S(1)} %get-tuple-element.12), channel_id=1, source_target_pairs={{0,2},{1,3},{2,0},{3,1},{4,6},{5,7},{6,4},{7,5},{8,10},{9,11},{10,... | collective-permute-start | bytes 393224 | tf_op jit(solution)/shard_map/ppermute | solution.py:9
  86.3 0.7 broadcast_compare_fusion
  87.0 3.3 %collective-permute-done.17 = f32[64,512]{1,0:T(8,128)S(1)} collective-permute-done((f32[64,512]{1,0:T(8,128)S(1)}, f32[64,512]{1,0:T(8,128)S(1)}, u32[]{:S(2)}, u32[]{:S(2)}) %collective-permute-start.17) | collective-permute-done | bytes 131104 | tf_op jit(solution)/shard_map/ppermute | solution.py:9
  90.3 3.0 %fusion.13 = f32[64,2048]{1,0:T(8,128)S(1)} fusion(bf16[1,960,2048]{2,1,0:T(8,128)(2,1)} %param.6, s32[512]{0:T(512)S(1)} %iota_add_fusion, f32[64,512]{1,0:T(8,128)S(1)} %collective-permute-done.17, f32[64,512]{1,0:T(8,128)S(1)} %get-tuple-element.13, f32[64,512]{1,0:T(8,128)S(1)} %get-tuple-element.14, f32[1,64,960]{2,1,0:T(8,128)S(1)} %copy-done, ...), kind=kOutput, calls=%fused_computation.20 | convolution fusion | flops 141721600 | bytes 3148289 | tf_op jit(solution)/shard_map/dot_general | solution.py:77
  93.3 0.1 collective-permute-start.18
  93.4 1.5 %collective-permute-done.18 = f32[64,1024]{1,0:T(8,128)S(1)} collective-permute-done((f32[64,1024]{1,0:T(8,128)S(1)}, f32[64,1024]{1,0:T(8,128)S(1)}, u32[]{:S(2)}, u32[]{:S(2)}) %collective-permute-start.18) | collective-permute-done | bytes 262176 | tf_op jit(solution)/shard_map/ppermute | solution.py:9
  94.9 0.1 broadcast_select_fusion
  95.0 1.6 %collective-permute-start.19 = (f32[64,512]{1,0:T(8,128)S(1)}, f32[64,512]{1,0:T(8,128)S(1)}, u32[]{:S(2)}, u32[]{:S(2)}) collective-permute-start(f32[64,512]{1,0:T(8,128)S(1)} %get-tuple-element.9), channel_id=1, source_target_pairs={{0,2},{1,3},{2,0},{3,1},{4,6},{5,7},{6,4},{7,5},{8,10},{9,11},{10,... | collective-permute-start | bytes 393224 | tf_op jit(solution)/shard_map/ppermute | solution.py:9
  96.6 4.0 %collective-permute-done.19 = f32[64,512]{1,0:T(8,128)S(1)} collective-permute-done((f32[64,512]{1,0:T(8,128)S(1)}, f32[64,512]{1,0:T(8,128)S(1)}, u32[]{:S(2)}, u32[]{:S(2)}) %collective-permute-start.19) | collective-permute-done | bytes 131104 | tf_op jit(solution)/shard_map/ppermute | solution.py:9
  100.7 0.8 maximum_bitcast_fusion
  (30 shorter events, 0.6 us)
Async XLA Ops:
  0.0 36.5 %copy-start = (f32[1,64,960]{2,1,0:T(8,128)S(1)}, f32[1,64,960]{2,1,0:T(8,128)}, u32[]{:S(2)}) copy-start(f32[1,64,960]{2,1,0:T(8,128)} %param.4) | copy-start | bytes 737284
  3.6 1.7 %collective-permute-start = (f32[64,1024]{1,0:T(8,128)S(1)}, f32[64,1024]{1,0:T(8,128)S(1)}, u32[]{:S(2)}, u32[]{:S(2)}) collective-permute-start(f32[64,1024]{1,0:T(8,128)S(1)} %pad_maximum_fusion), channel_id=1, source_target_pairs={{0,1},{1,0},{2,3},{3,2},{4,5},{5,4},{6,7},{7,6},{8,9},{9,8},{10,11... | collective-permute-start | bytes 786440 | tf_op jit(solution)/shard_map/ppermute | solution.py:9
  5.3 6.7 %collective-permute-start.1 = (f32[64,512]{1,0:T(8,128)S(1)}, f32[64,512]{1,0:T(8,128)S(1)}, u32[]{:S(2)}, u32[]{:S(2)}) collective-permute-start(f32[64,512]{1,0:T(8,128)S(1)} %get-tuple-element.27), channel_id=1, source_target_pairs={{0,2},{1,3},{2,0},{3,1},{4,6},{5,7},{6,4},{7,5},{8,10},{9,11},{10,... | collective-permute-start | bytes 393224 | tf_op jit(solution)/shard_map/ppermute | solution.py:9
  12.1 5.0 %collective-permute-start.2 = (f32[64,512]{1,0:T(8,128)S(1)}, f32[64,512]{1,0:T(8,128)S(1)}, u32[]{:S(2)}, u32[]{:S(2)}) collective-permute-start(f32[64,512]{1,0:T(8,128)S(1)} %select_add_fusion.2), channel_id=1, source_target_pairs={{0,4},{4,0},{8,12},{12,8},{16,20},{20,16},{24,28},{28,24},{1,5},{5... | collective-permute-start | bytes 393224 | tf_op jit(solution)/shard_map/ppermute | solution.py:9
  17.2 5.0 %collective-permute-start.3 = (f32[64,512]{1,0:T(8,128)S(1)}, f32[64,512]{1,0:T(8,128)S(1)}, u32[]{:S(2)}, u32[]{:S(2)}) collective-permute-start(f32[64,512]{1,0:T(8,128)S(1)} %add.195), channel_id=1, source_target_pairs={{0,8},{4,12},{8,0},{12,4},{16,24},{20,28},{24,16},{28,20},{1,9},{5... | collective-permute-start | bytes 393224 | tf_op jit(solution)/shard_map/ppermute | solution.py:9
  22.2 7.7 %collective-permute-start.4 = (f32[64,512]{1,0:T(8,128)S(1)}, f32[64,512]{1,0:T(8,128)S(1)}, u32[]{:S(2)}, u32[]{:S(2)}) collective-permute-start(f32[64,512]{1,0:T(8,128)S(1)} %add.196), channel_id=1, source_target_pairs={{0,16},{4,20},{8,24},{12,28},{16,0},{20,4},{24,8},{28,12},{1,17},{... | collective-permute-start | bytes 393224 | tf_op jit(solution)/shard_map/ppermute | solution.py:9
  31.2 1.3 %collective-permute-start.5 = (f32[64,256]{1,0:T(8,128)S(1)}, f32[64,256]{1,0:T(8,128)S(1)}, u32[]{:S(2)}, u32[]{:S(2)}) collective-permute-start(f32[64,256]{1,0:T(8,128)S(1)} %pad_maximum_fusion.6), channel_id=1, source_target_pairs={{0,1},{1,0},{2,3},{3,2},{4,5},{5,4},{6,7},{7,6},{8,9},{9,8},{10,11... | collective-permute-start | bytes 196616 | tf_op jit(solution)/shard_map/ppermute | solution.py:9
  32.5 4.0 %collective-permute-start.6 = (f32[64,128]{1,0:T(8,128)S(1)}, f32[64,128]{1,0:T(8,128)S(1)}, u32[]{:S(2)}, u32[]{:S(2)}) collective-permute-start(f32[64,128]{1,0:T(8,128)S(1)} %get-tuple-element.24), channel_id=1, source_target_pairs={{0,2},{1,3},{2,0},{3,1},{4,6},{5,7},{6,4},{7,5},{8,10},{9,11},{10,... | collective-permute-start | bytes 98312 | tf_op jit(solution)/shard_map/ppermute | solution.py:9
  38.1 1.6 %collective-permute-start.7 = (f32[64,1024]{1,0:T(8,128)S(1)}, f32[64,1024]{1,0:T(8,128)S(1)}, u32[]{:S(2)}, u32[]{:S(2)}) collective-permute-start(f32[64,1024]{1,0:T(8,128)S(1)} %pad_maximum_fusion.1), channel_id=1, source_target_pairs={{0,1},{1,0},{2,3},{3,2},{4,5},{5,4},{6,7},{7,6},{8,9},{9,8},{10,11... | collective-permute-start | bytes 786440 | tf_op jit(solution)/shard_map/ppermute | solution.py:9
  39.8 5.6 %collective-permute-start.8 = (f32[64,512]{1,0:T(8,128)S(1)}, f32[64,512]{1,0:T(8,128)S(1)}, u32[]{:S(2)}, u32[]{:S(2)}) collective-permute-start(f32[64,512]{1,0:T(8,128)S(1)} %get-tuple-element.21), channel_id=1, source_target_pairs={{0,2},{1,3},{2,0},{3,1},{4,6},{5,7},{6,4},{7,5},{8,10},{9,11},{10,... | collective-permute-start | bytes 393224 | tf_op jit(solution)/shard_map/ppermute | solution.py:9
  45.4 5.0 %collective-permute-start.9 = (f32[64,512]{1,0:T(8,128)S(1)}, f32[64,512]{1,0:T(8,128)S(1)}, u32[]{:S(2)}, u32[]{:S(2)}) collective-permute-start(f32[64,512]{1,0:T(8,128)S(1)} %select_add_fusion.1), channel_id=1, source_target_pairs={{0,4},{4,0},{8,12},{12,8},{16,20},{20,16},{24,28},{28,24},{1,5},{5... | collective-permute-start | bytes 393224 | tf_op jit(solution)/shard_map/ppermute | solution.py:9
  50.5 5.0 %collective-permute-start.10 = (f32[64,512]{1,0:T(8,128)S(1)}, f32[64,512]{1,0:T(8,128)S(1)}, u32[]{:S(2)}, u32[]{:S(2)}) collective-permute-start(f32[64,512]{1,0:T(8,128)S(1)} %add.210), channel_id=1, source_target_pairs={{0,8},{4,12},{8,0},{12,4},{16,24},{20,28},{24,16},{28,20},{1,9},{5... | collective-permute-start | bytes 393224 | tf_op jit(solution)/shard_map/ppermute | solution.py:9
  58.6 1.4 %collective-permute-start.11 = (f32[64,512]{1,0:T(8,128)S(1)}, f32[64,512]{1,0:T(8,128)S(1)}, u32[]{:S(2)}, u32[]{:S(2)}) collective-permute-start(f32[64,512]{1,0:T(8,128)S(1)} %pad_maximum_fusion.5), channel_id=1, source_target_pairs={{0,1},{1,0},{2,3},{3,2},{4,5},{5,4},{6,7},{7,6},{8,9},{9,8},{10,11... | collective-permute-start | bytes 393224 | tf_op jit(solution)/shard_map/ppermute | solution.py:9
  60.1 4.3 %collective-permute-start.12 = (f32[64,256]{1,0:T(8,128)S(1)}, f32[64,256]{1,0:T(8,128)S(1)}, u32[]{:S(2)}, u32[]{:S(2)}) collective-permute-start(f32[64,256]{1,0:T(8,128)S(1)} %get-tuple-element.18), channel_id=1, source_target_pairs={{0,2},{1,3},{2,0},{3,1},{4,6},{5,7},{6,4},{7,5},{8,10},{9,11},{10,... | collective-permute-start | bytes 196616 | tf_op jit(solution)/shard_map/ppermute | solution.py:9
  66.5 1.6 %collective-permute-start.13 = (f32[64,1024]{1,0:T(8,128)S(1)}, f32[64,1024]{1,0:T(8,128)S(1)}, u32[]{:S(2)}, u32[]{:S(2)}) collective-permute-start(f32[64,1024]{1,0:T(8,128)S(1)} %pad_maximum_fusion.2), channel_id=1, source_target_pairs={{0,1},{1,0},{2,3},{3,2},{4,5},{5,4},{6,7},{7,6},{8,9},{9,8},{10,11... | collective-permute-start | bytes 786440 | tf_op jit(solution)/shard_map/ppermute | solution.py:9
  68.2 5.6 %collective-permute-start.14 = (f32[64,512]{1,0:T(8,128)S(1)}, f32[64,512]{1,0:T(8,128)S(1)}, u32[]{:S(2)}, u32[]{:S(2)}) collective-permute-start(f32[64,512]{1,0:T(8,128)S(1)} %get-tuple-element.15), channel_id=1, source_target_pairs={{0,2},{1,3},{2,0},{3,1},{4,6},{5,7},{6,4},{7,5},{8,10},{9,11},{10,... | collective-permute-start | bytes 393224 | tf_op jit(solution)/shard_map/ppermute | solution.py:9
  73.8 5.0 %collective-permute-start.15 = (f32[64,512]{1,0:T(8,128)S(1)}, f32[64,512]{1,0:T(8,128)S(1)}, u32[]{:S(2)}, u32[]{:S(2)}) collective-permute-start(f32[64,512]{1,0:T(8,128)S(1)} %select_add_fusion), channel_id=1, source_target_pairs={{0,4},{4,0},{8,12},{12,8},{16,20},{20,16},{24,28},{28,24},{1,5},{5... | collective-permute-start | bytes 393224 | tf_op jit(solution)/shard_map/ppermute | solution.py:9
  83.0 1.6 %collective-permute-start.16 = (f32[64,1024]{1,0:T(8,128)S(1)}, f32[64,1024]{1,0:T(8,128)S(1)}, u32[]{:S(2)}, u32[]{:S(2)}) collective-permute-start(f32[64,1024]{1,0:T(8,128)S(1)} %pad_maximum_fusion.3), channel_id=1, source_target_pairs={{0,1},{1,0},{2,3},{3,2},{4,5},{5,4},{6,7},{7,6},{8,9},{9,8},{10,11... | collective-permute-start | bytes 786440 | tf_op jit(solution)/shard_map/ppermute | solution.py:9
  84.7 5.6 %collective-permute-start.17 = (f32[64,512]{1,0:T(8,128)S(1)}, f32[64,512]{1,0:T(8,128)S(1)}, u32[]{:S(2)}, u32[]{:S(2)}) collective-permute-start(f32[64,512]{1,0:T(8,128)S(1)} %get-tuple-element.12), channel_id=1, source_target_pairs={{0,2},{1,3},{2,0},{3,1},{4,6},{5,7},{6,4},{7,5},{8,10},{9,11},{10,... | collective-permute-start | bytes 393224 | tf_op jit(solution)/shard_map/ppermute | solution.py:9
  93.3 1.6 %collective-permute-start.18 = (f32[64,1024]{1,0:T(8,128)S(1)}, f32[64,1024]{1,0:T(8,128)S(1)}, u32[]{:S(2)}, u32[]{:S(2)}) collective-permute-start(f32[64,1024]{1,0:T(8,128)S(1)} %pad_maximum_fusion.4), channel_id=1, source_target_pairs={{0,1},{1,0},{2,3},{3,2},{4,5},{5,4},{6,7},{7,6},{8,9},{9,8},{10,11... | collective-permute-start | bytes 786440 | tf_op jit(solution)/shard_map/ppermute | solution.py:9
  95.0 5.6 %collective-permute-start.19 = (f32[64,512]{1,0:T(8,128)S(1)}, f32[64,512]{1,0:T(8,128)S(1)}, u32[]{:S(2)}, u32[]{:S(2)}) collective-permute-start(f32[64,512]{1,0:T(8,128)S(1)} %get-tuple-element.9), channel_id=1, source_target_pairs={{0,2},{1,3},{2,0},{3,1},{4,6},{5,7},{6,4},{7,5},{8,10},{9,11},{10,... | collective-permute-start | bytes 393224 | tf_op jit(solution)/shard_map/ppermute | solution.py:9

commit v2 on v0

v2 whole, which is shorter than its diff:
```python
import jax
import jax.numpy as jnp
from jax import lax
from jax.sharding import PartitionSpec as P


def exchanged(block, leaf_flip, panel_flip):
    leaf_count, panel_count = lax.axis_size("leaf"), lax.axis_size("panel")
    if leaf_flip == 0:
        return lax.ppermute(block, "panel", [(i, i ^ panel_flip) for i in range(panel_count)])
    if panel_flip == 0:
        return lax.ppermute(block, "leaf", [(i, i ^ leaf_flip) for i in range(leaf_count)])
    flip = leaf_flip * panel_count + panel_flip
    return lax.ppermute(
        block, ("leaf", "panel"), [(i, i ^ flip) for i in range(leaf_count * panel_count)]
    )


def chunk_order(count):
    bits = count.bit_length() - 1
    return sorted(range(count), key=lambda m: [-(m >> b & 1) for b in range(bits)])


def reduced(chunk_of, leaf_bits):
    count = lax.axis_size("panel")
    bits = count.bit_length() - 1
    held = {}
    arrived = {}
    for m in chunk_order(count):
        held[m] = chunk_of(m)
        if m & 1:
            arrived[m ^ 1] = exchanged(held[m], 0, 1)
    for bit in range(1, bits + 1):
        held = {m: held[m] + arrived[m] for m in arrived}
        arrived = {}
        if bit == bits:
            break
        step = 1 << bit
        if bit == bits - 1 and leaf_bits > 0:
            far, near = held[step], held[0]
            from_panel = exchanged(far, 0, step)
            from_leaf = exchanged(near, 1, 0)
            from_both = exchanged(far, 1, step)
            total = (near + from_panel) + (from_leaf + from_both)
            for leaf_bit in range(1, leaf_bits):
                total = total + exchanged(total, 1 << leaf_bit, 0)
            return total
        for m in sorted(held, reverse=True):
            if m & step:
                arrived[m ^ step] = exchanged(held[m], 0, step)
    return held[0]


def per_device(adjoint_rhs, panel_tiles, diag_inverse, front_sizes):
    leaf_count = lax.axis_size("leaf")
    panel_count = lax.axis_size("panel")
    levels = leaf_count.bit_length()
    leaf_pos = lax.axis_index("leaf")
    panel_pos = lax.axis_index("panel")
    sep_rows = diag_inverse.shape[2]
    strip = sep_rows // panel_count
    tiles = panel_tiles[0]
    inverse = diag_inverse[0]
    solved = []
    results = []
    base = {}

    def sizes(height):
        group_size = leaf_count >> height
        col_width = sep_rows // group_size
        share = col_width // panel_count
        col_start = sum((upper * (sep_rows // (leaf_count >> upper)) for upper in range(height)))
        row_start = sum(
            (sep_rows // (leaf_count >> upper) // panel_count for upper in range(height))
        )
        return group_size, col_width, share, col_start, row_start

    def own_rows(height):
        group_size, col_width, share, _, _ = sizes(height)
        return (leaf_pos % group_size) * col_width + panel_pos * share + jnp.arange(share)

    def masked(block, low, rows):
        columns = low + jnp.arange(block.shape[1])
        kept = jnp.where(columns[None, :] <= rows[:, None], block.astype(jnp.float32), 0.0)
        one = (columns[None, :] == rows[:, None]).astype(jnp.float32)
        return (kept + one).astype(jnp.bfloat16)

    def factor(height, m):
        _, _, share, _, row_start = sizes(height)
        low = (panel_pos ^ m) * strip
        block = lax.dynamic_slice(inverse, (row_start, low), (share, strip))
        return masked(block, low, own_rows(height))

    def coupling(height, m):
        _, col_width, share, col_start, _ = sizes(height)
        low = col_start + (height - 1) * col_width + (panel_pos ^ m) * share
        return lax.dynamic_slice(tiles, (0, low), (tiles.shape[0], share))

    def part(whole, m):
        width = whole.shape[1] // panel_count
        return lax.dynamic_slice(whole, (0, (panel_pos ^ m) * width), (whole.shape[0], width))

    factors = {}
    couplings = {}
    for height in range(1, levels):
        couplings[height] = lax.optimization_barrier(
            {m: coupling(height, m) for m in range(panel_count)}
        )
        factors[height] = lax.optimization_barrier(
            {m: factor(height, m) for m in range(panel_count)}
        )

    for height in range(levels):
        group_size, _, share, _, row_start = sizes(height)
        rows = own_rows(height)
        resid = adjoint_rhs[0, :, row_start : row_start + share]
        if height > 0:

            def update(m):
                term = jnp.dot(
                    solved[-1], couplings[height][m], preferred_element_type=jnp.float32
                )
                return term + part(base[height], m) if height in base else term

            resid = resid - reduced(update, 0)
        front_id = (1 << height) - 1 + leaf_pos // group_size
        live_size = lax.dynamic_slice(front_sizes, (front_id,), (1,)) if height else front_sizes[:1]
        resid_low = jnp.where(rows[None, :] < live_size[:, None], resid, 0.0).astype(jnp.bfloat16)
        if height == 0:
            whole = masked(inverse[row_start : row_start + share], 0, rows)
            terms = jnp.dot(resid_low, whole, preferred_element_type=jnp.float32)
            mine = reduced(lambda m: part(terms, m), levels - 1 - height)
        else:
            mine = reduced(
                lambda m: jnp.dot(
                    resid_low, factors[height][m], preferred_element_type=jnp.float32
                ),
                levels - 1 - height,
            )
        solved.append(mine.astype(jnp.bfloat16))
        results.append(mine)
        for later in range(height + 2, levels):
            _, width, _, start, _ = sizes(later)
            low = start + height * width
            term = jnp.dot(
                solved[-1], tiles[:, low : low + width], preferred_element_type=jnp.float32
            )
            base[later] = base[later] + term if later in base else term
    return jnp.stack(results, axis=0)[None]


def solution(mesh):
    in_specs = (P("leaf", None, "panel"), P("leaf", "panel", None), P("leaf", "panel", None), P())
    out_specs = P("leaf", None, None, "panel")

    return jax.shard_map(
        per_device, mesh=mesh, in_specs=in_specs, out_specs=out_specs, check_vma=False
    )
```

time: 237 us -> 95.6 us (0.40)
  waiting for transfers between devices: 166 us -> 30.4 us
  starting transfers between devices: 10.2 us -> 27.8 us
  between operations: 13.6 us -> 0.48 us
  local copies, waits for them, and re-layouts: 17.7 us -> 6.28 us
  other arithmetic: 7.41 us -> 11.1 us
  matrix products: 21.8 us -> 18.9 us
    reduce_scatter x7 -> x0, waiting for transfers between devices: 149 us -> none  [the longest x4 89.8 us: per_device(): mine = lax.psum_scatter(terms, 'panel', scatter_dimension=1, tiled=True)]
    ppermute x6 -> x30, starting transfers between devices: 9.97 us -> 27.8 us  [the longest x21 16.8 us: exchanged(): lax.ppermute(block, 'panel', [(i, i ^ panel_flip) for i in range(panel_co...]
    ppermute x6 -> x30, waiting for transfers between devices: 16.7 us -> 30.4 us  [the longest x21 18.5 us: exchanged(): lax.ppermute(block, 'panel', [(i, i ^ panel_flip) for i in range(panel_co...]
    unnamed x5 -> x6, local copies, waits for them, and re-layouts: 8.71 us -> 0.01 us
    dynamic_slice x0 -> x5, local copies, waits for them, and re-layouts: none -> 6.26 us  [the longest x3 4.77 us: coupling(): return lax.dynamic_slice(tiles, (0, low), (tiles.shape[0], share))]
    slice x3 -> x0, local copies, waits for them, and re-layouts: 6.2 us -> none  [per_device(): panel_tiles[0, :, col_start:col_start + height * col_width]]
    convert_element_type x0 -> x4, other arithmetic: none -> 5.69 us  [the longest x3 5.65 us: masked(): return (kept + one).astype(jnp.bfloat16)]
    dot_general x7 -> x28, matrix products: 21.8 us -> 18.9 us  [the longest x12 7.04 us: per_device(): jnp.dot(resid_low, factors[height][m], preferred_element_type=jnp.float32)]
  transfers between devices with their start and end apart: 13 -> 30, of which waited for: 12 -> 21; matrix products, arithmetic and copies ran while one was open for 8% -> 25% of each run, Pallas kernels for 0% -> 0%
where the time goes in v2:
time: 95.6 us; the launch traced here: 95 us
  waiting for transfers between devices  30.4 us (32%)
  starting transfers between devices  27.8 us (29%)
  matrix products  18.9 us (20%)
  other arithmetic  11.1 us (12%)
  local copies, waits for them, and re-layouts  6.28 us (7%)
    ppermute x21, waiting for transfers between devices, exchanged(): lax.ppermute(block, 'panel', [(i, i ^ panel_flip) for i in range(panel_co...  18.5 us
    ppermute x21, starting transfers between devices, exchanged(): lax.ppermute(block, 'panel', [(i, i ^ panel_flip) for i in range(panel_co...  16.8 us
    ppermute x6, waiting for transfers between devices, exchanged(): lax.ppermute(block, 'leaf', [(i, i ^ leaf_flip) for i in range(leaf_count)])  9.34 us
    dot_general x12, matrix products, per_device(): jnp.dot(resid_low, factors[height][m], preferred_element_type=jnp.float32)  7.04 us
    ppermute x6, starting transfers between devices, exchanged(): lax.ppermute(block, 'leaf', [(i, i ^ leaf_flip) for i in range(leaf_count)])  6.68 us
    dot_general x3, matrix products, per_device(): jnp.dot(solved[-1], tiles[:, low:low + width], preferred_element_type=jnp...  5.66 us
    convert_element_type x3, other arithmetic, masked(): return (kept + one).astype(jnp.bfloat16)  5.65 us
    dot_general x12, matrix products, update(): jnp.dot(solved[-1], couplings[height][m], preferred_element_type=jnp.floa...  4.82 us
  transfers between devices with their start and end apart: 30, of which 21 were waited for; matrix products, arithmetic and copies ran while one was open for 25% of the time, Pallas kernels for 0%

profile of v2, /device:TPU:0, one launch (start us, length us, event | category | flops | bytes accessed | tf_op | source)
XLA Modules:
  0.0 95.0 jit_solution(3650967618232295553)
XLA Ops:
  0.0 1.5 %fusion.59 = (s32[1]{0:T(128)}, s32[1]{0:T(128)}, s32[1]{0:T(128)}, s32[1]{0:T(128)}) fusion(s32[15]{0:T(128)} %param.7, s32[]{:T(128)S(6)} %select_n.230, s32[]{:T(128)S(6)} %select_n.204, s32[]{:T(128)S(6)} %select_n.216), kind=kLoop, calls=%fused_computation.125 | loop fusion | bytes 44 | tf_op jit(solution)/shard_map/dynamic_slice | solution.py:127
  1.5 0.7 broadcast_compare_fusion.3
  2.1 1.3 %fusion.40 = f32[64,2048]{1,0:T(8,128)S(1)} fusion(bf16[1,960,2048]{2,1,0:T(8,128)(2,1)} %param.6, s32[64]{0:T(128)S(1)} %iota_add_fusion.6, f32[1,64,960]{2,1,0:T(8,128)} %param.4, pred[64]{0:T(512)(128)(4,1)S(1)} %broadcast_compare_fusion.3), kind=kOutput, calls=%fused_computation.73 | convolution fusion | flops 17698816 | bytes 803136 | tf_op jit(solution)/shard_map/dot_general | solution.py:131
  4.1 0.9 collective-permute-done.1
  5.5 2.5 %fusion.32 = (bf16[256,512]{1,0:T(8,128)(2,1)}, bf16[256,512]{1,0:T(8,128)(2,1)S(1)}, bf16[256,512]{1,0:T(8,128)(2,1)}, bf16[256,512]{1,0:T(8,128)(2,1)S(1)}) fusion(bf16[1,960,2048]{2,1,0:T(8,128)(2,1)} %param.6, s32[]{:T(128)S(6)} %select_n.201, s32[512]{0:T(512)S(1)} %get-tuple-element.89, s32[256]{0:T(256)S(1)} %iota_add_fusion.4, s32[]{:T(128)S(6)} %select_n.200, ...), kind=kLoop, calls=%fused_computation.55 | loop fusion | flops 3670016 | bytes 2106384 | tf_op jit(solution)/shard_map/convert_element_type | solution.py:86
  8.0 2.7 %collective-permute-start.2 = (f32[64,512]{1,0:T(8,128)S(1)}, f32[64,512]{1,0:T(8,128)S(1)}, u32[]{:S(2)}, u32[]{:S(2)}) collective-permute-start(f32[64,512]{1,0:T(8,128)S(1)} %get-tuple-element.79), channel_id=1, source_target_pairs={{0,2},{1,3},{2,0},{3,1},{4,6},{5,7},{6,4},{7,5},{8,10},{9,11},{10,... | collective-permute-start | bytes 393224 | tf_op jit(solution)/shard_map/ppermute | solution.py:10
  10.7 1.4 %collective-permute-start.4 = (f32[64,512]{1,0:T(8,128)S(1)}, f32[64,512]{1,0:T(8,128)S(1)}, u32[]{:S(2)}, u32[]{:S(2)}) collective-permute-start(f32[64,512]{1,0:T(8,128)S(1)} %get-tuple-element.79), channel_id=1, source_target_pairs={{0,6},{1,7},{2,4},{3,5},{4,2},{5,3},{6,0},{7,1},{8,14},{9,15},{10,... | collective-permute-start | bytes 393224 | tf_op jit(solution)/shard_map/ppermute | solution.py:14
  12.3 1.1 %dynamic-slice_bitcast_fusion.8 = (bf16[512,128]{1,0:T(8,128)(2,1)S(1)}, bf16[512,128]{1,0:T(8,128)(2,1)S(1)}, bf16[512,128]{1,0:T(8,128)(2,1)S(1)}, bf16[512,128]{1,0:T(8,128)(2,1)S(1)}) fusion(bf16[1,512,8704]{2,1,0:T(8,128)(2,1)} %param.5, s32[]{:T(128)S(6)} %select_n.208, s32[]{:T(128)S(6)} %select_n.207, s32[]{:T(128)S(6)} %select_n.206, s32[]{:T(128)S(6)} %select_n.205), kind=kLoop, calls=%fused_computation.95 | loop fusion | bytes 1048592 | tf_op jit(solution)/shard_map/dynamic_slice | solution.py:97
  13.5 3.6 %collective-permute-done.2 = f32[64,512]{1,0:T(8,128)S(1)} collective-permute-done((f32[64,512]{1,0:T(8,128)S(1)}, f32[64,512]{1,0:T(8,128)S(1)}, u32[]{:S(2)}, u32[]{:S(2)}) %collective-permute-start.2) | collective-permute-done | bytes 131104 | tf_op jit(solution)/shard_map/ppermute | solution.py:10
  17.0 1.0 %collective-permute-done.4 = f32[64,512]{1,0:T(8,128)S(1)} collective-permute-done((f32[64,512]{1,0:T(8,128)S(1)}, f32[64,512]{1,0:T(8,128)S(1)}, u32[]{:S(2)}, u32[]{:S(2)}) %collective-permute-start.4) | collective-permute-done | bytes 131104 | tf_op jit(solution)/shard_map/ppermute | solution.py:14
  18.0 0.8 collective-permute-done.3
  18.8 1.8 %collective-permute-start.5 = (f32[64,512]{1,0:T(8,128)S(1)}, f32[64,512]{1,0:T(8,128)S(1)}, u32[]{:S(2)}, u32[]{:S(2)}) collective-permute-start(f32[64,512]{1,0:T(8,128)S(1)} %add_add_fusion.2), channel_id=1, source_target_pairs={{0,8},{4,12},{8,0},{12,4},{16,24},{20,28},{24,16},{28,20},{1,9},{5... | collective-permute-start | bytes 393224 | tf_op jit(solution)/shard_map/ppermute | solution.py:12
  20.7 2.1 %fusion.43 = (bf16[128,512]{1,0:T(8,128)(2,1)}, bf16[128,512]{1,0:T(8,128)(2,1)S(1)}, bf16[128,512]{1,0:T(8,128)(2,1)}, bf16[128,512]{1,0:T(8,128)(2,1)S(1)}) fusion(bf16[1,960,2048]{2,1,0:T(8,128)(2,1)} %param.6, s32[]{:T(128)S(6)} %select_n.201, s32[512]{0:T(512)S(1)} %get-tuple-element.89, s32[128]{0:T(128)S(1)} %iota_add_fusion.5, s32[]{:T(128)S(6)} %select_n.200, ...), kind=kLoop, calls=%fused_computation.76 | loop fusion | flops 1835008 | bytes 1057296 | tf_op jit(solution)/shard_map/convert_element_type | solution.py:86
  22.7 1.1 %collective-permute-done.5 = f32[64,512]{1,0:T(8,128)S(1)} collective-permute-done((f32[64,512]{1,0:T(8,128)S(1)}, f32[64,512]{1,0:T(8,128)S(1)}, u32[]{:S(2)}, u32[]{:S(2)}) %collective-permute-start.5) | collective-permute-done | bytes 131104 | tf_op jit(solution)/shard_map/ppermute | solution.py:12
  23.9 2.9 %collective-permute-start.6 = (f32[64,512]{1,0:T(8,128)S(1)}, f32[64,512]{1,0:T(8,128)S(1)}, u32[]{:S(2)}, u32[]{:S(2)}) collective-permute-start(f32[64,512]{1,0:T(8,128)S(1)} %add.488), channel_id=1, source_target_pairs={{0,16},{4,20},{8,24},{12,28},{16,0},{20,4},{24,8},{28,12},{1,17},{... | collective-permute-start | bytes 393224 | tf_op jit(solution)/shard_map/ppermute | solution.py:12
  26.7 1.7 %dynamic-slice_bitcast_fusion = (bf16[512,512]{1,0:T(8,128)(2,1)S(1)}, bf16[512,512]{1,0:T(8,128)(2,1)S(1)}, bf16[512,512]{1,0:T(8,128)(2,1)S(1)}, bf16[512,512]{1,0:T(8,128)(2,1)S(1)}) fusion(bf16[1,512,8704]{2,1,0:T(8,128)(2,1)} %param.5, s32[]{:T(128)S(6)} %select_n.234, s32[]{:T(128)S(6)} %select_n.232, s32[]{:T(128)S(6)} %select_n.231, s32[]{:T(128)S(6)} %select_n.233), kind=kLoop, calls=%fused_computation.65 | loop fusion | bytes 4194320 | tf_op jit(solution)/shard_map/dynamic_slice | solution.py:97
  28.4 3.0 %collective-permute-done.6 = f32[64,512]{1,0:T(8,128)S(1)} collective-permute-done((f32[64,512]{1,0:T(8,128)S(1)}, f32[64,512]{1,0:T(8,128)S(1)}, u32[]{:S(2)}, u32[]{:S(2)}) %collective-permute-start.6) | collective-permute-done | bytes 131104 | tf_op jit(solution)/shard_map/ppermute | solution.py:12
  31.4 0.7 add_bitcast_fusion.1
  32.5 0.6 collective-permute-start.7
  33.7 1.6 %collective-permute-start.9 = (f32[64,128]{1,0:T(8,128)S(1)}, f32[64,128]{1,0:T(8,128)S(1)}, u32[]{:S(2)}, u32[]{:S(2)}) collective-permute-start(f32[64,128]{1,0:T(8,128)S(1)} %convolution_add_fusion.15), channel_id=1, source_target_pairs={{0,2},{1,3},{2,0},{3,1},{4,6},{5,7},{6,4},{7,5},{8,10},{9,11},{10,... | collective-permute-start | bytes 98312 | tf_op jit(solution)/shard_map/ppermute | solution.py:10
  35.2 0.6 broadcast_compare_fusion.2
  35.9 1.7 %collective-permute-done.9 = f32[64,128]{1,0:T(8,128)S(1)} collective-permute-done((f32[64,128]{1,0:T(8,128)S(1)}, f32[64,128]{1,0:T(8,128)S(1)}, u32[]{:S(2)}, u32[]{:S(2)}) %collective-permute-start.9) | collective-permute-done | bytes 32800 | tf_op jit(solution)/shard_map/ppermute | solution.py:10
  37.6 1.0 %fusion.20 = bf16[64,128]{1,0:T(8,128)(2,1)S(1)} fusion(f32[64,128]{1,0:T(8,128)S(1)} %collective-permute-done.9, f32[64,128]{1,0:T(8,128)S(1)} %collective-permute-done.7, bf16[64,512]{1,0:T(8,128)(2,1)S(1)} %get-tuple-element.82, bf16[512,128]{1,0:T(8,128)(2,1)S(1)} %get-tuple-element.29, f32[1,64,960]{2,1,0:T(8,128)} %param.4, ...), kind=kOutput, calls=%fused_computation.37 | convolution fusion | flops 8429568 | bytes 311424 | tf_op jit(solution)/shard_map/dot_general | solution.py:120
  38.6 1.0 %fusion.63 = f32[64,512]{1,0:T(8,128)S(1)} fusion(bf16[64,128]{1,0:T(8,128)(2,1)S(1)} %fusion.20, bf16[128,512]{1,0:T(8,128)(2,1)} %get-tuple-element.36), kind=kOutput, calls=%fused_computation.129 | convolution fusion | flops 8388608 | bytes 278528 | tf_op jit(solution)/shard_map/dot_general | solution.py:135
  39.8 1.0 %fusion.62 = f32[64,512]{1,0:T(8,128)S(1)} fusion(bf16[64,128]{1,0:T(8,128)(2,1)S(1)} %fusion.20, bf16[128,512]{1,0:T(8,128)(2,1)} %get-tuple-element.34), kind=kOutput, calls=%fused_computation.128 | convolution fusion | flops 8388608 | bytes 278528 | tf_op jit(solution)/shard_map/dot_general | solution.py:135
  40.8 0.6 collective-permute-start.10
  41.4 0.8 convolution_add_fusion.7
  42.2 1.5 %collective-permute-start.12 = (f32[64,512]{1,0:T(8,128)}, f32[64,512]{1,0:T(8,128)}, u32[]{:S(2)}, u32[]{:S(2)}) collective-permute-start(f32[64,512]{1,0:T(8,128)} %convolution_add_fusion.7), channel_id=1, source_target_pairs={{0,2},{1,3},{2,0},{3,1},{4,6},{5,7},{6,4},{7,5},{8,10},{9,11},{10,... | collective-permute-start | bytes 393224 | tf_op jit(solution)/shard_map/ppermute | solution.py:10
  43.7 1.4 %collective-permute-start.14 = (f32[64,512]{1,0:T(8,128)}, f32[64,512]{1,0:T(8,128)}, u32[]{:S(2)}, u32[]{:S(2)}) collective-permute-start(f32[64,512]{1,0:T(8,128)} %convolution_add_fusion.7), channel_id=1, source_target_pairs={{0,6},{1,7},{2,4},{3,5},{4,2},{5,3},{6,0},{7,1},{8,14},{9,15},{10,... | collective-permute-start | bytes 393224 | tf_op jit(solution)/shard_map/ppermute | solution.py:14
  45.1 0.8 convolution_add_fusion.8
  46.5 2.0 %dynamic-slice_bitcast_fusion.4 = (bf16[512,256]{1,0:T(8,128)(2,1)}, bf16[512,256]{1,0:T(8,128)(2,1)S(1)}, bf16[512,256]{1,0:T(8,128)(2,1)S(1)}, bf16[512,256]{1,0:T(8,128)(2,1)S(1)}) fusion(bf16[1,512,8704]{2,1,0:T(8,128)(2,1)} %param.5, s32[]{:T(128)S(6)} %select_n.220, s32[]{:T(128)S(6)} %select_n.219, s32[]{:T(128)S(6)} %select_n.218, s32[]{:T(128)S(6)} %select_n.217), kind=kLoop, calls=%fused_computation.86 | loop fusion | bytes 2097168 | tf_op jit(solution)/shard_map/dynamic_slice | solution.py:97
  48.4 0.8 broadcast_compare_fusion.1
  49.3 1.2 %collective-permute-done.12 = f32[64,512]{1,0:T(8,128)} collective-permute-done((f32[64,512]{1,0:T(8,128)}, f32[64,512]{1,0:T(8,128)}, u32[]{:S(2)}, u32[]{:S(2)}) %collective-permute-start.12) | collective-permute-done | bytes 131104 | tf_op jit(solution)/shard_map/ppermute | solution.py:10
  50.9 1.0 %collective-permute-done.13 = f32[64,512]{1,0:T(8,128)} collective-permute-done((f32[64,512]{1,0:T(8,128)}, f32[64,512]{1,0:T(8,128)}, u32[]{:S(2)}, u32[]{:S(2)}) %collective-permute-start.13) | collective-permute-done | bytes 131104 | tf_op jit(solution)/shard_map/ppermute | solution.py:12
  52.0 1.1 %add_add_fusion.1 = f32[64,512]{1,0:T(8,128)S(1)} fusion(f32[64,512]{1,0:T(8,128)} %collective-permute-done.13, f32[64,512]{1,0:T(8,128)} %collective-permute-done.14, f32[64,512]{1,0:T(8,128)} %convolution_add_fusion.8, f32[64,512]{1,0:T(8,128)} %collective-permute-done.12), kind=kLoop, calls=%fused_computation.94 | loop fusion | flops 98304 | bytes 655360 | tf_op jit(solution)/shard_map/add | solution.py:44
  53.1 0.7 collective-permute-start.15
  53.8 1.5 %fusion.21 = f32[64,1024]{1,0:T(8,128)S(1)} fusion(bf16[64,512]{1,0:T(8,128)(2,1)S(1)} %get-tuple-element.82, bf16[512,8704]{1,0:T(8,128)(2,1)} %bitcast.137), kind=kOutput, calls=%fused_computation.38 | convolution fusion | flops 67108864 | bytes 1376256 | tf_op jit(solution)/shard_map/dot_general | solution.py:145
  55.4 2.8 %collective-permute-done.15 = f32[64,512]{1,0:T(8,128)S(1)} collective-permute-done((f32[64,512]{1,0:T(8,128)S(1)}, f32[64,512]{1,0:T(8,128)S(1)}, u32[]{:S(2)}, u32[]{:S(2)}) %collective-permute-start.15) | collective-permute-done | bytes 131104 | tf_op jit(solution)/shard_map/ppermute | solution.py:12
  58.1 1.1 %convolution_add_fusion.11 = f32[64,256]{1,0:T(8,128)S(1)} fusion(bf16[64,512]{1,0:T(8,128)(2,1)S(1)} %get-tuple-element.84, bf16[512,256]{1,0:T(8,128)(2,1)} %get-tuple-element.40, f32[64,1024]{1,0:T(8,128)S(1)} %fusion.21, s32[]{:T(128)S(6)} %select_n.224), kind=kOutput, calls=%fused_computation.22 | convolution fusion | flops 16793600 | bytes 458756 | tf_op jit(solution)/shard_map/dot_general | solution.py:120
  59.5 0.6 collective-permute-start.16
  60.8 1.6 %collective-permute-start.18 = (f32[64,256]{1,0:T(8,128)S(1)}, f32[64,256]{1,0:T(8,128)S(1)}, u32[]{:S(2)}, u32[]{:S(2)}) collective-permute-start(f32[64,256]{1,0:T(8,128)S(1)} %fusion.11), channel_id=1, source_target_pairs={{0,2},{1,3},{2,0},{3,1},{4,6},{5,7},{6,4},{7,5},{8,10},{9,11},{10,... | collective-permute-start | bytes 196616 | tf_op jit(solution)/shard_map/ppermute | solution.py:10
  62.3 2.1 %fusion = f32[64,2048]{1,0:T(8,128)S(1)} fusion(bf16[64,512]{1,0:T(8,128)(2,1)S(1)} %get-tuple-element.84, bf16[512,8704]{1,0:T(8,128)(2,1)} %bitcast.138), kind=kOutput, calls=%fused_computation.1 | convolution fusion | flops 134217728 | bytes 2686976 | tf_op jit(solution)/shard_map/dot_general | solution.py:145
  64.4 0.7 collective-permute-done.18
  65.1 1.1 %fusion.16 = bf16[64,256]{1,0:T(8,128)(2,1)S(1)} fusion(f32[64,256]{1,0:T(8,128)S(1)} %collective-permute-done.18, f32[64,256]{1,0:T(8,128)S(1)} %collective-permute-done.16, bf16[64,512]{1,0:T(8,128)(2,1)S(1)} %get-tuple-element.84, bf16[512,256]{1,0:T(8,128)(2,1)S(1)} %get-tuple-element.37, f32[64,1024]{1,0:T(8,128)S(1)} %fusion.21, s32[]{:T(128)S(6)} %select_n.221, ...), kind=kOutput, calls=%fused_computation.31 | convolution fusion | flops 16875520 | bytes 622852 | tf_op jit(solution)/shard_map/dot_general | solution.py:120
  66.2 1.1 %fusion.65 = f32[64,512]{1,0:T(8,128)S(1)} fusion(bf16[64,256]{1,0:T(8,128)(2,1)S(1)} %fusion.16, bf16[256,512]{1,0:T(8,128)(2,1)} %get-tuple-element.44), kind=kOutput, calls=%fused_computation.131 | convolution fusion | flops 16777216 | bytes 425984 | tf_op jit(solution)/shard_map/dot_general | solution.py:135
  67.4 1.1 %fusion.64 = f32[64,512]{1,0:T(8,128)S(1)} fusion(bf16[64,256]{1,0:T(8,128)(2,1)S(1)} %fusion.16, bf16[256,512]{1,0:T(8,128)(2,1)} %get-tuple-element.42), kind=kOutput, calls=%fused_computation.130 | convolution fusion | flops 16777216 | bytes 425984 | tf_op jit(solution)/shard_map/dot_general | solution.py:135
  68.5 0.6 collective-permute-start.19
  69.2 1.6 %collective-permute-start.21 = (f32[64,512]{1,0:T(8,128)S(1)}, f32[64,512]{1,0:T(8,128)S(1)}, u32[]{:S(2)}, u32[]{:S(2)}) collective-permute-start(f32[64,512]{1,0:T(8,128)S(1)} %convolution_add_fusion.9), channel_id=1, source_target_pairs={{0,2},{1,3},{2,0},{3,1},{4,6},{5,7},{6,4},{7,5},{8,10},{9,11},{10,... | collective-permute-start | bytes 393224 | tf_op jit(solution)/shard_map/ppermute | solution.py:10
  70.8 1.4 %collective-permute-start.23 = (f32[64,512]{1,0:T(8,128)S(1)}, f32[64,512]{1,0:T(8,128)S(1)}, u32[]{:S(2)}, u32[]{:S(2)}) collective-permute-start(f32[64,512]{1,0:T(8,128)S(1)} %convolution_add_fusion.9), channel_id=1, source_target_pairs={{0,6},{1,7},{2,4},{3,5},{4,2},{5,3},{6,0},{7,1},{8,14},{9,15},{10,... | collective-permute-start | bytes 393224 | tf_op jit(solution)/shard_map/ppermute | solution.py:14
  72.4 0.6 collective-permute-start.22
  73.0 2.1 %convolution_add_fusion = f32[64,2048]{1,0:T(8,128)S(1)} fusion(f32[64,2048]{1,0:T(8,128)S(1)} %fusion, bf16[64,512]{1,0:T(8,128)(2,1)S(1)} %get-tuple-element.82, bf16[512,8704]{1,0:T(8,128)(2,1)} %bitcast.139), kind=kOutput, calls=%fused_computation | convolution fusion | flops 134348800 | bytes 3211264 | tf_op jit(solution)/shard_map/dot_general | solution.py:145
  75.1 1.9 %collective-permute-done.21 = f32[64,512]{1,0:T(8,128)S(1)} collective-permute-done((f32[64,512]{1,0:T(8,128)S(1)}, f32[64,512]{1,0:T(8,128)S(1)}, u32[]{:S(2)}, u32[]{:S(2)}) %collective-permute-start.21) | collective-permute-done | bytes 131104 | tf_op jit(solution)/shard_map/ppermute | solution.py:10
  76.9 1.1 %collective-permute-done.23 = f32[64,512]{1,0:T(8,128)S(1)} collective-permute-done((f32[64,512]{1,0:T(8,128)S(1)}, f32[64,512]{1,0:T(8,128)S(1)}, u32[]{:S(2)}, u32[]{:S(2)}) %collective-permute-start.23) | collective-permute-done | bytes 131104 | tf_op jit(solution)/shard_map/ppermute | solution.py:14
  78.0 0.7 collective-permute-done.22
  79.3 0.6 collective-permute-start.24
  79.8 0.6 collective-permute-done.25
  80.6 1.6 %collective-permute-start.26 = (f32[64,512]{1,0:T(8,128)S(1)}, f32[64,512]{1,0:T(8,128)S(1)}, u32[]{:S(2)}, u32[]{:S(2)}) collective-permute-start(f32[64,512]{1,0:T(8,128)S(1)} %fusion.5), channel_id=1, source_target_pairs={{0,2},{1,3},{2,0},{3,1},{4,6},{5,7},{6,4},{7,5},{8,10},{9,11},{10,... | collective-permute-start | bytes 393224 | tf_op jit(solution)/shard_map/ppermute | solution.py:10
  82.2 1.0 %fusion.24 = (bf16[512,512]{1,0:T(8,128)(2,1)S(1)}, bf16[512,512]{1,0:T(8,128)(2,1)S(1)}, bf16[512,512]{1,0:T(8,128)(2,1)S(1)}, bf16[512,512]{1,0:T(8,128)(2,1)S(1)}) fusion(bf16[1,960,2048]{2,1,0:T(8,128)(2,1)S(1)} %copy-done, s32[]{:T(128)S(6)} %select_n.201, s32[512]{0:T(512)S(1)} %get-tuple-element.89, s32[512]{0:T(512)S(1)} %iota_add_fusion.3, ...), kind=kLoop, calls=%fused_computation.42 | loop fusion | flops 7340032 | bytes 4204560 | tf_op jit(solution)/shard_map/convert_element_type | solution.py:86
  83.8 2.4 %collective-permute-done.26 = f32[64,512]{1,0:T(8,128)S(1)} collective-permute-done((f32[64,512]{1,0:T(8,128)S(1)}, f32[64,512]{1,0:T(8,128)S(1)}, u32[]{:S(2)}, u32[]{:S(2)}) %collective-permute-start.26) | collective-permute-done | bytes 131104 | tf_op jit(solution)/shard_map/ppermute | solution.py:10
  86.9 0.6 collective-permute-start.27
  87.5 0.6 collective-permute-done.28
  88.3 1.6 %collective-permute-start.29 = (f32[64,512]{1,0:T(8,128)S(1)}, f32[64,512]{1,0:T(8,128)S(1)}, u32[]{:S(2)}, u32[]{:S(2)}) collective-permute-start(f32[64,512]{1,0:T(8,128)S(1)} %convolution_add_fusion.1), channel_id=1, source_target_pairs={{0,2},{1,3},{2,0},{3,1},{4,6},{5,7},{6,4},{7,5},{8,10},{9,11},{10,... | collective-permute-start | bytes 393224 | tf_op jit(solution)/shard_map/ppermute | solution.py:10
  89.9 4.0 %collective-permute-done.29 = f32[64,512]{1,0:T(8,128)S(1)} collective-permute-done((f32[64,512]{1,0:T(8,128)S(1)}, f32[64,512]{1,0:T(8,128)S(1)}, u32[]{:S(2)}, u32[]{:S(2)}) %collective-permute-start.29) | collective-permute-done | bytes 131104 | tf_op jit(solution)/shard_map/ppermute | solution.py:10
  94.1 0.8 maximum_bitcast_fusion
  (57 shorter events, 7.0 us)
Async XLA Ops:
  3.5 1.5 %collective-permute-start.1 = (f32[64,512]{1,0:T(8,128)S(1)}, f32[64,512]{1,0:T(8,128)S(1)}, u32[]{:S(2)}, u32[]{:S(2)}) collective-permute-start(f32[64,512]{1,0:T(8,128)S(1)} %constant_dynamic-slice_fusion), channel_id=1, source_target_pairs={{0,1},{1,0},{2,3},{3,2},{4,5},{5,4},{6,7},{7,6},{8,9},{9,8},{10,11... | collective-permute-start | bytes 393224 | tf_op jit(solution)/shard_map/ppermute | solution.py:10
  5.1 7.0 %collective-permute-start = (f32[64,512]{1,0:T(8,128)S(1)}, f32[64,512]{1,0:T(8,128)S(1)}, u32[]{:S(2)}, u32[]{:S(2)}) collective-permute-start(f32[64,512]{1,0:T(8,128)S(1)} %get-tuple-element.80), channel_id=1, source_target_pairs={{0,1},{1,0},{2,3},{3,2},{4,5},{5,4},{6,7},{7,6},{8,9},{9,8},{10,11... | collective-permute-start | bytes 393224 | tf_op jit(solution)/shard_map/ppermute | solution.py:10
  8.0 9.0 %collective-permute-start.2 = (f32[64,512]{1,0:T(8,128)S(1)}, f32[64,512]{1,0:T(8,128)S(1)}, u32[]{:S(2)}, u32[]{:S(2)}) collective-permute-start(f32[64,512]{1,0:T(8,128)S(1)} %get-tuple-element.79), channel_id=1, source_target_pairs={{0,2},{1,3},{2,0},{3,1},{4,6},{5,7},{6,4},{7,5},{8,10},{9,11},{10,... | collective-permute-start | bytes 393224 | tf_op jit(solution)/shard_map/ppermute | solution.py:10
  10.7 7.3 %collective-permute-start.4 = (f32[64,512]{1,0:T(8,128)S(1)}, f32[64,512]{1,0:T(8,128)S(1)}, u32[]{:S(2)}, u32[]{:S(2)}) collective-permute-start(f32[64,512]{1,0:T(8,128)S(1)} %get-tuple-element.79), channel_id=1, source_target_pairs={{0,6},{1,7},{2,4},{3,5},{4,2},{5,3},{6,0},{7,1},{8,14},{9,15},{10,... | collective-permute-start | bytes 393224 | tf_op jit(solution)/shard_map/ppermute | solution.py:14
  12.2 6.6 %collective-permute-start.3 = (f32[64,512]{1,0:T(8,128)S(1)}, f32[64,512]{1,0:T(8,128)S(1)}, u32[]{:S(2)}, u32[]{:S(2)}) collective-permute-start(f32[64,512]{1,0:T(8,128)S(1)} %dynamic-slice_add_fusion.1), channel_id=1, source_target_pairs={{0,4},{4,0},{8,12},{12,8},{16,20},{20,16},{24,28},{28,24},{1,5},{5... | collective-permute-start | bytes 393224 | tf_op jit(solution)/shard_map/ppermute | solution.py:12
  18.8 5.0 %collective-permute-start.5 = (f32[64,512]{1,0:T(8,128)S(1)}, f32[64,512]{1,0:T(8,128)S(1)}, u32[]{:S(2)}, u32[]{:S(2)}) collective-permute-start(f32[64,512]{1,0:T(8,128)S(1)} %add_add_fusion.2), channel_id=1, source_target_pairs={{0,8},{4,12},{8,0},{12,4},{16,24},{20,28},{24,16},{28,20},{1,9},{5... | collective-permute-start | bytes 393224 | tf_op jit(solution)/shard_map/ppermute | solution.py:12
  23.9 7.5 %collective-permute-start.6 = (f32[64,512]{1,0:T(8,128)S(1)}, f32[64,512]{1,0:T(8,128)S(1)}, u32[]{:S(2)}, u32[]{:S(2)}) collective-permute-start(f32[64,512]{1,0:T(8,128)S(1)} %add.488), channel_id=1, source_target_pairs={{0,16},{4,20},{8,24},{12,28},{16,0},{20,4},{24,8},{28,12},{1,17},{... | collective-permute-start | bytes 393224 | tf_op jit(solution)/shard_map/ppermute | solution.py:12
  32.2 1.3 %collective-permute-start.8 = (f32[64,128]{1,0:T(8,128)S(1)}, f32[64,128]{1,0:T(8,128)S(1)}, u32[]{:S(2)}, u32[]{:S(2)}) collective-permute-start(f32[64,128]{1,0:T(8,128)S(1)} %fusion.61), channel_id=1, source_target_pairs={{0,1},{1,0},{2,3},{3,2},{4,5},{5,4},{6,7},{7,6},{8,9},{9,8},{10,11... | collective-permute-start | bytes 98312 | tf_op jit(solution)/shard_map/ppermute | solution.py:10
  32.5 3.5 %collective-permute-start.7 = (f32[64,128]{1,0:T(8,128)S(1)}, f32[64,128]{1,0:T(8,128)S(1)}, u32[]{:S(2)}, u32[]{:S(2)}) collective-permute-start(f32[64,128]{1,0:T(8,128)S(1)} %fusion.60), channel_id=1, source_target_pairs={{0,1},{1,0},{2,3},{3,2},{4,5},{5,4},{6,7},{7,6},{8,9},{9,8},{10,11... | collective-permute-start | bytes 98312 | tf_op jit(solution)/shard_map/ppermute | solution.py:10
  33.7 4.0 %collective-permute-start.9 = (f32[64,128]{1,0:T(8,128)S(1)}, f32[64,128]{1,0:T(8,128)S(1)}, u32[]{:S(2)}, u32[]{:S(2)}) collective-permute-start(f32[64,128]{1,0:T(8,128)S(1)} %convolution_add_fusion.15), channel_id=1, source_target_pairs={{0,2},{1,3},{2,0},{3,1},{4,6},{5,7},{6,4},{7,5},{8,10},{9,11},{10,... | collective-permute-start | bytes 98312 | tf_op jit(solution)/shard_map/ppermute | solution.py:10
  39.7 1.7 %collective-permute-start.11 = (f32[64,512]{1,0:T(8,128)S(1)}, f32[64,512]{1,0:T(8,128)S(1)}, u32[]{:S(2)}, u32[]{:S(2)}) collective-permute-start(f32[64,512]{1,0:T(8,128)S(1)} %fusion.63), channel_id=1, source_target_pairs={{0,1},{1,0},{2,3},{3,2},{4,5},{5,4},{6,7},{7,6},{8,9},{9,8},{10,11... | collective-permute-start | bytes 393224 | tf_op jit(solution)/shard_map/ppermute | solution.py:10
  40.8 4.3 %collective-permute-start.10 = (f32[64,512]{1,0:T(8,128)S(1)}, f32[64,512]{1,0:T(8,128)S(1)}, u32[]{:S(2)}, u32[]{:S(2)}) collective-permute-start(f32[64,512]{1,0:T(8,128)S(1)} %fusion.62), channel_id=1, source_target_pairs={{0,1},{1,0},{2,3},{3,2},{4,5},{5,4},{6,7},{7,6},{8,9},{9,8},{10,11... | collective-permute-start | bytes 393224 | tf_op jit(solution)/shard_map/ppermute | solution.py:10
  42.2 8.3 %collective-permute-start.12 = (f32[64,512]{1,0:T(8,128)}, f32[64,512]{1,0:T(8,128)}, u32[]{:S(2)}, u32[]{:S(2)}) collective-permute-start(f32[64,512]{1,0:T(8,128)} %convolution_add_fusion.7), channel_id=1, source_target_pairs={{0,2},{1,3},{2,0},{3,1},{4,6},{5,7},{6,4},{7,5},{8,10},{9,11},{10,... | collective-permute-start | bytes 393224 | tf_op jit(solution)/shard_map/ppermute | solution.py:10
  43.7 7.2 %collective-permute-start.14 = (f32[64,512]{1,0:T(8,128)}, f32[64,512]{1,0:T(8,128)}, u32[]{:S(2)}, u32[]{:S(2)}) collective-permute-start(f32[64,512]{1,0:T(8,128)} %convolution_add_fusion.7), channel_id=1, source_target_pairs={{0,6},{1,7},{2,4},{3,5},{4,2},{5,3},{6,0},{7,1},{8,14},{9,15},{10,... | collective-permute-start | bytes 393224 | tf_op jit(solution)/shard_map/ppermute | solution.py:14
  45.9 6.0 %collective-permute-start.13 = (f32[64,512]{1,0:T(8,128)}, f32[64,512]{1,0:T(8,128)}, u32[]{:S(2)}, u32[]{:S(2)}) collective-permute-start(f32[64,512]{1,0:T(8,128)} %convolution_add_fusion.8), channel_id=1, source_target_pairs={{0,4},{4,0},{8,12},{12,8},{16,20},{20,16},{24,28},{28,24},{1,5},{5... | collective-permute-start | bytes 393224 | tf_op jit(solution)/shard_map/ppermute | solution.py:12
  48.4 33.7 %copy-start = (bf16[1,960,2048]{2,1,0:T(8,128)(2,1)S(1)}, bf16[1,960,2048]{2,1,0:T(8,128)(2,1)}, u32[]{:S(2)}) copy-start(bf16[1,960,2048]{2,1,0:T(8,128)(2,1)} %param.6) | copy-start | bytes 11796484
  53.1 5.0 %collective-permute-start.15 = (f32[64,512]{1,0:T(8,128)S(1)}, f32[64,512]{1,0:T(8,128)S(1)}, u32[]{:S(2)}, u32[]{:S(2)}) collective-permute-start(f32[64,512]{1,0:T(8,128)S(1)} %add_add_fusion.1), channel_id=1, source_target_pairs={{0,8},{4,12},{8,0},{12,4},{16,24},{20,28},{24,16},{28,20},{1,9},{5... | collective-permute-start | bytes 393224 | tf_op jit(solution)/shard_map/ppermute | solution.py:12
  55.3 30.9 %copy-start.2 = (f32[1,64,960]{2,1,0:T(8,128)S(1)}, f32[1,64,960]{2,1,0:T(8,128)}, u32[]{:S(2)}) copy-start(f32[1,64,960]{2,1,0:T(8,128)} %param.4) | copy-start | bytes 737284
  59.3 1.3 %collective-permute-start.17 = (f32[64,256]{1,0:T(8,128)S(1)}, f32[64,256]{1,0:T(8,128)S(1)}, u32[]{:S(2)}, u32[]{:S(2)}) collective-permute-start(f32[64,256]{1,0:T(8,128)S(1)} %convolution_add_fusion.11), channel_id=1, source_target_pairs={{0,1},{1,0},{2,3},{3,2},{4,5},{5,4},{6,7},{7,6},{8,9},{9,8},{10,11... | collective-permute-start | bytes 196616 | tf_op jit(solution)/shard_map/ppermute | solution.py:10
  59.5 4.9 %collective-permute-start.16 = (f32[64,256]{1,0:T(8,128)S(1)}, f32[64,256]{1,0:T(8,128)S(1)}, u32[]{:S(2)}, u32[]{:S(2)}) collective-permute-start(f32[64,256]{1,0:T(8,128)S(1)} %convolution_add_fusion.13), channel_id=1, source_target_pairs={{0,1},{1,0},{2,3},{3,2},{4,5},{5,4},{6,7},{7,6},{8,9},{9,8},{10,11... | collective-permute-start | bytes 196616 | tf_op jit(solution)/shard_map/ppermute | solution.py:10
  60.8 4.3 %collective-permute-start.18 = (f32[64,256]{1,0:T(8,128)S(1)}, f32[64,256]{1,0:T(8,128)S(1)}, u32[]{:S(2)}, u32[]{:S(2)}) collective-permute-start(f32[64,256]{1,0:T(8,128)S(1)} %fusion.11), channel_id=1, source_target_pairs={{0,2},{1,3},{2,0},{3,1},{4,6},{5,7},{6,4},{7,5},{8,10},{9,11},{10,... | collective-permute-start | bytes 196616 | tf_op jit(solution)/shard_map/ppermute | solution.py:10
  64.4 29.7 %copy-start.1 = (f32[1,64,512]{2,1,0:T(8,128)S(1)}, f32[1,64,512]{2,1,0:T(8,128)}, u32[]{:S(2)}) copy-start(f32[1,64,512]{2,1,0:T(8,128)} %get-tuple-element.81) | copy-start | bytes 393220
  67.3 1.8 %collective-permute-start.20 = (f32[64,512]{1,0:T(8,128)S(1)}, f32[64,512]{1,0:T(8,128)S(1)}, u32[]{:S(2)}, u32[]{:S(2)}) collective-permute-start(f32[64,512]{1,0:T(8,128)S(1)} %fusion.65), channel_id=1, source_target_pairs={{0,1},{1,0},{2,3},{3,2},{4,5},{5,4},{6,7},{7,6},{8,9},{9,8},{10,11... | collective-permute-start | bytes 393224 | tf_op jit(solution)/shard_map/ppermute | solution.py:10
  68.5 3.8 %collective-permute-start.19 = (f32[64,512]{1,0:T(8,128)S(1)}, f32[64,512]{1,0:T(8,128)S(1)}, u32[]{:S(2)}, u32[]{:S(2)}) collective-permute-start(f32[64,512]{1,0:T(8,128)S(1)} %fusion.64), channel_id=1, source_target_pairs={{0,1},{1,0},{2,3},{3,2},{4,5},{5,4},{6,7},{7,6},{8,9},{9,8},{10,11... | collective-permute-start | bytes 393224 | tf_op jit(solution)/shard_map/ppermute | solution.py:10
  69.2 7.7 %collective-permute-start.21 = (f32[64,512]{1,0:T(8,128)S(1)}, f32[64,512]{1,0:T(8,128)S(1)}, u32[]{:S(2)}, u32[]{:S(2)}) collective-permute-start(f32[64,512]{1,0:T(8,128)S(1)} %convolution_add_fusion.9), channel_id=1, source_target_pairs={{0,2},{1,3},{2,0},{3,1},{4,6},{5,7},{6,4},{7,5},{8,10},{9,11},{10,... | collective-permute-start | bytes 393224 | tf_op jit(solution)/shard_map/ppermute | solution.py:10
  70.8 7.3 %collective-permute-start.23 = (f32[64,512]{1,0:T(8,128)S(1)}, f32[64,512]{1,0:T(8,128)S(1)}, u32[]{:S(2)}, u32[]{:S(2)}) collective-permute-start(f32[64,512]{1,0:T(8,128)S(1)} %convolution_add_fusion.9), channel_id=1, source_target_pairs={{0,6},{1,7},{2,4},{3,5},{4,2},{5,3},{6,0},{7,1},{8,14},{9,15},{10,... | collective-permute-start | bytes 393224 | tf_op jit(solution)/shard_map/ppermute | solution.py:14
  72.4 6.3 %collective-permute-start.22 = (f32[64,512]{1,0:T(8,128)S(1)}, f32[64,512]{1,0:T(8,128)S(1)}, u32[]{:S(2)}, u32[]{:S(2)}) collective-permute-start(f32[64,512]{1,0:T(8,128)S(1)} %convolution_add_fusion.10), channel_id=1, source_target_pairs={{0,4},{4,0},{8,12},{12,8},{16,20},{20,16},{24,28},{28,24},{1,5},{5... | collective-permute-start | bytes 393224 | tf_op jit(solution)/shard_map/ppermute | solution.py:12
  79.0 1.4 %collective-permute-start.25 = (f32[64,512]{1,0:T(8,128)S(1)}, f32[64,512]{1,0:T(8,128)S(1)}, u32[]{:S(2)}, u32[]{:S(2)}) collective-permute-start(f32[64,512]{1,0:T(8,128)S(1)} %convolution_add_fusion.3), channel_id=1, source_target_pairs={{0,1},{1,0},{2,3},{3,2},{4,5},{5,4},{6,7},{7,6},{8,9},{9,8},{10,11... | collective-permute-start | bytes 393224 | tf_op jit(solution)/shard_map/ppermute | solution.py:10
  79.3 4.5 %collective-permute-start.24 = (f32[64,512]{1,0:T(8,128)S(1)}, f32[64,512]{1,0:T(8,128)S(1)}, u32[]{:S(2)}, u32[]{:S(2)}) collective-permute-start(f32[64,512]{1,0:T(8,128)S(1)} %convolution_add_fusion.5), channel_id=1, source_target_pairs={{0,1},{1,0},{2,3},{3,2},{4,5},{5,4},{6,7},{7,6},{8,9},{9,8},{10,11... | collective-permute-start | bytes 393224 | tf_op jit(solution)/shard_map/ppermute | solution.py:10
  80.6 5.6 %collective-permute-start.26 = (f32[64,512]{1,0:T(8,128)S(1)}, f32[64,512]{1,0:T(8,128)S(1)}, u32[]{:S(2)}, u32[]{:S(2)}) collective-permute-start(f32[64,512]{1,0:T(8,128)S(1)} %fusion.5), channel_id=1, source_target_pairs={{0,2},{1,3},{2,0},{3,1},{4,6},{5,7},{6,4},{7,5},{8,10},{9,11},{10,... | collective-permute-start | bytes 393224 | tf_op jit(solution)/shard_map/ppermute | solution.py:10
  86.7 1.4 %collective-permute-start.28 = (f32[64,512]{1,0:T(8,128)S(1)}, f32[64,512]{1,0:T(8,128)S(1)}, u32[]{:S(2)}, u32[]{:S(2)}) collective-permute-start(f32[64,512]{1,0:T(8,128)S(1)} %fusion.67), channel_id=1, source_target_pairs={{0,1},{1,0},{2,3},{3,2},{4,5},{5,4},{6,7},{7,6},{8,9},{9,8},{10,11... | collective-permute-start | bytes 393224 | tf_op jit(solution)/shard_map/ppermute | solution.py:10
  86.9 2.9 %collective-permute-start.27 = (f32[64,512]{1,0:T(8,128)S(1)}, f32[64,512]{1,0:T(8,128)S(1)}, u32[]{:S(2)}, u32[]{:S(2)}) collective-permute-start(f32[64,512]{1,0:T(8,128)S(1)} %fusion.66), channel_id=1, source_target_pairs={{0,1},{1,0},{2,3},{3,2},{4,5},{5,4},{6,7},{7,6},{8,9},{9,8},{10,11... | collective-permute-start | bytes 393224 | tf_op jit(solution)/shard_map/ppermute | solution.py:10
  88.3 5.6 %collective-permute-start.29 = (f32[64,512]{1,0:T(8,128)S(1)}, f32[64,512]{1,0:T(8,128)S(1)}, u32[]{:S(2)}, u32[]{:S(2)}) collective-permute-start(f32[64,512]{1,0:T(8,128)S(1)} %convolution_add_fusion.1), channel_id=1, source_target_pairs={{0,2},{1,3},{2,0},{3,1},{4,6},{5,7},{6,4},{7,5},{8,10},{9,11},{10,... | collective-permute-start | bytes 393224 | tf_op jit(solution)/shard_map/ppermute | solution.py:10

commit v3 on v2

--- a/solution.py
+++ b/solution.py
@@ -21,15 +21,27 @@
     return sorted(range(count), key=lambda m: [-(m >> b & 1) for b in range(bits)])
 
 
-def reduced(chunk_of, leaf_bits):
+def reduced(chunk_of, leaf_bits, direct=False, joined=False):
     count = lax.axis_size("panel")
     bits = count.bit_length() - 1
     held = {}
     arrived = {}
+    if direct:
+        total = None
+        for m in range(count - 1, -1, -1):
+            chunk = chunk_of(m)
+            got = exchanged(chunk, 0, m) if m else chunk
+            total = got if total is None else total + got
+        return total
     for m in chunk_order(count):
         held[m] = chunk_of(m)
-        if m & 1:
+        if m & 1 and not joined:
             arrived[m ^ 1] = exchanged(held[m], 0, 1)
+    if joined:
+        odd = [m for m in held if m & 1]
+        width = held[odd[0]].shape[1]
+        got = exchanged(jnp.concatenate([held[m] for m in odd], axis=1), 0, 1)
+        arrived = {m ^ 1: got[:, i * width : (i + 1) * width] for i, m in enumerate(odd)}
     for bit in range(1, bits + 1):
         held = {m: held[m] + arrived[m] for m in arrived}
         arrived = {}
@@ -49,6 +61,10 @@
             if m & step:
                 arrived[m ^ step] = exchanged(held[m], 0, step)
     return held[0]
+
+
+def exchanged_in_one(panel_count, share):
+    return panel_count <= 4 and share <= 256
 
 
 def per_device(adjoint_rhs, panel_tiles, diag_inverse, front_sizes):
@@ -100,8 +116,26 @@
         width = whole.shape[1] // panel_count
         return lax.dynamic_slice(whole, (0, (panel_pos ^ m) * width), (whole.shape[0], width))
 
+    def alive(height):
+        group_size, _, _, _, _ = sizes(height)
+        front_id = (1 << height) - 1 + leaf_pos // group_size
+        live_size = lax.dynamic_slice(front_sizes, (front_id,), (1,)) if height else front_sizes[:1]
+        return (own_rows(height) < live_size)[None, :]
+
+    def right_of(height):
+        _, _, share, _, row_start = sizes(height)
+        return adjoint_rhs[0, :, row_start : row_start + share]
+
+    def in_one(height):
+        return exchanged_in_one(panel_count, sizes(height)[2])
+
     factors = {}
     couplings = {}
+    lives = {}
+    rights = {}
+    lives = lax.optimization_barrier({h: alive(h) for h in range(1, levels)})
+    for height in range(1, levels):
+        rights[height] = lax.optimization_barrier(right_of(height))
     for height in range(1, levels):
         couplings[height] = lax.optimization_barrier(
             {m: coupling(height, m) for m in range(panel_count)}
@@ -111,25 +145,28 @@
         )
 
     for height in range(levels):
-        group_size, _, share, _, row_start = sizes(height)
+        _, _, share, _, row_start = sizes(height)
         rows = own_rows(height)
-        resid = adjoint_rhs[0, :, row_start : row_start + share]
-        if height > 0:
+        if height == 0:
+            resid = right_of(0)
+            live = alive(0)
+        else:
+            live = lives[height]
 
             def update(m):
                 term = jnp.dot(
                     solved[-1], couplings[height][m], preferred_element_type=jnp.float32
                 )
-                return term + part(base[height], m) if height in base else term
+                for early in base.get(height, ()):
+                    term = term + part(early, m)
+                return term
 
-            resid = resid - reduced(update, 0)
-        front_id = (1 << height) - 1 + leaf_pos // group_size
-        live_size = lax.dynamic_slice(front_sizes, (front_id,), (1,)) if height else front_sizes[:1]
-        resid_low = jnp.where(rows[None, :] < live_size[:, None], resid, 0.0).astype(jnp.bfloat16)
+            resid = rights[height] - reduced(update, 0, direct=in_one(height))
+        resid_low = jnp.where(live, resid, 0.0).astype(jnp.bfloat16)
         if height == 0:
             whole = masked(inverse[row_start : row_start + share], 0, rows)
             terms = jnp.dot(resid_low, whole, preferred_element_type=jnp.float32)
-            mine = reduced(lambda m: part(terms, m), levels - 1 - height)
+            mine = reduced(lambda m: part(terms, m), levels - 1 - height, joined=True)
         else:
             mine = reduced(
                 lambda m: jnp.dot(
@@ -145,7 +182,7 @@
             term = jnp.dot(
                 solved[-1], tiles[:, low : low + width], preferred_element_type=jnp.float32
             )
-            base[later] = base[later] + term if later in base else term
+            base.setdefault(later, []).append(term)
     return jnp.stack(results, axis=0)[None]
 
 

time: 95.6 us -> 104 us (1.088)
  local copies, waits for them, and re-layouts: 6.28 us -> 11.3 us
  other arithmetic: 11.1 us -> 15.3 us
  starting transfers between devices: 27.8 us -> 26.2 us
  matrix products: 18.9 us -> 20 us
    squeeze x0 -> x3, local copies, waits for them, and re-layouts: none -> 3.21 us  [right_of(): return adjoint_rhs[0, :, row_start:row_start + share]]
    ppermute x6, waiting for transfers between devices: 9.34 us -> 12 us  [exchanged(): lax.ppermute(block, 'leaf', [(i, i ^ leaf_flip) for i in range(leaf_count)])]
    ppermute x3, waiting for transfers between devices: 2.5 us -> 0.14 us  [exchanged(): lax.ppermute(block, ('leaf', 'panel'), [(i, i ^ flip) for i in range(leaf...]
    ppermute x21 -> x20, starting transfers between devices: 16.8 us -> 14.5 us  [exchanged(): lax.ppermute(block, 'panel', [(i, i ^ panel_flip) for i in range(panel_co...]
    dot_general x12, matrix products: 4.82 us -> 6.87 us  [update(): jnp.dot(solved[-1], couplings[height][m], preferred_element_type=jnp.floa...]
    dynamic_slice x3, local copies, waits for them, and re-layouts: 4.77 us -> 6.6 us  [coupling(): return lax.dynamic_slice(tiles, (0, low), (tiles.shape[0], share))]
    add x2 -> x1, other arithmetic: 0.04 us -> 1.66 us  [reduced(): held = {m: held[m] + arrived[m] for m in arrived}]
    ppermute x21 -> x20, waiting for transfers between devices: 18.5 us -> 18.1 us  [exchanged(): lax.ppermute(block, 'panel', [(i, i ^ panel_flip) for i in range(panel_co...]
  transfers between devices with their start and end apart: 30 -> 29, of which waited for: 21 -> 17; matrix products, arithmetic and copies ran while one was open for 25% -> 30% of each run, Pallas kernels for 0% -> 0%
where the time goes in v3:
time: 104 us
  waiting for transfers between devices  30.2 us (29%)
  starting transfers between devices  26.2 us (25%)
  matrix products  20 us (19%)
  other arithmetic  15.3 us (15%)
  local copies, waits for them, and re-layouts  11.3 us (11%)
    ppermute x20, waiting for transfers between devices, exchanged(): lax.ppermute(block, 'panel', [(i, i ^ panel_flip) for i in range(panel_co...  18.1 us
    ppermute x20, starting transfers between devices, exchanged(): lax.ppermute(block, 'panel', [(i, i ^ panel_flip) for i in range(panel_co...  14.5 us
    ppermute x6, waiting for transfers between devices, exchanged(): lax.ppermute(block, 'leaf', [(i, i ^ leaf_flip) for i in range(leaf_count)])  12 us
    dot_general x12, matrix products, update(): jnp.dot(solved[-1], couplings[height][m], preferred_element_type=jnp.floa...  6.87 us
    dynamic_slice x3, local copies, waits for them, and re-layouts, coupling(): return lax.dynamic_slice(tiles, (0, low), (tiles.shape[0], share))  6.6 us
    ppermute x6, starting transfers between devices, exchanged(): lax.ppermute(block, 'leaf', [(i, i ^ leaf_flip) for i in range(leaf_count)])  6.5 us
    convert_element_type x3, other arithmetic, masked(): return (kept + one).astype(jnp.bfloat16)  6.46 us
    dot_general x12, matrix products, per_device(): jnp.dot(resid_low, factors[height][m], preferred_element_type=jnp.float32)  6.18 us
  transfers between devices with their start and end apart: 29, of which 17 were waited for; matrix products, arithmetic and copies ran while one was open for 30% of the time, Pallas kernels for 0%

profile of v3, /device:TPU:0, one launch (start us, length us, event | category | flops | bytes accessed | tf_op | source)
XLA Modules:
  0.0 103.5 jit_solution(11291705964213209130)
XLA Ops:
  0.0 1.5 %fusion.54 = (s32[1]{0:T(128)}, s32[1]{0:T(128)}, s32[1]{0:T(128)}, s32[1]{0:T(128)}) fusion(s32[15]{0:T(128)} %param.7, s32[]{:T(128)S(6)} %select_n.214, s32[]{:T(128)S(6)} %select_n.210, s32[]{:T(128)S(6)} %select_n.213), kind=kLoop, calls=%fused_computation.123 | loop fusion | bytes 44 | tf_op jit(solution)/shard_map/dynamic_slice | solution.py:122
  1.5 0.7 broadcast_compare_fusion
  2.1 1.3 %fusion.35 = f32[64,2048]{1,0:T(8,128)S(1)} fusion(bf16[1,960,2048]{2,1,0:T(8,128)(2,1)} %param.6, s32[64]{0:T(128)S(1)} %iota_add_fusion.6, f32[1,64,960]{2,1,0:T(8,128)} %param.4, pred[64]{0:T(512)(128)(4,1)S(1)} %broadcast_compare_fusion), kind=kOutput, calls=%fused_computation.65 | convolution fusion | flops 17698816 | bytes 803136 | tf_op jit(solution)/shard_map/dot_general | solution.py:168
  3.5 0.7 pad_maximum_fusion
  4.7 1.6 %slice_bitcast_fusion.1 = f32[64,256]{1,0:T(8,128)} fusion(f32[1,64,960]{2,1,0:T(8,128)} %param.4), kind=kLoop, calls=%fused_computation.97 | loop fusion | bytes 131072 | tf_op jit(solution)/shard_map/squeeze | solution.py:127
  6.3 2.5 %fusion.19 = (bf16[512,512]{1,0:T(8,128)(2,1)S(1)}, bf16[512,512]{1,0:T(8,128)(2,1)S(1)}, bf16[512,512]{1,0:T(8,128)(2,1)S(1)}, bf16[512,512]{1,0:T(8,128)(2,1)S(1)}) fusion(bf16[1,960,2048]{2,1,0:T(8,128)(2,1)} %param.6, s32[]{:T(128)S(6)} %select_n.205, s32[512]{0:T(512)S(1)} %get-tuple-element.97, s32[512]{0:T(512)S(1)} %get-tuple-element.100, ...), kind=kLoop, calls=%fused_computation.34 | loop fusion | flops 7340032 | bytes 4204560 | tf_op jit(solution)/shard_map/convert_element_type | solution.py:102
  8.9 1.4 %fusion.38 = (bf16[128,512]{1,0:T(8,128)(2,1)S(1)}, bf16[128,512]{1,0:T(8,128)(2,1)S(1)}, bf16[128,512]{1,0:T(8,128)(2,1)S(1)}, bf16[128,512]{1,0:T(8,128)(2,1)S(1)}) fusion(bf16[1,960,2048]{2,1,0:T(8,128)(2,1)} %param.6, s32[]{:T(128)S(6)} %select_n.205, s32[512]{0:T(512)S(1)} %get-tuple-element.97, s32[128]{0:T(128)S(1)} %iota_add_fusion.5, ...), kind=kLoop, calls=%fused_computation.69 | loop fusion | flops 1835008 | bytes 1057296 | tf_op jit(solution)/shard_map/convert_element_type | solution.py:102
  10.3 2.5 %fusion.27 = (bf16[256,512]{1,0:T(8,128)(2,1)}, bf16[256,512]{1,0:T(8,128)(2,1)}, bf16[256,512]{1,0:T(8,128)(2,1)}, bf16[256,512]{1,0:T(8,128)(2,1)S(1)}) fusion(bf16[1,960,2048]{2,1,0:T(8,128)(2,1)} %param.6, s32[]{:T(128)S(6)} %select_n.205, s32[512]{0:T(512)S(1)} %get-tuple-element.97, s32[256]{0:T(256)S(1)} %iota_add_fusion.4, s32[]{:T(128)S(6)} %select_n.207, ...), kind=kLoop, calls=%fused_computation.47 | loop fusion | flops 3670016 | bytes 2106384 | tf_op jit(solution)/shard_map/convert_element_type | solution.py:102
  12.8 1.7 %slice_add_fusion = (f32[64,512]{1,0:T(8,128)}, f32[64,512]{1,0:T(8,128)S(1)}) fusion(f32[64,1024]{1,0:T(8,128)} %collective-permute-done, f32[64,2048]{1,0:T(8,128)S(1)} %fusion.35, s32[]{:T(128)S(6)} %select_n.207, s32[]{:T(128)S(6)} %select_n.204), kind=kLoop, calls=%fused_computation.86 | loop fusion | flops 65536 | bytes 786440 | tf_op jit(solution)/shard_map/add | solution.py:46
  14.5 2.5 %collective-permute-start.1 = (f32[64,512]{1,0:T(8,128)}, f32[64,512]{1,0:T(8,128)S(1)}, u32[]{:S(2)}, u32[]{:S(2)}) collective-permute-start(f32[64,512]{1,0:T(8,128)} %get-tuple-element.85), channel_id=1, source_target_pairs={{0,2},{1,3},{2,0},{3,1},{4,6},{5,7},{6,4},{7,5},{8,10},{9,11},{10,... | collective-permute-start | bytes 393224 | tf_op jit(solution)/shard_map/ppermute | solution.py:10
  17.0 1.4 %collective-permute-start.3 = (f32[64,512]{1,0:T(8,128)}, f32[64,512]{1,0:T(8,128)}, u32[]{:S(2)}, u32[]{:S(2)}) collective-permute-start(f32[64,512]{1,0:T(8,128)} %get-tuple-element.85), channel_id=1, source_target_pairs={{0,6},{1,7},{2,4},{3,5},{4,2},{5,3},{6,0},{7,1},{8,14},{9,15},{10,... | collective-permute-start | bytes 393224 | tf_op jit(solution)/shard_map/ppermute | solution.py:14
  18.5 1.5 %slice_bitcast_fusion.2 = f32[64,128]{1,0:T(8,128)} fusion(f32[1,64,960]{2,1,0:T(8,128)} %param.4), kind=kLoop, calls=%fused_computation.103 | loop fusion | bytes 65536 | tf_op jit(solution)/shard_map/squeeze | solution.py:127
  20.0 1.8 %dynamic-slice_bitcast_fusion.8 = (bf16[512,128]{1,0:T(8,128)(2,1)S(1)}, bf16[512,128]{1,0:T(8,128)(2,1)S(1)}, bf16[512,128]{1,0:T(8,128)(2,1)S(1)}, bf16[512,128]{1,0:T(8,128)(2,1)}) fusion(bf16[1,512,8704]{2,1,0:T(8,128)(2,1)} %param.5, s32[]{:T(128)S(6)} %select_n.218, s32[]{:T(128)S(6)} %select_n.217, s32[]{:T(128)S(6)} %select_n.216, s32[]{:T(128)S(6)} %select_n.215), kind=kLoop, calls=%fused_computation.91 | loop fusion | bytes 1048592 | tf_op jit(solution)/shard_map/dynamic_slice | solution.py:113
  21.8 2.0 %collective-permute-done.1 = f32[64,512]{1,0:T(8,128)S(1)} collective-permute-done((f32[64,512]{1,0:T(8,128)}, f32[64,512]{1,0:T(8,128)S(1)}, u32[]{:S(2)}, u32[]{:S(2)}) %collective-permute-start.1) | collective-permute-done | bytes 131104 | tf_op jit(solution)/shard_map/ppermute | solution.py:10
  23.8 1.7 %collective-permute-done.2 = f32[64,512]{1,0:T(8,128)} collective-permute-done((f32[64,512]{1,0:T(8,128)S(1)}, f32[64,512]{1,0:T(8,128)}, u32[]{:S(2)}, u32[]{:S(2)}) %collective-permute-start.2) | collective-permute-done | bytes 131104 | tf_op jit(solution)/shard_map/ppermute | solution.py:12
  25.6 1.1 %add_add_fusion.2 = f32[64,512]{1,0:T(8,128)S(1)} fusion(f32[64,512]{1,0:T(8,128)} %collective-permute-done.2, f32[64,512]{1,0:T(8,128)} %collective-permute-done.3, f32[64,512]{1,0:T(8,128)S(1)} %get-tuple-element.86, f32[64,512]{1,0:T(8,128)} %copy-done.4), kind=kLoop, calls=%fused_computation.95 | loop fusion | flops 98304 | bytes 655360 | tf_op jit(solution)/shard_map/add | solution.py:56
  26.7 1.8 %collective-permute-start.4 = (f32[64,512]{1,0:T(8,128)S(1)}, f32[64,512]{1,0:T(8,128)S(1)}, u32[]{:S(2)}, u32[]{:S(2)}) collective-permute-start(f32[64,512]{1,0:T(8,128)S(1)} %add_add_fusion.2), channel_id=1, source_target_pairs={{0,8},{4,12},{8,0},{12,4},{16,24},{20,28},{24,16},{28,20},{1,9},{5... | collective-permute-start | bytes 393224 | tf_op jit(solution)/shard_map/ppermute | solution.py:12
  28.5 0.6 add_compare_fusion.1
  29.1 0.7 add_compare_fusion
  29.8 2.0 %collective-permute-done.4 = f32[64,512]{1,0:T(8,128)S(1)} collective-permute-done((f32[64,512]{1,0:T(8,128)S(1)}, f32[64,512]{1,0:T(8,128)S(1)}, u32[]{:S(2)}, u32[]{:S(2)}) %collective-permute-start.4) | collective-permute-done | bytes 131104 | tf_op jit(solution)/shard_map/ppermute | solution.py:12
  31.8 2.7 %collective-permute-start.5 = (f32[64,512]{1,0:T(8,128)S(1)}, f32[64,512]{1,0:T(8,128)S(1)}, u32[]{:S(2)}, u32[]{:S(2)}) collective-permute-start(f32[64,512]{1,0:T(8,128)S(1)} %add.526), channel_id=1, source_target_pairs={{0,16},{4,20},{8,24},{12,28},{16,0},{20,4},{24,8},{28,12},{1,17},{... | collective-permute-start | bytes 393224 | tf_op jit(solution)/shard_map/ppermute | solution.py:12
  34.5 2.2 %dynamic-slice_bitcast_fusion.4 = (bf16[512,256]{1,0:T(8,128)(2,1)}, bf16[512,256]{1,0:T(8,128)(2,1)}, bf16[512,256]{1,0:T(8,128)(2,1)}, bf16[512,256]{1,0:T(8,128)(2,1)}) fusion(bf16[1,512,8704]{2,1,0:T(8,128)(2,1)} %param.5, s32[]{:T(128)S(6)} %select_n.227, s32[]{:T(128)S(6)} %select_n.226, s32[]{:T(128)S(6)} %select_n.225, s32[]{:T(128)S(6)} %select_n.224), kind=kLoop, calls=%fused_computation.79 | loop fusion | bytes 2097168 | tf_op jit(solution)/shard_map/dynamic_slice | solution.py:113
  36.7 3.0 %collective-permute-done.5 = f32[64,512]{1,0:T(8,128)S(1)} collective-permute-done((f32[64,512]{1,0:T(8,128)S(1)}, f32[64,512]{1,0:T(8,128)S(1)}, u32[]{:S(2)}, u32[]{:S(2)}) %collective-permute-start.5) | collective-permute-done | bytes 131104 | tf_op jit(solution)/shard_map/ppermute | solution.py:12
  39.8 0.7 add_bitcast_fusion.1
  40.6 1.1 %collective-permute-start.7 = (f32[64,128]{1,0:T(8,128)S(1)}, f32[64,128]{1,0:T(8,128)S(1)}, u32[]{:S(2)}, u32[]{:S(2)}) collective-permute-start(f32[64,128]{1,0:T(8,128)S(1)} %fusion.56), channel_id=1, source_target_pairs={{0,2},{1,3},{2,0},{3,1},{4,6},{5,7},{6,4},{7,5},{8,10},{9,11},{10,... | collective-permute-start | bytes 98312 | tf_op jit(solution)/shard_map/ppermute | solution.py:10
  42.1 1.2 %collective-permute-start.8 = (f32[64,128]{1,0:T(8,128)S(1)}, f32[64,128]{1,0:T(8,128)S(1)}, u32[]{:S(2)}, u32[]{:S(2)}) collective-permute-start(f32[64,128]{1,0:T(8,128)S(1)} %fusion.57), channel_id=1, source_target_pairs={{0,1},{1,0},{2,3},{3,2},{4,5},{5,4},{6,7},{7,6},{8,9},{9,8},{10,11... | collective-permute-start | bytes 98312 | tf_op jit(solution)/shard_map/ppermute | solution.py:10
  43.2 0.7 add_compare_fusion.2
  44.0 0.6 collective-permute-done.7
  44.6 0.7 collective-permute-done.6
  45.3 1.1 %select_convert_fusion.1 = bf16[64,128]{1,0:T(8,128)(2,1)S(1)} fusion(f32[64,128]{1,0:T(8,128)} %slice_bitcast_fusion.2, f32[64,128]{1,0:T(8,128)S(1)} %collective-permute-done.8, f32[64,128]{1,0:T(8,128)S(1)} %collective-permute-done.6, f32[64,128]{1,0:T(8,128)S(1)} %collective-permute-done.7, pred[128]{0:T(512)(128)(4,1)S(1)} %bitcast.142, ...), kind=kOutput, calls=%fused_computation.102 | convolution fusion | flops 8437760 | bytes 344192 | tf_op jit(solution)/shard_map/dot_general | solution.py:157
  47.3 0.6 collective-permute-done.10
  47.9 0.8 convolution_add_fusion.6
  48.7 1.0 collective-permute-start.11
  49.7 1.9 %collective-permute-start.13 = (f32[64,512]{1,0:T(8,128)}, f32[64,512]{1,0:T(8,128)}, u32[]{:S(2)}, u32[]{:S(2)}) collective-permute-start(f32[64,512]{1,0:T(8,128)} %convolution_add_fusion.6), channel_id=1, source_target_pairs={{0,6},{1,7},{2,4},{3,5},{4,2},{5,3},{6,0},{7,1},{8,14},{9,15},{10,... | collective-permute-start | bytes 393224 | tf_op jit(solution)/shard_map/ppermute | solution.py:14
  51.6 0.8 convolution_add_fusion.7
  53.0 2.6 %dynamic-slice_bitcast_fusion = (bf16[512,512]{1,0:T(8,128)(2,1)S(1)}, bf16[512,512]{1,0:T(8,128)(2,1)S(1)}, bf16[512,512]{1,0:T(8,128)(2,1)}, bf16[512,512]{1,0:T(8,128)(2,1)}) fusion(bf16[1,512,8704]{2,1,0:T(8,128)(2,1)} %param.5, s32[]{:T(128)S(6)} %select_n.240, s32[]{:T(128)S(6)} %select_n.238, s32[]{:T(128)S(6)} %select_n.237, s32[]{:T(128)S(6)} %select_n.239), kind=kLoop, calls=%fused_computation.57 | loop fusion | bytes 4194320 | tf_op jit(solution)/shard_map/dynamic_slice | solution.py:113
  55.7 1.7 %collective-permute-done.11 = f32[64,512]{1,0:T(8,128)} collective-permute-done((f32[64,512]{1,0:T(8,128)}, f32[64,512]{1,0:T(8,128)}, u32[]{:S(2)}, u32[]{:S(2)}) %collective-permute-start.11) | collective-permute-done | bytes 131104 | tf_op jit(solution)/shard_map/ppermute | solution.py:10
  57.4 1.2 %collective-permute-done.12 = f32[64,512]{1,0:T(8,128)} collective-permute-done((f32[64,512]{1,0:T(8,128)}, f32[64,512]{1,0:T(8,128)}, u32[]{:S(2)}, u32[]{:S(2)}) %collective-permute-start.12) | collective-permute-done | bytes 131104 | tf_op jit(solution)/shard_map/ppermute | solution.py:12
  58.6 1.1 %add_add_fusion.1 = f32[64,512]{1,0:T(8,128)S(1)} fusion(f32[64,512]{1,0:T(8,128)} %collective-permute-done.12, f32[64,512]{1,0:T(8,128)} %collective-permute-done.13, f32[64,512]{1,0:T(8,128)} %convolution_add_fusion.7, f32[64,512]{1,0:T(8,128)} %collective-permute-done.11), kind=kLoop, calls=%fused_computation.90 | loop fusion | flops 98304 | bytes 655360 | tf_op jit(solution)/shard_map/add | solution.py:56
  59.8 0.7 collective-permute-start.14
  60.5 1.5 %fusion.16 = f32[64,1024]{1,0:T(8,128)S(1)} fusion(bf16[64,512]{1,0:T(8,128)(2,1)S(1)} %get-tuple-element.90, bf16[512,8704]{1,0:T(8,128)(2,1)} %bitcast.138), kind=kOutput, calls=%fused_computation.30 | convolution fusion | flops 67108864 | bytes 1376256 | tf_op jit(solution)/shard_map/dot_general | solution.py:182
  62.0 2.8 %collective-permute-done.14 = f32[64,512]{1,0:T(8,128)S(1)} collective-permute-done((f32[64,512]{1,0:T(8,128)S(1)}, f32[64,512]{1,0:T(8,128)S(1)}, u32[]{:S(2)}, u32[]{:S(2)}) %collective-permute-start.14) | collective-permute-done | bytes 131104 | tf_op jit(solution)/shard_map/ppermute | solution.py:12
  64.8 1.1 %convolution_add_fusion.12 = f32[64,256]{1,0:T(8,128)S(1)} fusion(bf16[64,512]{1,0:T(8,128)(2,1)S(1)} %get-tuple-element.92, bf16[512,256]{1,0:T(8,128)(2,1)} %get-tuple-element.43, f32[64,1024]{1,0:T(8,128)S(1)} %fusion.16, s32[]{:T(128)S(6)} %select_n.229), kind=kOutput, calls=%fused_computation.28 | convolution fusion | flops 16793600 | bytes 458756 | tf_op jit(solution)/shard_map/dot_general | solution.py:157
  65.9 1.1 %collective-permute-start.16 = (f32[64,256]{1,0:T(8,128)S(1)}, f32[64,256]{1,0:T(8,128)S(1)}, u32[]{:S(2)}, u32[]{:S(2)}) collective-permute-start(f32[64,256]{1,0:T(8,128)S(1)} %convolution_add_fusion.12), channel_id=1, source_target_pairs={{0,2},{1,3},{2,0},{3,1},{4,6},{5,7},{6,4},{7,5},{8,10},{9,11},{10,... | collective-permute-start | bytes 196616 | tf_op jit(solution)/shard_map/ppermute | solution.py:10
  67.0 1.1 %convolution_add_fusion.13 = f32[64,256]{1,0:T(8,128)S(1)} fusion(bf16[64,512]{1,0:T(8,128)(2,1)S(1)} %get-tuple-element.92, bf16[512,256]{1,0:T(8,128)(2,1)} %get-tuple-element.42, f32[64,1024]{1,0:T(8,128)S(1)} %fusion.16, s32[]{:T(128)S(6)} %select_n.228), kind=kOutput, calls=%fused_computation.29 | convolution fusion | flops 16793600 | bytes 458756 | tf_op jit(solution)/shard_map/dot_general | solution.py:157
  68.2 1.1 %convolution_add_fusion.11 = f32[64,256]{1,0:T(8,128)S(1)} fusion(bf16[64,512]{1,0:T(8,128)(2,1)S(1)} %get-tuple-element.92, bf16[512,256]{1,0:T(8,128)(2,1)} %get-tuple-element.44, f32[64,1024]{1,0:T(8,128)S(1)} %fusion.16, s32[]{:T(128)S(6)} %select_n.230), kind=kOutput, calls=%fused_computation.27 | convolution fusion | flops 16793600 | bytes 458756 | tf_op jit(solution)/shard_map/dot_general | solution.py:157
  69.4 1.2 %collective-permute-start.17 = (f32[64,256]{1,0:T(8,128)S(1)}, f32[64,256]{1,0:T(8,128)S(1)}, u32[]{:S(2)}, u32[]{:S(2)}) collective-permute-start(f32[64,256]{1,0:T(8,128)S(1)} %convolution_add_fusion.11), channel_id=1, source_target_pairs={{0,1},{1,0},{2,3},{3,2},{4,5},{5,4},{6,7},{7,6},{8,9},{9,8},{10,11... | collective-permute-start | bytes 196616 | tf_op jit(solution)/shard_map/ppermute | solution.py:10
  70.5 2.1 %fusion.2 = f32[64,2048]{1,0:T(8,128)S(1)} fusion(bf16[64,512]{1,0:T(8,128)(2,1)S(1)} %get-tuple-element.90, bf16[512,8704]{1,0:T(8,128)(2,1)} %bitcast.139), kind=kOutput, calls=%fused_computation.2 | convolution fusion | flops 134217728 | bytes 2686976 | tf_op jit(solution)/shard_map/dot_general | solution.py:182
  72.6 1.1 %select_convert_fusion = bf16[64,256]{1,0:T(8,128)(2,1)S(1)} fusion(f32[64,256]{1,0:T(8,128)} %slice_bitcast_fusion.1, f32[64,256]{1,0:T(8,128)S(1)} %collective-permute-done.17, f32[64,256]{1,0:T(8,128)S(1)} %collective-permute-done.15, f32[64,256]{1,0:T(8,128)S(1)} %collective-permute-done.16, pred[256]{0:T(512)(128)(4,1)S(1)} %reduce, ...), kind=kOutput, calls=%fused_computation.96 | convolution fusion | flops 16891904 | bytes 688388 | tf_op jit(solution)/shard_map/dot_general | solution.py:157
  73.8 1.1 %fusion.61 = f32[64,512]{1,0:T(8,128)S(1)} fusion(bf16[64,256]{1,0:T(8,128)(2,1)S(1)} %select_convert_fusion, bf16[256,512]{1,0:T(8,128)(2,1)} %get-tuple-element.49), kind=kOutput, calls=%fused_computation.130 | convolution fusion | flops 16777216 | bytes 425984 | tf_op jit(solution)/shard_map/dot_general | solution.py:172
  75.0 1.1 %fusion.60 = f32[64,512]{1,0:T(8,128)S(1)} fusion(bf16[64,256]{1,0:T(8,128)(2,1)S(1)} %select_convert_fusion, bf16[256,512]{1,0:T(8,128)(2,1)} %get-tuple-element.47), kind=kOutput, calls=%fused_computation.129 | convolution fusion | flops 16777216 | bytes 425984 | tf_op jit(solution)/shard_map/dot_general | solution.py:172
  76.6 1.1 %convolution_add_fusion.8 = f32[64,512]{1,0:T(8,128)S(1)} fusion(f32[64,512]{1,0:T(8,128)S(1)} %collective-permute-done.19, bf16[64,256]{1,0:T(8,128)(2,1)S(1)} %select_convert_fusion, bf16[256,512]{1,0:T(8,128)(2,1)} %get-tuple-element.48), kind=kOutput, calls=%fused_computation.23 | convolution fusion | flops 16809984 | bytes 557056 | tf_op jit(solution)/shard_map/dot_general | solution.py:172
  77.7 1.1 %collective-permute-start.20 = (f32[64,512]{1,0:T(8,128)S(1)}, f32[64,512]{1,0:T(8,128)S(1)}, u32[]{:S(2)}, u32[]{:S(2)}) collective-permute-start(f32[64,512]{1,0:T(8,128)S(1)} %convolution_add_fusion.8), channel_id=1, source_target_pairs={{0,2},{1,3},{2,0},{3,1},{4,6},{5,7},{6,4},{7,5},{8,10},{9,11},{10,... | collective-permute-start | bytes 393224 | tf_op jit(solution)/shard_map/ppermute | solution.py:10
  78.8 1.9 %collective-permute-start.22 = (f32[64,512]{1,0:T(8,128)S(1)}, f32[64,512]{1,0:T(8,128)S(1)}, u32[]{:S(2)}, u32[]{:S(2)}) collective-permute-start(f32[64,512]{1,0:T(8,128)S(1)} %convolution_add_fusion.8), channel_id=1, source_target_pairs={{0,6},{1,7},{2,4},{3,5},{4,2},{5,3},{6,0},{7,1},{8,14},{9,15},{10,... | collective-permute-start | bytes 393224 | tf_op jit(solution)/shard_map/ppermute | solution.py:14
  80.9 0.6 collective-permute-start.21
  81.5 2.1 %fusion = f32[64,2048]{1,0:T(8,128)S(1)} fusion(bf16[64,512]{1,0:T(8,128)(2,1)S(1)} %get-tuple-element.92, bf16[512,8704]{1,0:T(8,128)(2,1)} %bitcast.140), kind=kOutput, calls=%fused_computation | convolution fusion | flops 134217728 | bytes 2686976 | tf_op jit(solution)/shard_map/dot_general | solution.py:182
  83.6 2.4 %collective-permute-done.20 = f32[64,512]{1,0:T(8,128)S(1)} collective-permute-done((f32[64,512]{1,0:T(8,128)S(1)}, f32[64,512]{1,0:T(8,128)S(1)}, u32[]{:S(2)}, u32[]{:S(2)}) %collective-permute-start.20) | collective-permute-done | bytes 131104 | tf_op jit(solution)/shard_map/ppermute | solution.py:10
  86.1 1.2 %collective-permute-done.21 = f32[64,512]{1,0:T(8,128)S(1)} collective-permute-done((f32[64,512]{1,0:T(8,128)S(1)}, f32[64,512]{1,0:T(8,128)S(1)}, u32[]{:S(2)}, u32[]{:S(2)}) %collective-permute-start.21) | collective-permute-done | bytes 131104 | tf_op jit(solution)/shard_map/ppermute | solution.py:12
  89.2 1.1 %collective-permute-start.25 = (f32[64,512]{1,0:T(8,128)S(1)}, f32[64,512]{1,0:T(8,128)S(1)}, u32[]{:S(2)}, u32[]{:S(2)}) collective-permute-start(f32[64,512]{1,0:T(8,128)S(1)} %fusion.8), channel_id=1, source_target_pairs={{0,2},{1,3},{2,0},{3,1},{4,6},{5,7},{6,4},{7,5},{8,10},{9,11},{10,... | collective-permute-start | bytes 393224 | tf_op jit(solution)/shard_map/ppermute | solution.py:10
  90.4 4.4 %collective-permute-done.25 = f32[64,512]{1,0:T(8,128)S(1)} collective-permute-done((f32[64,512]{1,0:T(8,128)S(1)}, f32[64,512]{1,0:T(8,128)S(1)}, u32[]{:S(2)}, u32[]{:S(2)}) %collective-permute-start.25) | collective-permute-done | bytes 131104 | tf_op jit(solution)/shard_map/ppermute | solution.py:10
  96.1 0.6 collective-permute-done.27
  96.8 1.1 %collective-permute-start.28 = (f32[64,512]{1,0:T(8,128)S(1)}, f32[64,512]{1,0:T(8,128)S(1)}, u32[]{:S(2)}, u32[]{:S(2)}) collective-permute-start(f32[64,512]{1,0:T(8,128)S(1)} %convolution_add_fusion), channel_id=1, source_target_pairs={{0,2},{1,3},{2,0},{3,1},{4,6},{5,7},{6,4},{7,5},{8,10},{9,11},{10,... | collective-permute-start | bytes 393224 | tf_op jit(solution)/shard_map/ppermute | solution.py:10
  97.9 4.5 %collective-permute-done.28 = f32[64,512]{1,0:T(8,128)S(1)} collective-permute-done((f32[64,512]{1,0:T(8,128)S(1)}, f32[64,512]{1,0:T(8,128)S(1)}, u32[]{:S(2)}, u32[]{:S(2)}) %collective-permute-start.28) | collective-permute-done | bytes 131104 | tf_op jit(solution)/shard_map/ppermute | solution.py:10
  102.7 0.8 maximum_bitcast_fusion
  (63 shorter events, 7.3 us)
Async XLA Ops:
  4.2 8.6 %collective-permute-start = (f32[64,1024]{1,0:T(8,128)}, f32[64,1024]{1,0:T(8,128)}, u32[]{:S(2)}, u32[]{:S(2)}) collective-permute-start(f32[64,1024]{1,0:T(8,128)} %pad_maximum_fusion), channel_id=1, source_target_pairs={{0,1},{1,0},{2,3},{3,2},{4,5},{5,4},{6,7},{7,6},{8,9},{9,8},{10,11... | collective-permute-start | bytes 786440 | tf_op jit(solution)/shard_map/ppermute | solution.py:10
  14.5 9.3 %collective-permute-start.1 = (f32[64,512]{1,0:T(8,128)}, f32[64,512]{1,0:T(8,128)S(1)}, u32[]{:S(2)}, u32[]{:S(2)}) collective-permute-start(f32[64,512]{1,0:T(8,128)} %get-tuple-element.85), channel_id=1, source_target_pairs={{0,2},{1,3},{2,0},{3,1},{4,6},{5,7},{6,4},{7,5},{8,10},{9,11},{10,... | collective-permute-start | bytes 393224 | tf_op jit(solution)/shard_map/ppermute | solution.py:10
  17.0 8.6 %collective-permute-start.3 = (f32[64,512]{1,0:T(8,128)}, f32[64,512]{1,0:T(8,128)}, u32[]{:S(2)}, u32[]{:S(2)}) collective-permute-start(f32[64,512]{1,0:T(8,128)} %get-tuple-element.85), channel_id=1, source_target_pairs={{0,6},{1,7},{2,4},{3,5},{4,2},{5,3},{6,0},{7,1},{8,14},{9,15},{10,... | collective-permute-start | bytes 393224 | tf_op jit(solution)/shard_map/ppermute | solution.py:14
  18.4 7.1 %collective-permute-start.2 = (f32[64,512]{1,0:T(8,128)S(1)}, f32[64,512]{1,0:T(8,128)}, u32[]{:S(2)}, u32[]{:S(2)}) collective-permute-start(f32[64,512]{1,0:T(8,128)S(1)} %get-tuple-element.86), channel_id=1, source_target_pairs={{0,4},{4,0},{8,12},{12,8},{16,20},{20,16},{24,28},{28,24},{1,5},{5... | collective-permute-start | bytes 393224 | tf_op jit(solution)/shard_map/ppermute | solution.py:12
  23.8 1.7 %copy-start.4 = (f32[64,512]{1,0:T(8,128)}, f32[64,512]{1,0:T(8,128)S(1)}, u32[]{:S(2)}) copy-start(f32[64,512]{1,0:T(8,128)S(1)} %collective-permute-done.1) | copy-start | bytes 393220
  26.7 5.1 %collective-permute-start.4 = (f32[64,512]{1,0:T(8,128)S(1)}, f32[64,512]{1,0:T(8,128)S(1)}, u32[]{:S(2)}, u32[]{:S(2)}) collective-permute-start(f32[64,512]{1,0:T(8,128)S(1)} %add_add_fusion.2), channel_id=1, source_target_pairs={{0,8},{4,12},{8,0},{12,4},{16,24},{20,28},{24,16},{28,20},{1,9},{5... | collective-permute-start | bytes 393224 | tf_op jit(solution)/shard_map/ppermute | solution.py:12
  31.8 8.0 %collective-permute-start.5 = (f32[64,512]{1,0:T(8,128)S(1)}, f32[64,512]{1,0:T(8,128)S(1)}, u32[]{:S(2)}, u32[]{:S(2)}) collective-permute-start(f32[64,512]{1,0:T(8,128)S(1)} %add.526), channel_id=1, source_target_pairs={{0,16},{4,20},{8,24},{12,28},{16,0},{20,4},{24,8},{28,12},{1,17},{... | collective-permute-start | bytes 393224 | tf_op jit(solution)/shard_map/ppermute | solution.py:12
  40.6 4.0 %collective-permute-start.7 = (f32[64,128]{1,0:T(8,128)S(1)}, f32[64,128]{1,0:T(8,128)S(1)}, u32[]{:S(2)}, u32[]{:S(2)}) collective-permute-start(f32[64,128]{1,0:T(8,128)S(1)} %fusion.56), channel_id=1, source_target_pairs={{0,2},{1,3},{2,0},{3,1},{4,6},{5,7},{6,4},{7,5},{8,10},{9,11},{10,... | collective-permute-start | bytes 98312 | tf_op jit(solution)/shard_map/ppermute | solution.py:10
  41.8 3.4 %collective-permute-start.6 = (f32[64,128]{1,0:T(8,128)S(1)}, f32[64,128]{1,0:T(8,128)S(1)}, u32[]{:S(2)}, u32[]{:S(2)}) collective-permute-start(f32[64,128]{1,0:T(8,128)S(1)} %fusion.55), channel_id=1, source_target_pairs={{0,3},{1,2},{2,1},{3,0},{4,7},{5,6},{6,5},{7,4},{8,11},{9,10},{10,... | collective-permute-start | bytes 98312 | tf_op jit(solution)/shard_map/ppermute | solution.py:10
  42.1 3.2 %collective-permute-start.8 = (f32[64,128]{1,0:T(8,128)S(1)}, f32[64,128]{1,0:T(8,128)S(1)}, u32[]{:S(2)}, u32[]{:S(2)}) collective-permute-start(f32[64,128]{1,0:T(8,128)S(1)} %fusion.57), channel_id=1, source_target_pairs={{0,1},{1,0},{2,3},{3,2},{4,5},{5,4},{6,7},{7,6},{8,9},{9,8},{10,11... | collective-permute-start | bytes 98312 | tf_op jit(solution)/shard_map/ppermute | solution.py:10
  46.5 1.4 %collective-permute-start.10 = (f32[64,512]{1,0:T(8,128)S(1)}, f32[64,512]{1,0:T(8,128)S(1)}, u32[]{:S(2)}, u32[]{:S(2)}) collective-permute-start(f32[64,512]{1,0:T(8,128)S(1)} %fusion.59), channel_id=1, source_target_pairs={{0,1},{1,0},{2,3},{3,2},{4,5},{5,4},{6,7},{7,6},{8,9},{9,8},{10,11... | collective-permute-start | bytes 393224 | tf_op jit(solution)/shard_map/ppermute | solution.py:10
  46.7 4.9 %collective-permute-start.9 = (f32[64,512]{1,0:T(8,128)S(1)}, f32[64,512]{1,0:T(8,128)S(1)}, u32[]{:S(2)}, u32[]{:S(2)}) collective-permute-start(f32[64,512]{1,0:T(8,128)S(1)} %fusion.58), channel_id=1, source_target_pairs={{0,1},{1,0},{2,3},{3,2},{4,5},{5,4},{6,7},{7,6},{8,9},{9,8},{10,11... | collective-permute-start | bytes 393224 | tf_op jit(solution)/shard_map/ppermute | solution.py:10
  48.7 8.7 %collective-permute-start.11 = (f32[64,512]{1,0:T(8,128)}, f32[64,512]{1,0:T(8,128)}, u32[]{:S(2)}, u32[]{:S(2)}) collective-permute-start(f32[64,512]{1,0:T(8,128)} %convolution_add_fusion.6), channel_id=1, source_target_pairs={{0,2},{1,3},{2,0},{3,1},{4,6},{5,7},{6,4},{7,5},{8,10},{9,11},{10,... | collective-permute-start | bytes 393224 | tf_op jit(solution)/shard_map/ppermute | solution.py:10
  49.7 7.6 %collective-permute-start.13 = (f32[64,512]{1,0:T(8,128)}, f32[64,512]{1,0:T(8,128)}, u32[]{:S(2)}, u32[]{:S(2)}) collective-permute-start(f32[64,512]{1,0:T(8,128)} %convolution_add_fusion.6), channel_id=1, source_target_pairs={{0,6},{1,7},{2,4},{3,5},{4,2},{5,3},{6,0},{7,1},{8,14},{9,15},{10,... | collective-permute-start | bytes 393224 | tf_op jit(solution)/shard_map/ppermute | solution.py:14
  52.5 6.2 %collective-permute-start.12 = (f32[64,512]{1,0:T(8,128)}, f32[64,512]{1,0:T(8,128)}, u32[]{:S(2)}, u32[]{:S(2)}) collective-permute-start(f32[64,512]{1,0:T(8,128)} %convolution_add_fusion.7), channel_id=1, source_target_pairs={{0,4},{4,0},{8,12},{12,8},{16,20},{20,16},{24,28},{28,24},{1,5},{5... | collective-permute-start | bytes 393224 | tf_op jit(solution)/shard_map/ppermute | solution.py:12
  55.7 33.3 %copy-start.1 = (bf16[512,512]{1,0:T(8,128)(2,1)S(1)}, bf16[512,512]{1,0:T(8,128)(2,1)}, u32[]{:S(2)}) copy-start(bf16[512,512]{1,0:T(8,128)(2,1)} %get-tuple-element.53) | copy-start | bytes 1572868
  55.7 34.6 %copy-start.3 = (f32[1,64,960]{2,1,0:T(8,128)S(1)}, f32[1,64,960]{2,1,0:T(8,128)}, u32[]{:S(2)}) copy-start(f32[1,64,960]{2,1,0:T(8,128)} %param.4) | copy-start | bytes 737284
  55.7 39.1 %copy-start = (bf16[512,512]{1,0:T(8,128)(2,1)S(1)}, bf16[512,512]{1,0:T(8,128)(2,1)}, u32[]{:S(2)}) copy-start(bf16[512,512]{1,0:T(8,128)(2,1)} %get-tuple-element.51) | copy-start | bytes 1572868
  59.8 5.0 %collective-permute-start.14 = (f32[64,512]{1,0:T(8,128)S(1)}, f32[64,512]{1,0:T(8,128)S(1)}, u32[]{:S(2)}, u32[]{:S(2)}) collective-permute-start(f32[64,512]{1,0:T(8,128)S(1)} %add_add_fusion.1), channel_id=1, source_target_pairs={{0,8},{4,12},{8,0},{12,4},{16,24},{20,28},{24,16},{28,20},{1,9},{5... | collective-permute-start | bytes 393224 | tf_op jit(solution)/shard_map/ppermute | solution.py:12
  65.9 36.7 %copy-start.2 = (f32[1,64,512]{2,1,0:T(8,128)S(1)}, f32[1,64,512]{2,1,0:T(8,128)}, u32[]{:S(2)}) copy-start(f32[1,64,512]{2,1,0:T(8,128)} %get-tuple-element.89) | copy-start | bytes 393220
  65.9 6.6 %collective-permute-start.16 = (f32[64,256]{1,0:T(8,128)S(1)}, f32[64,256]{1,0:T(8,128)S(1)}, u32[]{:S(2)}, u32[]{:S(2)}) collective-permute-start(f32[64,256]{1,0:T(8,128)S(1)} %convolution_add_fusion.12), channel_id=1, source_target_pairs={{0,2},{1,3},{2,0},{3,1},{4,6},{5,7},{6,4},{7,5},{8,10},{9,11},{10,... | collective-permute-start | bytes 196616 | tf_op jit(solution)/shard_map/ppermute | solution.py:10
  68.2 4.4 %collective-permute-start.15 = (f32[64,256]{1,0:T(8,128)S(1)}, f32[64,256]{1,0:T(8,128)S(1)}, u32[]{:S(2)}, u32[]{:S(2)}) collective-permute-start(f32[64,256]{1,0:T(8,128)S(1)} %convolution_add_fusion.13), channel_id=1, source_target_pairs={{0,3},{1,2},{2,1},{3,0},{4,7},{5,6},{6,5},{7,4},{8,11},{9,10},{10,... | collective-permute-start | bytes 196616 | tf_op jit(solution)/shard_map/ppermute | solution.py:10
  69.4 3.3 %collective-permute-start.17 = (f32[64,256]{1,0:T(8,128)S(1)}, f32[64,256]{1,0:T(8,128)S(1)}, u32[]{:S(2)}, u32[]{:S(2)}) collective-permute-start(f32[64,256]{1,0:T(8,128)S(1)} %convolution_add_fusion.11), channel_id=1, source_target_pairs={{0,1},{1,0},{2,3},{3,2},{4,5},{5,4},{6,7},{7,6},{8,9},{9,8},{10,11... | collective-permute-start | bytes 196616 | tf_op jit(solution)/shard_map/ppermute | solution.py:10
  74.9 1.8 %collective-permute-start.19 = (f32[64,512]{1,0:T(8,128)S(1)}, f32[64,512]{1,0:T(8,128)S(1)}, u32[]{:S(2)}, u32[]{:S(2)}) collective-permute-start(f32[64,512]{1,0:T(8,128)S(1)} %fusion.61), channel_id=1, source_target_pairs={{0,1},{1,0},{2,3},{3,2},{4,5},{5,4},{6,7},{7,6},{8,9},{9,8},{10,11... | collective-permute-start | bytes 393224 | tf_op jit(solution)/shard_map/ppermute | solution.py:10
  76.1 4.7 %collective-permute-start.18 = (f32[64,512]{1,0:T(8,128)S(1)}, f32[64,512]{1,0:T(8,128)S(1)}, u32[]{:S(2)}, u32[]{:S(2)}) collective-permute-start(f32[64,512]{1,0:T(8,128)S(1)} %fusion.60), channel_id=1, source_target_pairs={{0,1},{1,0},{2,3},{3,2},{4,5},{5,4},{6,7},{7,6},{8,9},{9,8},{10,11... | collective-permute-start | bytes 393224 | tf_op jit(solution)/shard_map/ppermute | solution.py:10
  77.7 8.2 %collective-permute-start.20 = (f32[64,512]{1,0:T(8,128)S(1)}, f32[64,512]{1,0:T(8,128)S(1)}, u32[]{:S(2)}, u32[]{:S(2)}) collective-permute-start(f32[64,512]{1,0:T(8,128)S(1)} %convolution_add_fusion.8), channel_id=1, source_target_pairs={{0,2},{1,3},{2,0},{3,1},{4,6},{5,7},{6,4},{7,5},{8,10},{9,11},{10,... | collective-permute-start | bytes 393224 | tf_op jit(solution)/shard_map/ppermute | solution.py:10
  78.8 7.3 %collective-permute-start.22 = (f32[64,512]{1,0:T(8,128)S(1)}, f32[64,512]{1,0:T(8,128)S(1)}, u32[]{:S(2)}, u32[]{:S(2)}) collective-permute-start(f32[64,512]{1,0:T(8,128)S(1)} %convolution_add_fusion.8), channel_id=1, source_target_pairs={{0,6},{1,7},{2,4},{3,5},{4,2},{5,3},{6,0},{7,1},{8,14},{9,15},{10,... | collective-permute-start | bytes 393224 | tf_op jit(solution)/shard_map/ppermute | solution.py:14
  80.9 6.4 %collective-permute-start.21 = (f32[64,512]{1,0:T(8,128)S(1)}, f32[64,512]{1,0:T(8,128)S(1)}, u32[]{:S(2)}, u32[]{:S(2)}) collective-permute-start(f32[64,512]{1,0:T(8,128)S(1)} %convolution_add_fusion.9), channel_id=1, source_target_pairs={{0,4},{4,0},{8,12},{12,8},{16,20},{20,16},{24,28},{28,24},{1,5},{5... | collective-permute-start | bytes 393224 | tf_op jit(solution)/shard_map/ppermute | solution.py:12
  87.5 1.4 %collective-permute-start.24 = (f32[64,512]{1,0:T(8,128)S(1)}, f32[64,512]{1,0:T(8,128)S(1)}, u32[]{:S(2)}, u32[]{:S(2)}) collective-permute-start(f32[64,512]{1,0:T(8,128)S(1)} %fusion.6), channel_id=1, source_target_pairs={{0,1},{1,0},{2,3},{3,2},{4,5},{5,4},{6,7},{7,6},{8,9},{9,8},{10,11... | collective-permute-start | bytes 393224 | tf_op jit(solution)/shard_map/ppermute | solution.py:10
  87.8 2.5 %collective-permute-start.23 = (f32[64,512]{1,0:T(8,128)S(1)}, f32[64,512]{1,0:T(8,128)S(1)}, u32[]{:S(2)}, u32[]{:S(2)}) collective-permute-start(f32[64,512]{1,0:T(8,128)S(1)} %fusion.9), channel_id=1, source_target_pairs={{0,1},{1,0},{2,3},{3,2},{4,5},{5,4},{6,7},{7,6},{8,9},{9,8},{10,11... | collective-permute-start | bytes 393224 | tf_op jit(solution)/shard_map/ppermute | solution.py:10
  89.2 5.6 %collective-permute-start.25 = (f32[64,512]{1,0:T(8,128)S(1)}, f32[64,512]{1,0:T(8,128)S(1)}, u32[]{:S(2)}, u32[]{:S(2)}) collective-permute-start(f32[64,512]{1,0:T(8,128)S(1)} %fusion.8), channel_id=1, source_target_pairs={{0,2},{1,3},{2,0},{3,1},{4,6},{5,7},{6,4},{7,5},{8,10},{9,11},{10,... | collective-permute-start | bytes 393224 | tf_op jit(solution)/shard_map/ppermute | solution.py:10
  95.2 1.4 %collective-permute-start.27 = (f32[64,512]{1,0:T(8,128)S(1)}, f32[64,512]{1,0:T(8,128)S(1)}, u32[]{:S(2)}, u32[]{:S(2)}) collective-permute-start(f32[64,512]{1,0:T(8,128)S(1)} %fusion.63), channel_id=1, source_target_pairs={{0,1},{1,0},{2,3},{3,2},{4,5},{5,4},{6,7},{7,6},{8,9},{9,8},{10,11... | collective-permute-start | bytes 393224 | tf_op jit(solution)/shard_map/ppermute | solution.py:10
  95.5 2.4 %collective-permute-start.26 = (f32[64,512]{1,0:T(8,128)S(1)}, f32[64,512]{1,0:T(8,128)S(1)}, u32[]{:S(2)}, u32[]{:S(2)}) collective-permute-start(f32[64,512]{1,0:T(8,128)S(1)} %fusion.62), channel_id=1, source_target_pairs={{0,1},{1,0},{2,3},{3,2},{4,5},{5,4},{6,7},{7,6},{8,9},{9,8},{10,11... | collective-permute-start | bytes 393224 | tf_op jit(solution)/shard_map/ppermute | solution.py:10
  96.8 5.6 %collective-permute-start.28 = (f32[64,512]{1,0:T(8,128)S(1)}, f32[64,512]{1,0:T(8,128)S(1)}, u32[]{:S(2)}, u32[]{:S(2)}) collective-permute-start(f32[64,512]{1,0:T(8,128)S(1)} %convolution_add_fusion), channel_id=1, source_target_pairs={{0,2},{1,3},{2,0},{3,1},{4,6},{5,7},{6,4},{7,5},{8,10},{9,11},{10,... | collective-permute-start | bytes 393224 | tf_op jit(solution)/shard_map/ppermute | solution.py:10

commit v4 on v3

--- a/solution.py
+++ b/solution.py
@@ -21,6 +21,26 @@
     return sorted(range(count), key=lambda m: [-(m >> b & 1) for b in range(bits)])
 
 
+def halves_reduced(far, near, leaf_bits, step):
+    side = lax.axis_index("leaf") & 1
+    rows = near.shape[0] // 2
+
+    def half(block, flip):
+        return lax.dynamic_slice(block, ((side ^ flip) * rows, 0), (rows, block.shape[1]))
+
+    from_panel = exchanged(half(far, 0), 0, step)
+    from_leaf = exchanged(half(near, 1), 1, 0)
+    from_both = exchanged(half(far, 1), 1, step)
+    total = (half(near, 0) + from_panel) + (from_leaf + from_both)
+    for leaf_bit in range(leaf_bits - 1, 1, -1):
+        total = total + exchanged(total, 1 << leaf_bit, 0)
+    mine = total + exchanged(total, 2, 0)
+    other = exchanged(total, 1, 0) + exchanged(total, 3, 0)
+    low = jnp.where(side == 0, mine, other)
+    high = jnp.where(side == 0, other, mine)
+    return jnp.concatenate([low, high], axis=0)
+
+
 def reduced(chunk_of, leaf_bits, direct=False, joined=False):
     count = lax.axis_size("panel")
     bits = count.bit_length() - 1
@@ -28,7 +48,7 @@
     arrived = {}
     if direct:
         total = None
-        for m in range(count - 1, -1, -1):
+        for m in direct_order(count):
             chunk = chunk_of(m)
             got = exchanged(chunk, 0, m) if m else chunk
             total = got if total is None else total + got
@@ -50,17 +70,21 @@
         step = 1 << bit
         if bit == bits - 1 and leaf_bits > 0:
             far, near = held[step], held[0]
+            if leaf_bits > 1:
+                return halves_reduced(far, near, leaf_bits, step)
             from_panel = exchanged(far, 0, step)
             from_leaf = exchanged(near, 1, 0)
             from_both = exchanged(far, 1, step)
-            total = (near + from_panel) + (from_leaf + from_both)
-            for leaf_bit in range(1, leaf_bits):
-                total = total + exchanged(total, 1 << leaf_bit, 0)
-            return total
+            return (near + from_panel) + (from_leaf + from_both)
         for m in sorted(held, reverse=True):
             if m & step:
                 arrived[m ^ step] = exchanged(held[m], 0, step)
     return held[0]
+
+
+def direct_order(count):
+    half = count // 2
+    return [m for m in range(half, count)] + [m for m in range(half - 1, -1, -1)]
 
 
 def exchanged_in_one(panel_count, share):
@@ -116,11 +140,20 @@
         width = whole.shape[1] // panel_count
         return lax.dynamic_slice(whole, (0, (panel_pos ^ m) * width), (whole.shape[0], width))
 
-    def alive(height):
-        group_size, _, _, _, _ = sizes(height)
-        front_id = (1 << height) - 1 + leaf_pos // group_size
-        live_size = lax.dynamic_slice(front_sizes, (front_id,), (1,)) if height else front_sizes[:1]
-        return (own_rows(height) < live_size)[None, :]
+    def alive_later():
+        total = sum(sizes(height)[2] for height in range(1, levels))
+        place = jnp.arange(total)
+        rows = live = jnp.zeros((total,), jnp.int32)
+        start = 0
+        for height in range(1, levels):
+            group_size, col_width, share, _, _ = sizes(height)
+            front_id = (1 << height) - 1 + leaf_pos // group_size
+            first = (leaf_pos % group_size) * col_width + panel_pos * share
+            here = place >= start
+            rows = jnp.where(here, place - start + first, rows)
+            live = jnp.where(here, lax.dynamic_slice(late_sizes, (front_id,), (1,)), live)
+            start += share
+        return (rows < live)[None, :]
 
     def right_of(height):
         _, _, share, _, row_start = sizes(height)
@@ -129,11 +162,17 @@
     def in_one(height):
         return exchanged_in_one(panel_count, sizes(height)[2])
 
+    late_sizes = lax.optimization_barrier(front_sizes)
     factors = {}
     couplings = {}
     lives = {}
     rights = {}
-    lives = lax.optimization_barrier({h: alive(h) for h in range(1, levels)})
+    ends = lax.optimization_barrier(alive_later())
+    start = 0
+    for height in range(1, levels):
+        share = sizes(height)[2]
+        lives[height] = ends[:, start : start + share]
+        start += share
     for height in range(1, levels):
         rights[height] = lax.optimization_barrier(right_of(height))
     for height in range(1, levels):
@@ -149,7 +188,7 @@
         rows = own_rows(height)
         if height == 0:
             resid = right_of(0)
-            live = alive(0)
+            live = (own_rows(0) < front_sizes[:1])[None, :]
         else:
             live = lives[height]
 
@@ -157,9 +196,7 @@
                 term = jnp.dot(
                     solved[-1], couplings[height][m], preferred_element_type=jnp.float32
                 )
-                for early in base.get(height, ()):
-                    term = term + part(early, m)
-                return term
+                return term + part(base[height], m) if height in base else term
 
             resid = rights[height] - reduced(update, 0, direct=in_one(height))
         resid_low = jnp.where(live, resid, 0.0).astype(jnp.bfloat16)
@@ -182,7 +219,7 @@
             term = jnp.dot(
                 solved[-1], tiles[:, low : low + width], preferred_element_type=jnp.float32
             )
-            base.setdefault(later, []).append(term)
+            base[later] = lax.optimization_barrier(base[later] + term if later in base else term)
     return jnp.stack(results, axis=0)[None]
 
 

time: 104 us -> 107 us (1.029)
  starting transfers between devices: 26.2 us -> 30.9 us
  waiting for transfers between devices: 30.2 us -> 25.8 us
  matrix products: 20 us -> 24.3 us
  other arithmetic: 15.3 us -> 12.5 us
    ppermute x6 -> x10, starting transfers between devices: 6.5 us -> 13.1 us  [exchanged(): lax.ppermute(block, 'leaf', [(i, i ^ leaf_flip) for i in range(leaf_count)])]
    ppermute x6 -> x10, waiting for transfers between devices: 12 us -> 7.01 us  [exchanged(): lax.ppermute(block, 'leaf', [(i, i ^ leaf_flip) for i in range(leaf_count)])]
    dot_general x12, matrix products: 6.87 us -> 11.6 us  [update(): jnp.dot(solved[-1], couplings[height][m], preferred_element_type=jnp.floa...]
    ppermute x3, waiting for transfers between devices: 0.14 us -> 4.58 us  [exchanged(): lax.ppermute(block, ('leaf', 'panel'), [(i, i ^ flip) for i in range(leaf...]
    ppermute x20, waiting for transfers between devices: 18.1 us -> 14.3 us  [exchanged(): lax.ppermute(block, 'panel', [(i, i ^ panel_flip) for i in range(panel_co...]
    ppermute x3, starting transfers between devices: 5.22 us -> 2.75 us  [exchanged(): lax.ppermute(block, ('leaf', 'panel'), [(i, i ^ flip) for i in range(leaf...]
    add x1, other arithmetic: 1.66 us -> 0.04 us  [reduced(): held = {m: held[m] + arrived[m] for m in arrived}]
    add x3, other arithmetic: 2.22 us -> 0.89 us  [the longest x1 0.85 us: halves_reduced(): total = total + exchanged(total, 1 << leaf_bit, 0)]
  transfers between devices with their start and end apart: 29 -> 33, of which waited for: 17 -> 17; matrix products, arithmetic and copies ran while one was open for 30% -> 34% of each run, Pallas kernels for 0% -> 0%
where the time goes in v4:
time: 107 us; the launch traced here: 106 us
  starting transfers between devices  30.9 us (29%)
  waiting for transfers between devices  25.8 us (24%)
  matrix products  24.3 us (23%)
  other arithmetic  12.5 us (12%)
  local copies, waits for them, and re-layouts  12.2 us (11%)
    ppermute x20, starting transfers between devices, exchanged(): lax.ppermute(block, 'panel', [(i, i ^ panel_flip) for i in range(panel_co...  15 us
    ppermute x20, waiting for transfers between devices, exchanged(): lax.ppermute(block, 'panel', [(i, i ^ panel_flip) for i in range(panel_co...  14.3 us
    ppermute x10, starting transfers between devices, exchanged(): lax.ppermute(block, 'leaf', [(i, i ^ leaf_flip) for i in range(leaf_count)])  13.1 us
    dot_general x12, matrix products, update(): jnp.dot(solved[-1], couplings[height][m], preferred_element_type=jnp.floa...  11.6 us
    convert_element_type x3, other arithmetic, masked(): return (kept + one).astype(jnp.bfloat16)  7.17 us
    ppermute x10, waiting for transfers between devices, exchanged(): lax.ppermute(block, 'leaf', [(i, i ^ leaf_flip) for i in range(leaf_count)])  7.01 us
    dynamic_slice x3, local copies, waits for them, and re-layouts, coupling(): return lax.dynamic_slice(tiles, (0, low), (tiles.shape[0], share))  6.8 us
    dot_general x12, matrix products, per_device(): jnp.dot(resid_low, factors[height][m], preferred_element_type=jnp.float32)  5.68 us
  transfers between devices with their start and end apart: 33, of which 17 were waited for; matrix products, arithmetic and copies ran while one was open for 34% of the time, Pallas kernels for 0%

profile of v4, /device:TPU:0, one launch (start us, length us, event | category | flops | bytes accessed | tf_op | source)
XLA Modules:
  0.0 106.2 jit_solution(616243579841603756)
XLA Ops:
  0.0 0.7 broadcast_compare_fusion
  0.7 1.3 %fusion.30 = f32[64,2048]{1,0:T(8,128)S(1)} fusion(bf16[1,960,2048]{2,1,0:T(8,128)(2,1)} %param.6, s32[64]{0:T(128)S(1)} %iota_add_fusion.6, f32[1,64,960]{2,1,0:T(8,128)} %param.4, pred[64]{0:T(512)(128)(4,1)S(1)} %broadcast_compare_fusion), kind=kOutput, calls=%fused_computation.61 | convolution fusion | flops 17698816 | bytes 803136 | tf_op jit(solution)/shard_map/dot_general | solution.py:205
  2.6 1.5 %slice_bitcast_fusion.2 = f32[64,128]{1,0:T(8,128)} fusion(f32[1,64,960]{2,1,0:T(8,128)} %param.4), kind=kLoop, calls=%fused_computation.101 | loop fusion | bytes 65536 | tf_op jit(solution)/shard_map/squeeze | solution.py:160
  4.2 1.6 %slice_bitcast_fusion.1 = f32[64,256]{1,0:T(8,128)} fusion(f32[1,64,960]{2,1,0:T(8,128)} %param.4), kind=kLoop, calls=%fused_computation.97 | loop fusion | bytes 131072 | tf_op jit(solution)/shard_map/squeeze | solution.py:160
  5.8 2.5 %fusion.14 = (bf16[512,512]{1,0:T(8,128)(2,1)S(1)}, bf16[512,512]{1,0:T(8,128)(2,1)S(1)}, bf16[512,512]{1,0:T(8,128)(2,1)S(1)}, bf16[512,512]{1,0:T(8,128)(2,1)S(1)}) fusion(bf16[1,960,2048]{2,1,0:T(8,128)(2,1)} %param.6, s32[]{:T(128)S(6)} %select_n.279, s32[512]{0:T(512)S(1)} %get-tuple-element.94, s32[512]{0:T(512)S(1)} %get-tuple-element.97, ...), kind=kLoop, calls=%fused_computation.30 | loop fusion | flops 7340032 | bytes 4204560 | tf_op jit(solution)/shard_map/convert_element_type | solution.py:126
  8.3 2.2 %fusion.33 = (bf16[128,512]{1,0:T(8,128)(2,1)}, bf16[128,512]{1,0:T(8,128)(2,1)}, bf16[128,512]{1,0:T(8,128)(2,1)}, bf16[128,512]{1,0:T(8,128)(2,1)}) fusion(bf16[1,960,2048]{2,1,0:T(8,128)(2,1)} %param.6, s32[]{:T(128)S(6)} %select_n.279, s32[512]{0:T(512)S(1)} %get-tuple-element.94, s32[128]{0:T(128)S(1)} %iota_add_fusion.5, s32[]{:T(128)S(6)} %select_n.282, ...), kind=kLoop, calls=%fused_computation.65 | loop fusion | flops 1835008 | bytes 1057296 | tf_op jit(solution)/shard_map/convert_element_type | solution.py:126
  10.4 1.4 %fusion.54 = (s32[1]{0:T(128)}, s32[1]{0:T(128)}, s32[1]{0:T(128)}) fusion(s32[15]{0:T(128)} %param.7, s32[]{:T(128)S(6)} %select_n.290, s32[]{:T(128)S(6)} %select_n.294, s32[]{:T(128)S(6)} %select_n.292), kind=kLoop, calls=%fused_computation.136 | loop fusion | bytes 36 | tf_op jit(solution)/shard_map/dynamic_slice | solution.py:154
  11.8 1.9 %fusion.51 = pred[1,896]{1,0:T(4,128)(4,1)S(1)} fusion(s32[]{:T(128)} %bitcast.6, s32[]{:T(128)} %bitcast.5, s32[]{:T(128)} %bitcast.4, s32[]{:T(128)S(6)} %add.559, s32[]{:T(128)S(6)} %add.555, s32[]{:T(128)S(6)} %mul.38), kind=kLoop, calls=%fused_computation.124 | loop fusion | flops 10752 | bytes 920 | tf_op jit(solution)/shard_map/lt | solution.py:156
  13.8 2.5 %fusion.22 = (bf16[256,512]{1,0:T(8,128)(2,1)}, bf16[256,512]{1,0:T(8,128)(2,1)}, bf16[256,512]{1,0:T(8,128)(2,1)}, bf16[256,512]{1,0:T(8,128)(2,1)S(1)}) fusion(bf16[1,960,2048]{2,1,0:T(8,128)(2,1)} %param.6, s32[]{:T(128)S(6)} %select_n.279, s32[512]{0:T(512)S(1)} %get-tuple-element.94, s32[256]{0:T(256)S(1)} %iota_add_fusion.4, s32[]{:T(128)S(6)} %select_n.282, ...), kind=kLoop, calls=%fused_computation.43 | loop fusion | flops 3670016 | bytes 2106384 | tf_op jit(solution)/shard_map/convert_element_type | solution.py:126
  16.3 2.6 %collective-permute-start.1 = (f32[32,512]{1,0:T(8,128)S(1)}, f32[32,512]{1,0:T(8,128)S(1)}, u32[]{:S(2)}, u32[]{:S(2)}) collective-permute-start(f32[32,512]{1,0:T(8,128)S(1)} %get-tuple-element.89), channel_id=1, source_target_pairs={{0,2},{1,3},{2,0},{3,1},{4,6},{5,7},{6,4},{7,5},{8,10},{9,11},{10,... | collective-permute-start | bytes 196616 | tf_op jit(solution)/shard_map/ppermute | solution.py:10
  18.9 1.4 %collective-permute-start.3 = (f32[32,512]{1,0:T(8,128)S(1)}, f32[32,512]{1,0:T(8,128)S(1)}, u32[]{:S(2)}, u32[]{:S(2)}) collective-permute-start(f32[32,512]{1,0:T(8,128)S(1)} %get-tuple-element.90), channel_id=1, source_target_pairs={{0,6},{1,7},{2,4},{3,5},{4,2},{5,3},{6,0},{7,1},{8,14},{9,15},{10,... | collective-permute-start | bytes 196616 | tf_op jit(solution)/shard_map/ppermute | solution.py:14
  20.5 1.8 %collective-permute-done.1 = f32[32,512]{1,0:T(8,128)S(1)} collective-permute-done((f32[32,512]{1,0:T(8,128)S(1)}, f32[32,512]{1,0:T(8,128)S(1)}, u32[]{:S(2)}, u32[]{:S(2)}) %collective-permute-start.1) | collective-permute-done | bytes 65568 | tf_op jit(solution)/shard_map/ppermute | solution.py:10
  22.4 2.0 %collective-permute-done.3 = f32[32,512]{1,0:T(8,128)S(1)} collective-permute-done((f32[32,512]{1,0:T(8,128)S(1)}, f32[32,512]{1,0:T(8,128)S(1)}, u32[]{:S(2)}, u32[]{:S(2)}) %collective-permute-start.3) | collective-permute-done | bytes 65568 | tf_op jit(solution)/shard_map/ppermute | solution.py:14
  24.7 2.7 %collective-permute-start.4 = (f32[32,512]{1,0:T(8,128)S(1)}, f32[32,512]{1,0:T(8,128)}, u32[]{:S(2)}, u32[]{:S(2)}) collective-permute-start(f32[32,512]{1,0:T(8,128)S(1)} %add_add_fusion.2), channel_id=1, source_target_pairs={{0,16},{4,20},{8,24},{12,28},{16,0},{20,4},{24,8},{28,12},{1,17},{... | collective-permute-start | bytes 196616 | tf_op jit(solution)/shard_map/ppermute | solution.py:12
  27.3 2.7 %dynamic-slice_bitcast_fusion = (bf16[512,512]{1,0:T(8,128)(2,1)}, bf16[512,512]{1,0:T(8,128)(2,1)S(1)}, bf16[512,512]{1,0:T(8,128)(2,1)}, bf16[512,512]{1,0:T(8,128)(2,1)S(1)}) fusion(bf16[1,512,8704]{2,1,0:T(8,128)(2,1)} %param.5, s32[]{:T(128)S(6)} %select_n.324, s32[]{:T(128)S(6)} %select_n.322, s32[]{:T(128)S(6)} %select_n.321, s32[]{:T(128)S(6)} %select_n.323), kind=kLoop, calls=%fused_computation.53 | loop fusion | bytes 4194320 | tf_op jit(solution)/shard_map/dynamic_slice | solution.py:137
  30.1 0.8 add.549
  30.9 1.6 %collective-permute-start.5 = (f32[32,512]{1,0:T(8,128)S(1)}, f32[32,512]{1,0:T(8,128)S(1)}, u32[]{:S(2)}, u32[]{:S(2)}) collective-permute-start(f32[32,512]{1,0:T(8,128)S(1)} %add.549), channel_id=1, source_target_pairs={{0,8},{4,12},{8,0},{12,4},{16,24},{20,28},{24,16},{28,20},{1,9},{5... | collective-permute-start | bytes 196616 | tf_op jit(solution)/shard_map/ppermute | solution.py:12
  32.5 1.6 %collective-permute-start.6 = (f32[32,512]{1,0:T(8,128)S(1)}, f32[32,512]{1,0:T(8,128)}, u32[]{:S(2)}, u32[]{:S(2)}) collective-permute-start(f32[32,512]{1,0:T(8,128)S(1)} %add.549), channel_id=1, source_target_pairs={{0,4},{4,0},{8,12},{12,8},{16,20},{20,16},{24,28},{28,24},{1,5},{5... | collective-permute-start | bytes 196616 | tf_op jit(solution)/shard_map/ppermute | solution.py:12
  34.5 1.9 %dynamic-slice_bitcast_fusion.8 = (bf16[512,128]{1,0:T(8,128)(2,1)}, bf16[512,128]{1,0:T(8,128)(2,1)}, bf16[512,128]{1,0:T(8,128)(2,1)}, bf16[512,128]{1,0:T(8,128)(2,1)}) fusion(bf16[1,512,8704]{2,1,0:T(8,128)(2,1)} %param.5, s32[]{:T(128)S(6)} %select_n.300, s32[]{:T(128)S(6)} %select_n.299, s32[]{:T(128)S(6)} %select_n.298, s32[]{:T(128)S(6)} %select_n.297), kind=kLoop, calls=%fused_computation.88 | loop fusion | bytes 1048592 | tf_op jit(solution)/shard_map/dynamic_slice | solution.py:137
  36.4 1.1 %collective-permute-done.6 = f32[32,512]{1,0:T(8,128)} collective-permute-done((f32[32,512]{1,0:T(8,128)S(1)}, f32[32,512]{1,0:T(8,128)}, u32[]{:S(2)}, u32[]{:S(2)}) %collective-permute-start.6) | collective-permute-done | bytes 65568 | tf_op jit(solution)/shard_map/ppermute | solution.py:12
  37.5 1.9 %collective-permute-done.7 = f32[32,512]{1,0:T(8,128)} collective-permute-done((f32[32,512]{1,0:T(8,128)S(1)}, f32[32,512]{1,0:T(8,128)}, u32[]{:S(2)}, u32[]{:S(2)}) %collective-permute-start.7) | collective-permute-done | bytes 65568 | tf_op jit(solution)/shard_map/ppermute | solution.py:12
  39.4 0.9 broadcast_select_fusion.3
  40.3 0.6 copy-done.5
  40.9 1.7 %fusion.56 = f32[64,128]{1,0:T(8,128)} fusion(bf16[64,512]{1,0:T(8,128)(2,1)S(1)} %fusion.45, bf16[512,128]{1,0:T(8,128)(2,1)} %get-tuple-element.30), kind=kOutput, calls=%fused_computation.138 | convolution fusion | flops 8388608 | bytes 229376 | tf_op jit(solution)/shard_map/dot_general | solution.py:196
  42.6 1.7 %fusion.55 = f32[64,128]{1,0:T(8,128)} fusion(bf16[64,512]{1,0:T(8,128)(2,1)S(1)} %fusion.45, bf16[512,128]{1,0:T(8,128)(2,1)} %get-tuple-element.29), kind=kOutput, calls=%fused_computation.137 | convolution fusion | flops 8388608 | bytes 229376 | tf_op jit(solution)/shard_map/dot_general | solution.py:196
  44.3 1.3 %collective-permute-start.8 = (f32[64,128]{1,0:T(8,128)}, f32[64,128]{1,0:T(8,128)}, u32[]{:S(2)}, u32[]{:S(2)}) collective-permute-start(f32[64,128]{1,0:T(8,128)} %fusion.55), channel_id=1, source_target_pairs={{0,2},{1,3},{2,0},{3,1},{4,6},{5,7},{6,4},{7,5},{8,10},{9,11},{10,... | collective-permute-start | bytes 98312 | tf_op jit(solution)/shard_map/ppermute | solution.py:10
  45.5 1.7 %fusion.57 = f32[64,128]{1,0:T(8,128)} fusion(bf16[64,512]{1,0:T(8,128)(2,1)S(1)} %fusion.45, bf16[512,128]{1,0:T(8,128)(2,1)} %get-tuple-element.31), kind=kOutput, calls=%fused_computation.139 | convolution fusion | flops 8388608 | bytes 229376 | tf_op jit(solution)/shard_map/dot_general | solution.py:196
  47.2 0.6 collective-permute-start.10
  47.8 2.2 %dynamic-slice_bitcast_fusion.4 = (bf16[512,256]{1,0:T(8,128)(2,1)}, bf16[512,256]{1,0:T(8,128)(2,1)}, bf16[512,256]{1,0:T(8,128)(2,1)}, bf16[512,256]{1,0:T(8,128)(2,1)}) fusion(bf16[1,512,8704]{2,1,0:T(8,128)(2,1)} %param.5, s32[]{:T(128)S(6)} %select_n.311, s32[]{:T(128)S(6)} %select_n.310, s32[]{:T(128)S(6)} %select_n.309, s32[]{:T(128)S(6)} %select_n.308), kind=kLoop, calls=%fused_computation.75 | loop fusion | bytes 2097168 | tf_op jit(solution)/shard_map/dynamic_slice | solution.py:137
  50.1 1.2 %select_convert_fusion.1 = bf16[64,128]{1,0:T(8,128)(2,1)S(1)} fusion(f32[64,128]{1,0:T(8,128)} %slice_bitcast_fusion.2, f32[64,128]{1,0:T(8,128)} %collective-permute-done.10, f32[64,128]{1,0:T(8,128)} %collective-permute-done.8, f32[64,128]{1,0:T(8,128)} %collective-permute-done.9, pred[128]{0:T(512)(128)(4,1)S(1)} %slice_bitcast_fusion.3, ...), kind=kOutput, calls=%fused_computation.100 | convolution fusion | flops 8437760 | bytes 344192 | tf_op jit(solution)/shard_map/dot_general | solution.py:196
  51.3 1.1 %fusion.59 = f32[64,512]{1,0:T(8,128)S(1)} fusion(bf16[64,128]{1,0:T(8,128)(2,1)S(1)} %select_convert_fusion.1, bf16[128,512]{1,0:T(8,128)(2,1)} %get-tuple-element.36), kind=kOutput, calls=%fused_computation.141 | convolution fusion | flops 8388608 | bytes 278528 | tf_op jit(solution)/shard_map/dot_general | solution.py:209
  52.5 1.0 fusion.58
  54.1 1.1 convolution_add_fusion.7
  55.2 1.3 %collective-permute-start.13 = (f32[32,512]{1,0:T(8,128)S(1)}, f32[32,512]{1,0:T(8,128)S(1)}, u32[]{:S(2)}, u32[]{:S(2)}) collective-permute-start(f32[32,512]{1,0:T(8,128)S(1)} %get-tuple-element.87), channel_id=1, source_target_pairs={{0,2},{1,3},{2,0},{3,1},{4,6},{5,7},{6,4},{7,5},{8,10},{9,11},{10,... | collective-permute-start | bytes 196616 | tf_op jit(solution)/shard_map/ppermute | solution.py:10
  56.5 0.7 collective-permute-start.15
  57.2 1.1 convolution_add_fusion.8
  58.3 1.6 %collective-permute-start.14 = (f32[32,512]{1,0:T(8,128)S(1)}, f32[32,512]{1,0:T(8,128)S(1)}, u32[]{:S(2)}, u32[]{:S(2)}) collective-permute-start(f32[32,512]{1,0:T(8,128)S(1)} %constant_dynamic-slice_fusion.1), channel_id=1, source_target_pairs={{0,4},{4,0},{8,12},{12,8},{16,20},{20,16},{24,28},{28,24},{1,5},{5... | collective-permute-start | bytes 196616 | tf_op jit(solution)/shard_map/ppermute | solution.py:12
  59.9 2.1 %collective-permute-done.15 = f32[32,512]{1,0:T(8,128)S(1)} collective-permute-done((f32[32,512]{1,0:T(8,128)S(1)}, f32[32,512]{1,0:T(8,128)S(1)}, u32[]{:S(2)}, u32[]{:S(2)}) %collective-permute-start.15) | collective-permute-done | bytes 65568 | tf_op jit(solution)/shard_map/ppermute | solution.py:14
  62.6 0.6 collective-permute-start.16
  63.2 1.5 %collective-permute-start.17 = (f32[32,512]{1,0:T(8,128)S(1)}, f32[32,512]{1,0:T(8,128)S(1)}, u32[]{:S(2)}, u32[]{:S(2)}) collective-permute-start(f32[32,512]{1,0:T(8,128)S(1)} %add_add_fusion.1), channel_id=1, source_target_pairs={{0,4},{4,0},{8,12},{12,8},{16,20},{20,16},{24,28},{28,24},{1,5},{5... | collective-permute-start | bytes 196616 | tf_op jit(solution)/shard_map/ppermute | solution.py:12
  64.7 1.5 %collective-permute-start.18 = (f32[32,512]{1,0:T(8,128)S(1)}, f32[32,512]{1,0:T(8,128)S(1)}, u32[]{:S(2)}, u32[]{:S(2)}) collective-permute-start(f32[32,512]{1,0:T(8,128)S(1)} %add_add_fusion.1), channel_id=1, source_target_pairs={{0,12},{4,8},{8,4},{12,0},{16,28},{20,24},{24,20},{28,16},{1,13},{... | collective-permute-start | bytes 196616 | tf_op jit(solution)/shard_map/ppermute | solution.py:12
  66.2 1.5 %fusion.11 = f32[64,1024]{1,0:T(8,128)S(1)} fusion(bf16[64,512]{1,0:T(8,128)(2,1)S(1)} %fusion.45, bf16[512,8704]{1,0:T(8,128)(2,1)} %bitcast.140), kind=kOutput, calls=%fused_computation.26 | convolution fusion | flops 67108864 | bytes 1376256 | tf_op jit(solution)/shard_map/dot_general | solution.py:219
  67.7 2.1 %collective-permute-done.18 = f32[32,512]{1,0:T(8,128)S(1)} collective-permute-done((f32[32,512]{1,0:T(8,128)S(1)}, f32[32,512]{1,0:T(8,128)S(1)}, u32[]{:S(2)}, u32[]{:S(2)}) %collective-permute-start.18) | collective-permute-done | bytes 65568 | tf_op jit(solution)/shard_map/ppermute | solution.py:12
  69.9 1.1 %convolution_add_fusion.13 = f32[64,256]{1,0:T(8,128)S(1)} fusion(bf16[64,512]{1,0:T(8,128)(2,1)S(1)} %fusion.43, bf16[512,256]{1,0:T(8,128)(2,1)} %get-tuple-element.38, f32[64,1024]{1,0:T(8,128)S(1)} %fusion.11, s32[]{:T(128)S(6)} %select_n.313), kind=kOutput, calls=%fused_computation.24 | convolution fusion | flops 16793600 | bytes 458756 | tf_op jit(solution)/shard_map/dot_general | solution.py:196
  71.1 1.1 %convolution_add_fusion.14 = f32[64,256]{1,0:T(8,128)S(1)} fusion(bf16[64,512]{1,0:T(8,128)(2,1)S(1)} %fusion.43, bf16[512,256]{1,0:T(8,128)(2,1)} %get-tuple-element.37, f32[64,1024]{1,0:T(8,128)S(1)} %fusion.11, s32[]{:T(128)S(6)} %select_n.312), kind=kOutput, calls=%fused_computation.25 | convolution fusion | flops 16793600 | bytes 458756 | tf_op jit(solution)/shard_map/dot_general | solution.py:196
  72.2 1.4 %collective-permute-start.19 = (f32[64,256]{1,0:T(8,128)S(1)}, f32[64,256]{1,0:T(8,128)S(1)}, u32[]{:S(2)}, u32[]{:S(2)}) collective-permute-start(f32[64,256]{1,0:T(8,128)S(1)} %convolution_add_fusion.14), channel_id=1, source_target_pairs={{0,2},{1,3},{2,0},{3,1},{4,6},{5,7},{6,4},{7,5},{8,10},{9,11},{10,... | collective-permute-start | bytes 196616 | tf_op jit(solution)/shard_map/ppermute | solution.py:10
  73.6 1.1 %convolution_add_fusion.12 = f32[64,256]{1,0:T(8,128)S(1)} fusion(bf16[64,512]{1,0:T(8,128)(2,1)S(1)} %fusion.43, bf16[512,256]{1,0:T(8,128)(2,1)} %get-tuple-element.39, f32[64,1024]{1,0:T(8,128)S(1)} %fusion.11, s32[]{:T(128)S(6)} %select_n.314), kind=kOutput, calls=%fused_computation.23 | convolution fusion | flops 16793600 | bytes 458756 | tf_op jit(solution)/shard_map/dot_general | solution.py:196
  74.7 0.6 collective-permute-start.21
  75.3 2.1 %fusion.1 = f32[64,2048]{1,0:T(8,128)S(1)} fusion(bf16[64,512]{1,0:T(8,128)(2,1)S(1)} %fusion.45, bf16[512,8704]{1,0:T(8,128)(2,1)} %bitcast.141), kind=kOutput, calls=%fused_computation.2 | convolution fusion | flops 134217728 | bytes 2686976 | tf_op jit(solution)/shard_map/dot_general | solution.py:219
  77.4 1.1 %select_convert_fusion = bf16[64,256]{1,0:T(8,128)(2,1)S(1)} fusion(f32[64,256]{1,0:T(8,128)} %slice_bitcast_fusion.1, f32[64,256]{1,0:T(8,128)S(1)} %collective-permute-done.21, f32[64,256]{1,0:T(8,128)S(1)} %collective-permute-done.19, f32[64,256]{1,0:T(8,128)S(1)} %collective-permute-done.20, pred[256]{0:T(512)(128)(4,1)S(1)} %slice_reduce_fusion.1, ...), kind=kOutput, calls=%fused_computation.96 | convolution fusion | flops 16891904 | bytes 688388 | tf_op jit(solution)/shard_map/dot_general | solution.py:196
  79.5 0.6 collective-permute-done.23
  80.3 1.4 %collective-permute-start.24 = (f32[64,512]{1,0:T(8,128)S(1)}, f32[64,512]{1,0:T(8,128)S(1)}, u32[]{:S(2)}, u32[]{:S(2)}) collective-permute-start(f32[64,512]{1,0:T(8,128)S(1)} %convolution_add_fusion.9), channel_id=1, source_target_pairs={{0,2},{1,3},{2,0},{3,1},{4,6},{5,7},{6,4},{7,5},{8,10},{9,11},{10,... | collective-permute-start | bytes 393224 | tf_op jit(solution)/shard_map/ppermute | solution.py:10
  81.7 0.7 collective-permute-start.26
  82.5 1.6 %collective-permute-start.25 = (f32[64,512]{1,0:T(8,128)S(1)}, f32[64,512]{1,0:T(8,128)S(1)}, u32[]{:S(2)}, u32[]{:S(2)}) collective-permute-start(f32[64,512]{1,0:T(8,128)S(1)} %convolution_add_fusion.10), channel_id=1, source_target_pairs={{0,4},{4,0},{8,12},{12,8},{16,20},{20,16},{24,28},{28,24},{1,5},{5... | collective-permute-start | bytes 393224 | tf_op jit(solution)/shard_map/ppermute | solution.py:12
  84.1 2.1 %convolution_add_fusion = f32[64,2048]{1,0:T(8,128)S(1)} fusion(f32[64,2048]{1,0:T(8,128)S(1)} %fusion.1, bf16[64,512]{1,0:T(8,128)(2,1)S(1)} %fusion.43, bf16[512,8704]{1,0:T(8,128)(2,1)} %bitcast.142), kind=kOutput, calls=%fused_computation | convolution fusion | flops 134348800 | bytes 3211264 | tf_op jit(solution)/shard_map/dot_general | solution.py:219
  86.2 2.3 %collective-permute-done.24 = f32[64,512]{1,0:T(8,128)S(1)} collective-permute-done((f32[64,512]{1,0:T(8,128)S(1)}, f32[64,512]{1,0:T(8,128)S(1)}, u32[]{:S(2)}, u32[]{:S(2)}) %collective-permute-start.24) | collective-permute-done | bytes 131104 | tf_op jit(solution)/shard_map/ppermute | solution.py:10
  89.0 1.0 collective-permute-done.25
  91.1 0.6 collective-permute-done.28
  91.9 1.4 %collective-permute-start.29 = (f32[64,512]{1,0:T(8,128)S(1)}, f32[64,512]{1,0:T(8,128)S(1)}, u32[]{:S(2)}, u32[]{:S(2)}) collective-permute-start(f32[64,512]{1,0:T(8,128)S(1)} %fusion.5), channel_id=1, source_target_pairs={{0,2},{1,3},{2,0},{3,1},{4,6},{5,7},{6,4},{7,5},{8,10},{9,11},{10,... | collective-permute-start | bytes 393224 | tf_op jit(solution)/shard_map/ppermute | solution.py:10
  93.4 4.1 %collective-permute-done.29 = f32[64,512]{1,0:T(8,128)S(1)} collective-permute-done((f32[64,512]{1,0:T(8,128)S(1)}, f32[64,512]{1,0:T(8,128)S(1)}, u32[]{:S(2)}, u32[]{:S(2)}) %collective-permute-start.29) | collective-permute-done | bytes 131104 | tf_op jit(solution)/shard_map/ppermute | solution.py:10
  98.8 0.6 collective-permute-done.31
  99.5 1.4 %collective-permute-start.32 = (f32[64,512]{1,0:T(8,128)S(1)}, f32[64,512]{1,0:T(8,128)S(1)}, u32[]{:S(2)}, u32[]{:S(2)}) collective-permute-start(f32[64,512]{1,0:T(8,128)S(1)} %convolution_add_fusion.1), channel_id=1, source_target_pairs={{0,2},{1,3},{2,0},{3,1},{4,6},{5,7},{6,4},{7,5},{8,10},{9,11},{10,... | collective-permute-start | bytes 393224 | tf_op jit(solution)/shard_map/ppermute | solution.py:10
  101.0 4.2 %collective-permute-done.32 = f32[64,512]{1,0:T(8,128)S(1)} collective-permute-done((f32[64,512]{1,0:T(8,128)S(1)}, f32[64,512]{1,0:T(8,128)S(1)}, u32[]{:S(2)}, u32[]{:S(2)}) %collective-permute-start.32) | collective-permute-done | bytes 131104 | tf_op jit(solution)/shard_map/ppermute | solution.py:10
  105.4 0.8 maximum_bitcast_fusion
  (86 shorter events, 7.8 us)
Async XLA Ops:
  2.1 14.2 %collective-permute-start = (f32[64,1024]{1,0:T(8,128)S(1)}, f32[64,1024]{1,0:T(8,128)S(1)}, u32[]{:S(2)}, u32[]{:S(2)}) collective-permute-start(f32[64,1024]{1,0:T(8,128)S(1)} %pad_maximum_fusion), channel_id=1, source_target_pairs={{0,1},{1,0},{2,3},{3,2},{4,5},{5,4},{6,7},{7,6},{8,9},{9,8},{10,11... | collective-permute-start | bytes 786440 | tf_op jit(solution)/shard_map/ppermute | solution.py:10
  16.3 6.0 %collective-permute-start.1 = (f32[32,512]{1,0:T(8,128)S(1)}, f32[32,512]{1,0:T(8,128)S(1)}, u32[]{:S(2)}, u32[]{:S(2)}) collective-permute-start(f32[32,512]{1,0:T(8,128)S(1)} %get-tuple-element.89), channel_id=1, source_target_pairs={{0,2},{1,3},{2,0},{3,1},{4,6},{5,7},{6,4},{7,5},{8,10},{9,11},{10,... | collective-permute-start | bytes 196616 | tf_op jit(solution)/shard_map/ppermute | solution.py:10
  18.9 5.4 %collective-permute-start.3 = (f32[32,512]{1,0:T(8,128)S(1)}, f32[32,512]{1,0:T(8,128)S(1)}, u32[]{:S(2)}, u32[]{:S(2)}) collective-permute-start(f32[32,512]{1,0:T(8,128)S(1)} %get-tuple-element.90), channel_id=1, source_target_pairs={{0,6},{1,7},{2,4},{3,5},{4,2},{5,3},{6,0},{7,1},{8,14},{9,15},{10,... | collective-permute-start | bytes 196616 | tf_op jit(solution)/shard_map/ppermute | solution.py:14
  20.4 4.3 %collective-permute-start.2 = (f32[32,512]{1,0:T(8,128)S(1)}, f32[32,512]{1,0:T(8,128)S(1)}, u32[]{:S(2)}, u32[]{:S(2)}) collective-permute-start(f32[32,512]{1,0:T(8,128)S(1)} %constant_dynamic-slice_fusion.4), channel_id=1, source_target_pairs={{0,4},{4,0},{8,12},{12,8},{16,20},{20,16},{24,28},{28,24},{1,5},{5... | collective-permute-start | bytes 196616 | tf_op jit(solution)/shard_map/ppermute | solution.py:12
  24.7 5.4 %collective-permute-start.4 = (f32[32,512]{1,0:T(8,128)S(1)}, f32[32,512]{1,0:T(8,128)}, u32[]{:S(2)}, u32[]{:S(2)}) collective-permute-start(f32[32,512]{1,0:T(8,128)S(1)} %add_add_fusion.2), channel_id=1, source_target_pairs={{0,16},{4,20},{8,24},{12,28},{16,0},{20,4},{24,8},{28,12},{1,17},{... | collective-permute-start | bytes 196616 | tf_op jit(solution)/shard_map/ppermute | solution.py:12
  30.9 6.5 %copy-start.7 = (f32[32,512]{1,0:T(8,128)}, f32[32,512]{1,0:T(8,128)S(1)}, u32[]{:S(2)}) copy-start(f32[32,512]{1,0:T(8,128)S(1)} %add.549) | copy-start | bytes 196612
  30.9 5.5 %collective-permute-start.5 = (f32[32,512]{1,0:T(8,128)S(1)}, f32[32,512]{1,0:T(8,128)S(1)}, u32[]{:S(2)}, u32[]{:S(2)}) collective-permute-start(f32[32,512]{1,0:T(8,128)S(1)} %add.549), channel_id=1, source_target_pairs={{0,8},{4,12},{8,0},{12,4},{16,24},{20,28},{24,16},{28,20},{1,9},{5... | collective-permute-start | bytes 196616 | tf_op jit(solution)/shard_map/ppermute | solution.py:12
  32.5 4.9 %collective-permute-start.6 = (f32[32,512]{1,0:T(8,128)S(1)}, f32[32,512]{1,0:T(8,128)}, u32[]{:S(2)}, u32[]{:S(2)}) collective-permute-start(f32[32,512]{1,0:T(8,128)S(1)} %add.549), channel_id=1, source_target_pairs={{0,4},{4,0},{8,12},{12,8},{16,20},{20,16},{24,28},{28,24},{1,5},{5... | collective-permute-start | bytes 196616 | tf_op jit(solution)/shard_map/ppermute | solution.py:12
  34.1 5.3 %collective-permute-start.7 = (f32[32,512]{1,0:T(8,128)S(1)}, f32[32,512]{1,0:T(8,128)}, u32[]{:S(2)}, u32[]{:S(2)}) collective-permute-start(f32[32,512]{1,0:T(8,128)S(1)} %add.549), channel_id=1, source_target_pairs={{0,12},{4,8},{8,4},{12,0},{16,28},{20,24},{24,20},{28,16},{1,13},{... | collective-permute-start | bytes 196616 | tf_op jit(solution)/shard_map/ppermute | solution.py:12
  40.3 0.6 copy-start.5
  42.6 7.5 %collective-permute-start.9 = (f32[64,128]{1,0:T(8,128)}, f32[64,128]{1,0:T(8,128)}, u32[]{:S(2)}, u32[]{:S(2)}) collective-permute-start(f32[64,128]{1,0:T(8,128)} %fusion.56), channel_id=1, source_target_pairs={{0,3},{1,2},{2,1},{3,0},{4,7},{5,6},{6,5},{7,4},{8,11},{9,10},{10,... | collective-permute-start | bytes 98312 | tf_op jit(solution)/shard_map/ppermute | solution.py:10
  44.3 5.8 %collective-permute-start.8 = (f32[64,128]{1,0:T(8,128)}, f32[64,128]{1,0:T(8,128)}, u32[]{:S(2)}, u32[]{:S(2)}) collective-permute-start(f32[64,128]{1,0:T(8,128)} %fusion.55), channel_id=1, source_target_pairs={{0,2},{1,3},{2,0},{3,1},{4,6},{5,7},{6,4},{7,5},{8,10},{9,11},{10,... | collective-permute-start | bytes 98312 | tf_op jit(solution)/shard_map/ppermute | solution.py:10
  47.2 2.9 %collective-permute-start.10 = (f32[64,128]{1,0:T(8,128)}, f32[64,128]{1,0:T(8,128)}, u32[]{:S(2)}, u32[]{:S(2)}) collective-permute-start(f32[64,128]{1,0:T(8,128)} %fusion.57), channel_id=1, source_target_pairs={{0,1},{1,0},{2,3},{3,2},{4,5},{5,4},{6,7},{7,6},{8,9},{9,8},{10,11... | collective-permute-start | bytes 98312 | tf_op jit(solution)/shard_map/ppermute | solution.py:10
  50.0 28.5 %copy-start.4 = (bf16[256,512]{1,0:T(8,128)(2,1)S(1)}, bf16[256,512]{1,0:T(8,128)(2,1)}, u32[]{:S(2)}) copy-start(bf16[256,512]{1,0:T(8,128)(2,1)} %get-tuple-element.44) | copy-start | bytes 786436
  50.0 28.8 %copy-start.3 = (bf16[256,512]{1,0:T(8,128)(2,1)S(1)}, bf16[256,512]{1,0:T(8,128)(2,1)}, u32[]{:S(2)}) copy-start(bf16[256,512]{1,0:T(8,128)(2,1)} %get-tuple-element.42) | copy-start | bytes 786436
  50.0 30.1 %copy-start.2 = (bf16[256,512]{1,0:T(8,128)(2,1)S(1)}, bf16[256,512]{1,0:T(8,128)(2,1)}, u32[]{:S(2)}) copy-start(bf16[256,512]{1,0:T(8,128)(2,1)} %get-tuple-element.43) | copy-start | bytes 786436
  50.0 40.0 %copy-start = (bf16[512,512]{1,0:T(8,128)(2,1)S(1)}, bf16[512,512]{1,0:T(8,128)(2,1)}, u32[]{:S(2)}) copy-start(bf16[512,512]{1,0:T(8,128)(2,1)} %get-tuple-element.48) | copy-start | bytes 1572868
  50.1 43.2 %copy-start.8 = (f32[1,64,960]{2,1,0:T(8,128)S(1)}, f32[1,64,960]{2,1,0:T(8,128)}, u32[]{:S(2)}) copy-start(f32[1,64,960]{2,1,0:T(8,128)} %param.4) | copy-start | bytes 737284
  51.3 46.2 %copy-start.1 = (bf16[512,512]{1,0:T(8,128)(2,1)S(1)}, bf16[512,512]{1,0:T(8,128)(2,1)}, u32[]{:S(2)}) copy-start(bf16[512,512]{1,0:T(8,128)(2,1)} %get-tuple-element.45) | copy-start | bytes 1572868
  52.4 1.7 %collective-permute-start.12 = (f32[64,512]{1,0:T(8,128)S(1)}, f32[64,512]{1,0:T(8,128)S(1)}, u32[]{:S(2)}, u32[]{:S(2)}) collective-permute-start(f32[64,512]{1,0:T(8,128)S(1)} %fusion.59), channel_id=1, source_target_pairs={{0,1},{1,0},{2,3},{3,2},{4,5},{5,4},{6,7},{7,6},{8,9},{9,8},{10,11... | collective-permute-start | bytes 393224 | tf_op jit(solution)/shard_map/ppermute | solution.py:10
  53.6 3.6 %collective-permute-start.11 = (f32[64,512]{1,0:T(8,128)S(1)}, f32[64,512]{1,0:T(8,128)S(1)}, u32[]{:S(2)}, u32[]{:S(2)}) collective-permute-start(f32[64,512]{1,0:T(8,128)S(1)} %fusion.58), channel_id=1, source_target_pairs={{0,1},{1,0},{2,3},{3,2},{4,5},{5,4},{6,7},{7,6},{8,9},{9,8},{10,11... | collective-permute-start | bytes 393224 | tf_op jit(solution)/shard_map/ppermute | solution.py:10
  55.2 4.7 %collective-permute-start.13 = (f32[32,512]{1,0:T(8,128)S(1)}, f32[32,512]{1,0:T(8,128)S(1)}, u32[]{:S(2)}, u32[]{:S(2)}) collective-permute-start(f32[32,512]{1,0:T(8,128)S(1)} %get-tuple-element.87), channel_id=1, source_target_pairs={{0,2},{1,3},{2,0},{3,1},{4,6},{5,7},{6,4},{7,5},{8,10},{9,11},{10,... | collective-permute-start | bytes 196616 | tf_op jit(solution)/shard_map/ppermute | solution.py:10
  56.5 5.5 %collective-permute-start.15 = (f32[32,512]{1,0:T(8,128)S(1)}, f32[32,512]{1,0:T(8,128)S(1)}, u32[]{:S(2)}, u32[]{:S(2)}) collective-permute-start(f32[32,512]{1,0:T(8,128)S(1)} %get-tuple-element.88), channel_id=1, source_target_pairs={{0,6},{1,7},{2,4},{3,5},{4,2},{5,3},{6,0},{7,1},{8,14},{9,15},{10,... | collective-permute-start | bytes 196616 | tf_op jit(solution)/shard_map/ppermute | solution.py:14
  58.3 4.3 %collective-permute-start.14 = (f32[32,512]{1,0:T(8,128)S(1)}, f32[32,512]{1,0:T(8,128)S(1)}, u32[]{:S(2)}, u32[]{:S(2)}) collective-permute-start(f32[32,512]{1,0:T(8,128)S(1)} %constant_dynamic-slice_fusion.1), channel_id=1, source_target_pairs={{0,4},{4,0},{8,12},{12,8},{16,20},{20,16},{24,28},{28,24},{1,5},{5... | collective-permute-start | bytes 196616 | tf_op jit(solution)/shard_map/ppermute | solution.py:12
  62.6 5.1 %collective-permute-start.16 = (f32[32,512]{1,0:T(8,128)S(1)}, f32[32,512]{1,0:T(8,128)S(1)}, u32[]{:S(2)}, u32[]{:S(2)}) collective-permute-start(f32[32,512]{1,0:T(8,128)S(1)} %add_add_fusion.1), channel_id=1, source_target_pairs={{0,8},{4,12},{8,0},{12,4},{16,24},{20,28},{24,16},{28,20},{1,9},{5... | collective-permute-start | bytes 196616 | tf_op jit(solution)/shard_map/ppermute | solution.py:12
  63.2 4.5 %collective-permute-start.17 = (f32[32,512]{1,0:T(8,128)S(1)}, f32[32,512]{1,0:T(8,128)S(1)}, u32[]{:S(2)}, u32[]{:S(2)}) collective-permute-start(f32[32,512]{1,0:T(8,128)S(1)} %add_add_fusion.1), channel_id=1, source_target_pairs={{0,4},{4,0},{8,12},{12,8},{16,20},{20,16},{24,28},{28,24},{1,5},{5... | collective-permute-start | bytes 196616 | tf_op jit(solution)/shard_map/ppermute | solution.py:12
  64.7 5.2 %collective-permute-start.18 = (f32[32,512]{1,0:T(8,128)S(1)}, f32[32,512]{1,0:T(8,128)S(1)}, u32[]{:S(2)}, u32[]{:S(2)}) collective-permute-start(f32[32,512]{1,0:T(8,128)S(1)} %add_add_fusion.1), channel_id=1, source_target_pairs={{0,12},{4,8},{8,4},{12,0},{16,28},{20,24},{24,20},{28,16},{1,13},{... | collective-permute-start | bytes 196616 | tf_op jit(solution)/shard_map/ppermute | solution.py:12
  67.7 33.2 %copy-start.6 = (f32[32,512]{1,0:T(8,128)S(1)}, f32[32,512]{1,0:T(8,128)}, u32[]{:S(2)}) copy-start(f32[32,512]{1,0:T(8,128)} %copy-done.5) | copy-start | bytes 196612
  71.0 6.4 %collective-permute-start.20 = (f32[64,256]{1,0:T(8,128)S(1)}, f32[64,256]{1,0:T(8,128)S(1)}, u32[]{:S(2)}, u32[]{:S(2)}) collective-permute-start(f32[64,256]{1,0:T(8,128)S(1)} %convolution_add_fusion.13), channel_id=1, source_target_pairs={{0,3},{1,2},{2,1},{3,0},{4,7},{5,6},{6,5},{7,4},{8,11},{9,10},{10,... | collective-permute-start | bytes 196616 | tf_op jit(solution)/shard_map/ppermute | solution.py:10
  72.2 5.2 %collective-permute-start.19 = (f32[64,256]{1,0:T(8,128)S(1)}, f32[64,256]{1,0:T(8,128)S(1)}, u32[]{:S(2)}, u32[]{:S(2)}) collective-permute-start(f32[64,256]{1,0:T(8,128)S(1)} %convolution_add_fusion.14), channel_id=1, source_target_pairs={{0,2},{1,3},{2,0},{3,1},{4,6},{5,7},{6,4},{7,5},{8,10},{9,11},{10,... | collective-permute-start | bytes 196616 | tf_op jit(solution)/shard_map/ppermute | solution.py:10
  74.7 2.7 %collective-permute-start.21 = (f32[64,256]{1,0:T(8,128)S(1)}, f32[64,256]{1,0:T(8,128)S(1)}, u32[]{:S(2)}, u32[]{:S(2)}) collective-permute-start(f32[64,256]{1,0:T(8,128)S(1)} %convolution_add_fusion.12), channel_id=1, source_target_pairs={{0,1},{1,0},{2,3},{3,2},{4,5},{5,4},{6,7},{7,6},{8,9},{9,8},{10,11... | collective-permute-start | bytes 196616 | tf_op jit(solution)/shard_map/ppermute | solution.py:10
  78.7 1.4 %collective-permute-start.23 = (f32[64,512]{1,0:T(8,128)S(1)}, f32[64,512]{1,0:T(8,128)S(1)}, u32[]{:S(2)}, u32[]{:S(2)}) collective-permute-start(f32[64,512]{1,0:T(8,128)S(1)} %fusion.61), channel_id=1, source_target_pairs={{0,1},{1,0},{2,3},{3,2},{4,5},{5,4},{6,7},{7,6},{8,9},{9,8},{10,11... | collective-permute-start | bytes 393224 | tf_op jit(solution)/shard_map/ppermute | solution.py:10
  79.0 3.4 %collective-permute-start.22 = (f32[64,512]{1,0:T(8,128)S(1)}, f32[64,512]{1,0:T(8,128)S(1)}, u32[]{:S(2)}, u32[]{:S(2)}) collective-permute-start(f32[64,512]{1,0:T(8,128)S(1)} %fusion.60), channel_id=1, source_target_pairs={{0,1},{1,0},{2,3},{3,2},{4,5},{5,4},{6,7},{7,6},{8,9},{9,8},{10,11... | collective-permute-start | bytes 393224 | tf_op jit(solution)/shard_map/ppermute | solution.py:10
  80.3 8.2 %collective-permute-start.24 = (f32[64,512]{1,0:T(8,128)S(1)}, f32[64,512]{1,0:T(8,128)S(1)}, u32[]{:S(2)}, u32[]{:S(2)}) collective-permute-start(f32[64,512]{1,0:T(8,128)S(1)} %convolution_add_fusion.9), channel_id=1, source_target_pairs={{0,2},{1,3},{2,0},{3,1},{4,6},{5,7},{6,4},{7,5},{8,10},{9,11},{10,... | collective-permute-start | bytes 393224 | tf_op jit(solution)/shard_map/ppermute | solution.py:10
  81.7 7.3 %collective-permute-start.26 = (f32[64,512]{1,0:T(8,128)S(1)}, f32[64,512]{1,0:T(8,128)S(1)}, u32[]{:S(2)}, u32[]{:S(2)}) collective-permute-start(f32[64,512]{1,0:T(8,128)S(1)} %convolution_add_fusion.9), channel_id=1, source_target_pairs={{0,6},{1,7},{2,4},{3,5},{4,2},{5,3},{6,0},{7,1},{8,14},{9,15},{10,... | collective-permute-start | bytes 393224 | tf_op jit(solution)/shard_map/ppermute | solution.py:14
  82.5 7.5 %collective-permute-start.25 = (f32[64,512]{1,0:T(8,128)S(1)}, f32[64,512]{1,0:T(8,128)S(1)}, u32[]{:S(2)}, u32[]{:S(2)}) collective-permute-start(f32[64,512]{1,0:T(8,128)S(1)} %convolution_add_fusion.10), channel_id=1, source_target_pairs={{0,4},{4,0},{8,12},{12,8},{16,20},{20,16},{24,28},{28,24},{1,5},{5... | collective-permute-start | bytes 393224 | tf_op jit(solution)/shard_map/ppermute | solution.py:12
  90.2 1.4 %collective-permute-start.28 = (f32[64,512]{1,0:T(8,128)S(1)}, f32[64,512]{1,0:T(8,128)S(1)}, u32[]{:S(2)}, u32[]{:S(2)}) collective-permute-start(f32[64,512]{1,0:T(8,128)S(1)} %convolution_add_fusion.3), channel_id=1, source_target_pairs={{0,1},{1,0},{2,3},{3,2},{4,5},{5,4},{6,7},{7,6},{8,9},{9,8},{10,11... | collective-permute-start | bytes 393224 | tf_op jit(solution)/shard_map/ppermute | solution.py:10
  90.5 2.8 %collective-permute-start.27 = (f32[64,512]{1,0:T(8,128)S(1)}, f32[64,512]{1,0:T(8,128)S(1)}, u32[]{:S(2)}, u32[]{:S(2)}) collective-permute-start(f32[64,512]{1,0:T(8,128)S(1)} %convolution_add_fusion.5), channel_id=1, source_target_pairs={{0,1},{1,0},{2,3},{3,2},{4,5},{5,4},{6,7},{7,6},{8,9},{9,8},{10,11... | collective-permute-start | bytes 393224 | tf_op jit(solution)/shard_map/ppermute | solution.py:10
  91.9 5.6 %collective-permute-start.29 = (f32[64,512]{1,0:T(8,128)S(1)}, f32[64,512]{1,0:T(8,128)S(1)}, u32[]{:S(2)}, u32[]{:S(2)}) collective-permute-start(f32[64,512]{1,0:T(8,128)S(1)} %fusion.5), channel_id=1, source_target_pairs={{0,2},{1,3},{2,0},{3,1},{4,6},{5,7},{6,4},{7,5},{8,10},{9,11},{10,... | collective-permute-start | bytes 393224 | tf_op jit(solution)/shard_map/ppermute | solution.py:10
  97.9 1.4 %collective-permute-start.31 = (f32[64,512]{1,0:T(8,128)S(1)}, f32[64,512]{1,0:T(8,128)S(1)}, u32[]{:S(2)}, u32[]{:S(2)}) collective-permute-start(f32[64,512]{1,0:T(8,128)S(1)} %fusion.63), channel_id=1, source_target_pairs={{0,1},{1,0},{2,3},{3,2},{4,5},{5,4},{6,7},{7,6},{8,9},{9,8},{10,11... | collective-permute-start | bytes 393224 | tf_op jit(solution)/shard_map/ppermute | solution.py:10
  98.2 2.8 %collective-permute-start.30 = (f32[64,512]{1,0:T(8,128)S(1)}, f32[64,512]{1,0:T(8,128)S(1)}, u32[]{:S(2)}, u32[]{:S(2)}) collective-permute-start(f32[64,512]{1,0:T(8,128)S(1)} %fusion.62), channel_id=1, source_target_pairs={{0,1},{1,0},{2,3},{3,2},{4,5},{5,4},{6,7},{7,6},{8,9},{9,8},{10,11... | collective-permute-start | bytes 393224 | tf_op jit(solution)/shard_map/ppermute | solution.py:10
  99.5 5.6 %collective-permute-start.32 = (f32[64,512]{1,0:T(8,128)S(1)}, f32[64,512]{1,0:T(8,128)S(1)}, u32[]{:S(2)}, u32[]{:S(2)}) collective-permute-start(f32[64,512]{1,0:T(8,128)S(1)} %convolution_add_fusion.1), channel_id=1, source_target_pairs={{0,2},{1,3},{2,0},{3,1},{4,6},{5,7},{6,4},{7,5},{8,10},{9,11},{10,... | collective-permute-start | bytes 393224 | tf_op jit(solution)/shard_map/ppermute | solution.py:10

commit v5 on v4

--- a/solution.py
+++ b/solution.py
@@ -50,7 +50,7 @@
         total = None
         for m in direct_order(count):
             chunk = chunk_of(m)
-            got = exchanged(chunk, 0, m) if m else chunk
+            got = exchanged(chunk, 0, m) if m else lax.optimization_barrier(chunk)
             total = got if total is None else total + got
         return total
     for m in chunk_order(count):
@@ -76,6 +76,7 @@
             from_leaf = exchanged(near, 1, 0)
             from_both = exchanged(far, 1, step)
             return (near + from_panel) + (from_leaf + from_both)
+        held[0] = lax.optimization_barrier(held[0])
         for m in sorted(held, reverse=True):
             if m & step:
                 arrived[m ^ step] = exchanged(held[m], 0, step)
@@ -83,8 +84,7 @@
 
 
 def direct_order(count):
-    half = count // 2
-    return [m for m in range(half, count)] + [m for m in range(half - 1, -1, -1)]
+    return list(range(count - 1, -1, -1))
 
 
 def exchanged_in_one(panel_count, share):
@@ -143,7 +143,7 @@
     def alive_later():
         total = sum(sizes(height)[2] for height in range(1, levels))
         place = jnp.arange(total)
-        rows = live = jnp.zeros((total,), jnp.int32)
+        rows = fronts = jnp.zeros((total,), jnp.int32)
         start = 0
         for height in range(1, levels):
             group_size, col_width, share, _, _ = sizes(height)
@@ -151,8 +151,10 @@
             first = (leaf_pos % group_size) * col_width + panel_pos * share
             here = place >= start
             rows = jnp.where(here, place - start + first, rows)
-            live = jnp.where(here, lax.dynamic_slice(late_sizes, (front_id,), (1,)), live)
+            fronts = jnp.where(here, front_id, fronts)
             start += share
+        chosen = jnp.arange(late_sizes.shape[0])[:, None] == fronts[None, :]
+        live = jnp.sum(jnp.where(chosen, late_sizes[:, None], 0), axis=0)
         return (rows < live)[None, :]
 
     def right_of(height):
@@ -213,6 +215,9 @@
             )
         solved.append(mine.astype(jnp.bfloat16))
         results.append(mine)
+        if height == levels - 2:
+            early = jnp.stack(results + [jnp.zeros_like(mine)], axis=0)[None]
+            early = lax.optimization_barrier(early)
         for later in range(height + 2, levels):
             _, width, _, start, _ = sizes(later)
             low = start + height * width
@@ -220,7 +225,7 @@
                 solved[-1], tiles[:, low : low + width], preferred_element_type=jnp.float32
             )
             base[later] = lax.optimization_barrier(base[later] + term if later in base else term)
-    return jnp.stack(results, axis=0)[None]
+    return lax.dynamic_update_slice(early, results[-1][None, None], (0, levels - 1, 0, 0))
 
 
 def solution(mesh):

time: 107 us -> 108 us (level)
  matrix products: 24.3 us -> 18.4 us
  waiting for transfers between devices: 25.8 us -> 30.2 us
  other arithmetic: 12.5 us -> 14.1 us
    ppermute x10, waiting for transfers between devices: 7.01 us -> 13.7 us  [exchanged(): lax.ppermute(block, 'leaf', [(i, i ^ leaf_flip) for i in range(leaf_count)])]
    dot_general x12, matrix products: 11.6 us -> 5.76 us  [update(): jnp.dot(solved[-1], couplings[height][m], preferred_element_type=jnp.floa...]
    ppermute x3, waiting for transfers between devices: 4.58 us -> 1.72 us  [exchanged(): lax.ppermute(block, ('leaf', 'panel'), [(i, i ^ flip) for i in range(leaf...]
    lt x1, other arithmetic: 1.9 us -> 0.01 us  [alive_later(): return (rows < live)[None, :]]
    squeeze x3, local copies, waits for them, and re-layouts: 3.21 us -> 4.78 us  [right_of(): return adjoint_rhs[0, :, row_start:row_start + share]]
    dynamic_slice x1 -> x0, local copies, waits for them, and re-layouts: 1.38 us -> none  [alive_later(): lax.dynamic_slice(late_sizes, (front_id,), (1,))]
    ppermute x3, starting transfers between devices: 2.75 us -> 4.05 us  [exchanged(): lax.ppermute(block, ('leaf', 'panel'), [(i, i ^ flip) for i in range(leaf...]
    dynamic_slice x4, local copies, waits for them, and re-layouts: 0.06 us -> 1.32 us  [half(): lax.dynamic_slice(block, ((side ^ flip) * rows, 0), (rows, block.shape[1]))]
  transfers between devices with their start and end apart: 33 -> 33, of which waited for: 17 -> 19; matrix products, arithmetic and copies ran while one was open for 34% -> 33% of each run, Pallas kernels for 0% -> 0%
where the time goes in v5:
time: 108 us; the launch traced here: 107 us
  starting transfers between devices  31.2 us (29%)
  waiting for transfers between devices  30.2 us (28%)
  matrix products  18.4 us (17%)
  other arithmetic  14.1 us (13%)
  local copies, waits for them, and re-layouts  13 us (12%)
    ppermute x20, starting transfers between devices, exchanged(): lax.ppermute(block, 'panel', [(i, i ^ panel_flip) for i in range(panel_co...  15.2 us
    ppermute x20, waiting for transfers between devices, exchanged(): lax.ppermute(block, 'panel', [(i, i ^ panel_flip) for i in range(panel_co...  14.8 us
    ppermute x10, waiting for transfers between devices, exchanged(): lax.ppermute(block, 'leaf', [(i, i ^ leaf_flip) for i in range(leaf_count)])  13.7 us
    ppermute x10, starting transfers between devices, exchanged(): lax.ppermute(block, 'leaf', [(i, i ^ leaf_flip) for i in range(leaf_count)])  11.9 us
    convert_element_type x3, other arithmetic, masked(): return (kept + one).astype(jnp.bfloat16)  7.28 us
    dynamic_slice x3, local copies, waits for them, and re-layouts, coupling(): return lax.dynamic_slice(tiles, (0, low), (tiles.shape[0], share))  6.72 us
    dot_general x12, matrix products, update(): jnp.dot(solved[-1], couplings[height][m], preferred_element_type=jnp.floa...  5.76 us
    dot_general x3, matrix products, per_device(): jnp.dot(solved[-1], tiles[:, low:low + width], preferred_element_type=jnp...  5.66 us
  transfers between devices with their start and end apart: 33, of which 19 were waited for; matrix products, arithmetic and copies ran while one was open for 33% of the time, Pallas kernels for 0%

profile of v5, /device:TPU:0, one launch (start us, length us, event | category | flops | bytes accessed | tf_op | source)
XLA Modules:
  0.0 107.3 jit_solution(10074346257455616204)
XLA Ops:
  0.7 1.3 %fusion.24 = f32[64,2048]{1,0:T(8,128)S(1)} fusion(bf16[1,960,2048]{2,1,0:T(8,128)(2,1)} %param.6, s32[64]{0:T(128)S(1)} %iota_add_fusion.6, f32[1,64,960]{2,1,0:T(8,128)} %param.4, pred[64]{0:T(512)(128)(4,1)S(1)} %broadcast_compare_fusion), kind=kOutput, calls=%fused_computation.55 | convolution fusion | flops 17698816 | bytes 803136 | tf_op jit(solution)/shard_map/dot_general | solution.py:207
  2.1 0.8 pad_maximum_fusion
  3.3 1.5 %slice_bitcast_fusion.2 = f32[64,128]{1,0:T(8,128)} fusion(f32[1,64,960]{2,1,0:T(8,128)} %param.4), kind=kLoop, calls=%fused_computation.99 | loop fusion | bytes 65536 | tf_op jit(solution)/shard_map/squeeze | solution.py:162
  4.9 1.6 %slice_bitcast_fusion.1 = f32[64,256]{1,0:T(8,128)} fusion(f32[1,64,960]{2,1,0:T(8,128)} %param.4), kind=kLoop, calls=%fused_computation.93 | loop fusion | bytes 131072 | tf_op jit(solution)/shard_map/squeeze | solution.py:162
  6.5 1.7 %slice_bitcast_fusion = f32[64,512]{1,0:T(8,128)} fusion(f32[1,64,960]{2,1,0:T(8,128)} %param.4), kind=kLoop, calls=%fused_computation.82 | loop fusion | bytes 262144 | tf_op jit(solution)/shard_map/squeeze | solution.py:162
  8.1 0.7 select_reduce_fusion
  8.9 2.5 %fusion.8 = (bf16[512,512]{1,0:T(8,128)(2,1)S(1)}, bf16[512,512]{1,0:T(8,128)(2,1)S(1)}, bf16[512,512]{1,0:T(8,128)(2,1)S(1)}, bf16[512,512]{1,0:T(8,128)(2,1)S(1)}) fusion(bf16[1,960,2048]{2,1,0:T(8,128)(2,1)} %param.6, s32[]{:T(128)S(6)} %select_n.268, s32[512]{0:T(512)S(1)} %get-tuple-element.91, s32[512]{0:T(512)S(1)} %get-tuple-element.94, ...), kind=kLoop, calls=%fused_computation.24 | loop fusion | flops 7340032 | bytes 4204560 | tf_op jit(solution)/shard_map/convert_element_type | solution.py:126
  11.5 2.2 %fusion.27 = (bf16[128,512]{1,0:T(8,128)(2,1)}, bf16[128,512]{1,0:T(8,128)(2,1)}, bf16[128,512]{1,0:T(8,128)(2,1)}, bf16[128,512]{1,0:T(8,128)(2,1)}) fusion(bf16[1,960,2048]{2,1,0:T(8,128)(2,1)} %param.6, s32[]{:T(128)S(6)} %select_n.268, s32[512]{0:T(512)S(1)} %get-tuple-element.91, s32[128]{0:T(128)S(1)} %iota_add_fusion.5, s32[]{:T(128)S(6)} %select_n.271, ...), kind=kLoop, calls=%fused_computation.59 | loop fusion | flops 1835008 | bytes 1057296 | tf_op jit(solution)/shard_map/convert_element_type | solution.py:126
  13.6 2.1 %dynamic-slice_bitcast_fusion.4 = (bf16[512,256]{1,0:T(8,128)(2,1)}, bf16[512,256]{1,0:T(8,128)(2,1)}, bf16[512,256]{1,0:T(8,128)(2,1)}, bf16[512,256]{1,0:T(8,128)(2,1)S(1)}) fusion(bf16[1,512,8704]{2,1,0:T(8,128)(2,1)} %param.5, s32[]{:T(128)S(6)} %select_n.298, s32[]{:T(128)S(6)} %select_n.297, s32[]{:T(128)S(6)} %select_n.296, s32[]{:T(128)S(6)} %select_n.295), kind=kLoop, calls=%fused_computation.69 | loop fusion | bytes 2097168 | tf_op jit(solution)/shard_map/dynamic_slice | solution.py:137
  15.7 2.7 %dynamic-slice_bitcast_fusion = (bf16[512,512]{1,0:T(8,128)(2,1)}, bf16[512,512]{1,0:T(8,128)(2,1)}, bf16[512,512]{1,0:T(8,128)(2,1)S(1)}, bf16[512,512]{1,0:T(8,128)(2,1)S(1)}) fusion(bf16[1,512,8704]{2,1,0:T(8,128)(2,1)} %param.5, s32[]{:T(128)S(6)} %select_n.311, s32[]{:T(128)S(6)} %select_n.309, s32[]{:T(128)S(6)} %select_n.308, s32[]{:T(128)S(6)} %select_n.310), kind=kLoop, calls=%fused_computation.47 | loop fusion | bytes 4194320 | tf_op jit(solution)/shard_map/dynamic_slice | solution.py:137
  18.5 2.6 %fusion.16 = (bf16[256,512]{1,0:T(8,128)(2,1)}, bf16[256,512]{1,0:T(8,128)(2,1)}, bf16[256,512]{1,0:T(8,128)(2,1)}, bf16[256,512]{1,0:T(8,128)(2,1)}) fusion(bf16[1,960,2048]{2,1,0:T(8,128)(2,1)} %param.6, s32[]{:T(128)S(6)} %select_n.268, s32[512]{0:T(512)S(1)} %get-tuple-element.91, s32[256]{0:T(256)S(1)} %iota_add_fusion.4, s32[]{:T(128)S(6)} %select_n.271, ...), kind=kLoop, calls=%fused_computation.37 | loop fusion | flops 3670016 | bytes 2106384 | tf_op jit(solution)/shard_map/convert_element_type | solution.py:126
  21.0 1.1 %slice_add_fusion = (f32[64,512]{1,0:T(8,128)S(1)}, f32[64,512]{1,0:T(8,128)S(1)}) fusion(f32[64,1024]{1,0:T(8,128)} %collective-permute-done, f32[64,2048]{1,0:T(8,128)} %copy-done.9, s32[]{:T(128)S(6)} %select_n.271, s32[]{:T(128)S(6)} %select_n.267), kind=kLoop, calls=%fused_computation.76 | loop fusion | flops 65536 | bytes 786440 | tf_op jit(solution)/shard_map/add | solution.py:66
  22.2 0.7 constant_dynamic-slice_fusion.5
  22.8 2.5 %collective-permute-start.1 = (f32[32,512]{1,0:T(8,128)}, f32[32,512]{1,0:T(8,128)}, u32[]{:S(2)}, u32[]{:S(2)}) collective-permute-start(f32[32,512]{1,0:T(8,128)} %get-tuple-element.89), channel_id=1, source_target_pairs={{0,2},{1,3},{2,0},{3,1},{4,6},{5,7},{6,4},{7,5},{8,10},{9,11},{10,... | collective-permute-start | bytes 196616 | tf_op jit(solution)/shard_map/ppermute | solution.py:10
  25.3 1.4 %collective-permute-start.3 = (f32[32,512]{1,0:T(8,128)}, f32[32,512]{1,0:T(8,128)}, u32[]{:S(2)}, u32[]{:S(2)}) collective-permute-start(f32[32,512]{1,0:T(8,128)} %get-tuple-element.90), channel_id=1, source_target_pairs={{0,6},{1,7},{2,4},{3,5},{4,2},{5,3},{6,0},{7,1},{8,14},{9,15},{10,... | collective-permute-start | bytes 196616 | tf_op jit(solution)/shard_map/ppermute | solution.py:14
  27.5 1.9 %dynamic-slice_bitcast_fusion.8 = (bf16[512,128]{1,0:T(8,128)(2,1)}, bf16[512,128]{1,0:T(8,128)(2,1)}, bf16[512,128]{1,0:T(8,128)(2,1)}, bf16[512,128]{1,0:T(8,128)(2,1)}) fusion(bf16[1,512,8704]{2,1,0:T(8,128)(2,1)} %param.5, s32[]{:T(128)S(6)} %select_n.287, s32[]{:T(128)S(6)} %select_n.286, s32[]{:T(128)S(6)} %select_n.285, s32[]{:T(128)S(6)} %select_n.284), kind=kLoop, calls=%fused_computation.84 | loop fusion | bytes 1048592 | tf_op jit(solution)/shard_map/dynamic_slice | solution.py:137
  29.5 1.3 %collective-permute-done.3 = f32[32,512]{1,0:T(8,128)} collective-permute-done((f32[32,512]{1,0:T(8,128)}, f32[32,512]{1,0:T(8,128)}, u32[]{:S(2)}, u32[]{:S(2)}) %collective-permute-start.3) | collective-permute-done | bytes 65568 | tf_op jit(solution)/shard_map/ppermute | solution.py:14
  30.8 1.2 %collective-permute-done.2 = f32[32,512]{1,0:T(8,128)} collective-permute-done((f32[32,512]{1,0:T(8,128)}, f32[32,512]{1,0:T(8,128)}, u32[]{:S(2)}, u32[]{:S(2)}) %collective-permute-start.2) | collective-permute-done | bytes 65568 | tf_op jit(solution)/shard_map/ppermute | solution.py:12
  32.0 0.9 add_add_fusion.2
  32.9 2.7 %collective-permute-start.4 = (f32[32,512]{1,0:T(8,128)S(1)}, f32[32,512]{1,0:T(8,128)S(1)}, u32[]{:S(2)}, u32[]{:S(2)}) collective-permute-start(f32[32,512]{1,0:T(8,128)S(1)} %add_add_fusion.2), channel_id=1, source_target_pairs={{0,16},{4,20},{8,24},{12,28},{16,0},{20,4},{24,8},{28,12},{1,17},{... | collective-permute-start | bytes 196616 | tf_op jit(solution)/shard_map/ppermute | solution.py:12
  35.6 2.6 %collective-permute-done.4 = f32[32,512]{1,0:T(8,128)S(1)} collective-permute-done((f32[32,512]{1,0:T(8,128)S(1)}, f32[32,512]{1,0:T(8,128)S(1)}, u32[]{:S(2)}, u32[]{:S(2)}) %collective-permute-start.4) | collective-permute-done | bytes 65568 | tf_op jit(solution)/shard_map/ppermute | solution.py:12
  38.1 1.6 %collective-permute-start.5 = (f32[32,512]{1,0:T(8,128)S(1)}, f32[32,512]{1,0:T(8,128)S(1)}, u32[]{:S(2)}, u32[]{:S(2)}) collective-permute-start(f32[32,512]{1,0:T(8,128)S(1)} %add.534), channel_id=1, source_target_pairs={{0,8},{4,12},{8,0},{12,4},{16,24},{20,28},{24,16},{28,20},{1,9},{5... | collective-permute-start | bytes 196616 | tf_op jit(solution)/shard_map/ppermute | solution.py:12
  39.8 0.9 collective-permute-start.6
  40.7 1.0 collective-permute-start.7
  41.7 0.9 collective-permute-done.5
  42.6 1.5 %collective-permute-done.6 = f32[32,512]{1,0:T(8,128)S(1)} collective-permute-done((f32[32,512]{1,0:T(8,128)S(1)}, f32[32,512]{1,0:T(8,128)S(1)}, u32[]{:S(2)}, u32[]{:S(2)}) %collective-permute-start.6) | collective-permute-done | bytes 65568 | tf_op jit(solution)/shard_map/ppermute | solution.py:12
  44.1 1.8 %collective-permute-done.7 = f32[32,512]{1,0:T(8,128)S(1)} collective-permute-done((f32[32,512]{1,0:T(8,128)S(1)}, f32[32,512]{1,0:T(8,128)S(1)}, u32[]{:S(2)}, u32[]{:S(2)}) %collective-permute-start.7) | collective-permute-done | bytes 65568 | tf_op jit(solution)/shard_map/ppermute | solution.py:12
  45.9 1.1 fusion.49
  47.0 1.5 %collective-permute-start.9 = (f32[64,128]{1,0:T(8,128)S(1)}, f32[64,128]{1,0:T(8,128)S(1)}, u32[]{:S(2)}, u32[]{:S(2)}) collective-permute-start(f32[64,128]{1,0:T(8,128)S(1)} %fusion.49), channel_id=1, source_target_pairs={{0,2},{1,3},{2,0},{3,1},{4,6},{5,7},{6,4},{7,5},{8,10},{9,11},{10,... | collective-permute-start | bytes 98312 | tf_op jit(solution)/shard_map/ppermute | solution.py:10
  48.4 1.1 fusion.48
  49.6 1.1 fusion.50
  50.6 0.8 collective-permute-start.10
  51.4 2.1 %fusion.1 = f32[64,2048]{1,0:T(8,128)S(1)} fusion(bf16[64,512]{1,0:T(8,128)(2,1)S(1)} %fusion.39, bf16[512,8704]{1,0:T(8,128)(2,1)} %bitcast.138), kind=kOutput, calls=%fused_computation.2 | convolution fusion | flops 134217728 | bytes 2686976 | tf_op jit(solution)/shard_map/dot_general | solution.py:224
  53.5 1.1 %fusion.51 = f32[64,128]{1,0:T(8,128)S(1)} fusion(bf16[64,512]{1,0:T(8,128)(2,1)S(1)} %fusion.39, bf16[512,128]{1,0:T(8,128)(2,1)} %get-tuple-element.32), kind=kOutput, calls=%fused_computation.138 | convolution fusion | flops 8388608 | bytes 229376 | tf_op jit(solution)/shard_map/dot_general | solution.py:198
  54.6 0.8 select_convert_fusion.2
  55.4 1.0 fusion.53
  56.5 1.0 fusion.52
  58.1 1.0 convolution_add_fusion.7
  59.2 1.5 %collective-permute-start.13 = (f32[32,512]{1,0:T(8,128)S(1)}, f32[32,512]{1,0:T(8,128)S(1)}, u32[]{:S(2)}, u32[]{:S(2)}) collective-permute-start(f32[32,512]{1,0:T(8,128)S(1)} %get-tuple-element.87), channel_id=1, source_target_pairs={{0,2},{1,3},{2,0},{3,1},{4,6},{5,7},{6,4},{7,5},{8,10},{9,11},{10,... | collective-permute-start | bytes 196616 | tf_op jit(solution)/shard_map/ppermute | solution.py:10
  60.7 1.2 %collective-permute-start.15 = (f32[32,512]{1,0:T(8,128)S(1)}, f32[32,512]{1,0:T(8,128)S(1)}, u32[]{:S(2)}, u32[]{:S(2)}) collective-permute-start(f32[32,512]{1,0:T(8,128)S(1)} %get-tuple-element.88), channel_id=1, source_target_pairs={{0,6},{1,7},{2,4},{3,5},{4,2},{5,3},{6,0},{7,1},{8,14},{9,15},{10,... | collective-permute-start | bytes 196616 | tf_op jit(solution)/shard_map/ppermute | solution.py:14
  61.9 1.1 convolution_add_fusion.8
  62.9 1.0 collective-permute-start.14
  63.9 1.5 %fusion.5 = f32[64,1024]{1,0:T(8,128)S(1)} fusion(bf16[64,512]{1,0:T(8,128)(2,1)S(1)} %fusion.39, bf16[512,8704]{1,0:T(8,128)(2,1)} %bitcast.139), kind=kOutput, calls=%fused_computation.20 | convolution fusion | flops 67108864 | bytes 1376256 | tf_op jit(solution)/shard_map/dot_general | solution.py:224
  65.8 1.4 %collective-permute-done.14 = f32[32,512]{1,0:T(8,128)S(1)} collective-permute-done((f32[32,512]{1,0:T(8,128)S(1)}, f32[32,512]{1,0:T(8,128)S(1)}, u32[]{:S(2)}, u32[]{:S(2)}) %collective-permute-start.14) | collective-permute-done | bytes 65568 | tf_op jit(solution)/shard_map/ppermute | solution.py:12
  67.8 1.1 %collective-permute-start.17 = (f32[32,512]{1,0:T(8,128)S(1)}, f32[32,512]{1,0:T(8,128)S(1)}, u32[]{:S(2)}, u32[]{:S(2)}) collective-permute-start(f32[32,512]{1,0:T(8,128)S(1)} %add_add_fusion.1), channel_id=1, source_target_pairs={{0,4},{4,0},{8,12},{12,8},{16,20},{20,16},{24,28},{28,24},{1,5},{5... | collective-permute-start | bytes 196616 | tf_op jit(solution)/shard_map/ppermute | solution.py:12
  68.9 2.0 %collective-permute-start.18 = (f32[32,512]{1,0:T(8,128)S(1)}, f32[32,512]{1,0:T(8,128)S(1)}, u32[]{:S(2)}, u32[]{:S(2)}) collective-permute-start(f32[32,512]{1,0:T(8,128)S(1)} %add_add_fusion.1), channel_id=1, source_target_pairs={{0,12},{4,8},{8,4},{12,0},{16,28},{20,24},{24,20},{28,16},{1,13},{... | collective-permute-start | bytes 196616 | tf_op jit(solution)/shard_map/ppermute | solution.py:12
  70.9 0.8 collective-permute-done.16
  72.1 2.0 %collective-permute-done.18 = f32[32,512]{1,0:T(8,128)S(1)} collective-permute-done((f32[32,512]{1,0:T(8,128)S(1)}, f32[32,512]{1,0:T(8,128)S(1)}, u32[]{:S(2)}, u32[]{:S(2)}) %collective-permute-start.18) | collective-permute-done | bytes 65568 | tf_op jit(solution)/shard_map/ppermute | solution.py:12
  74.3 1.6 %collective-permute-start.20 = (f32[64,256]{1,0:T(8,128)S(1)}, f32[64,256]{1,0:T(8,128)S(1)}, u32[]{:S(2)}, u32[]{:S(2)}) collective-permute-start(f32[64,256]{1,0:T(8,128)S(1)} %convolution_add_fusion.13), channel_id=1, source_target_pairs={{0,2},{1,3},{2,0},{3,1},{4,6},{5,7},{6,4},{7,5},{8,10},{9,11},{10,... | collective-permute-start | bytes 196616 | tf_op jit(solution)/shard_map/ppermute | solution.py:10
  76.3 0.7 collective-permute-start.21
  77.1 1.5 %collective-permute-done.20 = f32[64,256]{1,0:T(8,128)S(1)} collective-permute-done((f32[64,256]{1,0:T(8,128)S(1)}, f32[64,256]{1,0:T(8,128)S(1)}, u32[]{:S(2)}, u32[]{:S(2)}) %collective-permute-start.20) | collective-permute-done | bytes 65568 | tf_op jit(solution)/shard_map/ppermute | solution.py:10
  78.6 1.4 %collective-permute-done.19 = f32[64,256]{1,0:T(8,128)S(1)} collective-permute-done((f32[64,256]{1,0:T(8,128)S(1)}, f32[64,256]{1,0:T(8,128)S(1)}, u32[]{:S(2)}, u32[]{:S(2)}) %collective-permute-start.19) | collective-permute-done | bytes 65568 | tf_op jit(solution)/shard_map/ppermute | solution.py:10
  81.8 1.0 collective-permute-start.24
  82.8 1.4 %collective-permute-start.26 = (f32[64,512]{1,0:T(8,128)S(1)}, f32[64,512]{1,0:T(8,128)S(1)}, u32[]{:S(2)}, u32[]{:S(2)}) collective-permute-start(f32[64,512]{1,0:T(8,128)S(1)} %convolution_add_fusion.9), channel_id=1, source_target_pairs={{0,6},{1,7},{2,4},{3,5},{4,2},{5,3},{6,0},{7,1},{8,14},{9,15},{10,... | collective-permute-start | bytes 393224 | tf_op jit(solution)/shard_map/ppermute | solution.py:14
  84.4 1.1 %collective-permute-start.25 = (f32[64,512]{1,0:T(8,128)S(1)}, f32[64,512]{1,0:T(8,128)S(1)}, u32[]{:S(2)}, u32[]{:S(2)}) collective-permute-start(f32[64,512]{1,0:T(8,128)S(1)} %convolution_add_fusion.10), channel_id=1, source_target_pairs={{0,4},{4,0},{8,12},{12,8},{16,20},{20,16},{24,28},{28,24},{1,5},{5... | collective-permute-start | bytes 393224 | tf_op jit(solution)/shard_map/ppermute | solution.py:12
  85.6 2.1 %convolution_add_fusion = f32[64,2048]{1,0:T(8,128)S(1)} fusion(f32[64,2048]{1,0:T(8,128)S(1)} %fusion.1, bf16[64,512]{1,0:T(8,128)(2,1)S(1)} %fusion.37, bf16[512,8704]{1,0:T(8,128)(2,1)} %bitcast.140), kind=kOutput, calls=%fused_computation | convolution fusion | flops 134348800 | bytes 3211264 | tf_op jit(solution)/shard_map/dot_general | solution.py:224
  87.7 2.5 %collective-permute-done.24 = f32[64,512]{1,0:T(8,128)S(1)} collective-permute-done((f32[64,512]{1,0:T(8,128)S(1)}, f32[64,512]{1,0:T(8,128)S(1)}, u32[]{:S(2)}, u32[]{:S(2)}) %collective-permute-start.24) | collective-permute-done | bytes 131104 | tf_op jit(solution)/shard_map/ppermute | solution.py:10
  90.2 1.2 %collective-permute-done.25 = f32[64,512]{1,0:T(8,128)S(1)} collective-permute-done((f32[64,512]{1,0:T(8,128)S(1)}, f32[64,512]{1,0:T(8,128)S(1)}, u32[]{:S(2)}, u32[]{:S(2)}) %collective-permute-start.25) | collective-permute-done | bytes 131104 | tf_op jit(solution)/shard_map/ppermute | solution.py:12
  92.6 0.9 maximum_bitcast_fusion
  93.7 1.3 %collective-permute-start.29 = (f32[64,512]{1,0:T(8,128)S(1)}, f32[64,512]{1,0:T(8,128)S(1)}, u32[]{:S(2)}, u32[]{:S(2)}) collective-permute-start(f32[64,512]{1,0:T(8,128)S(1)} %fusion.3), channel_id=1, source_target_pairs={{0,2},{1,3},{2,0},{3,1},{4,6},{5,7},{6,4},{7,5},{8,10},{9,11},{10,... | collective-permute-start | bytes 393224 | tf_op jit(solution)/shard_map/ppermute | solution.py:10
  95.2 4.0 %collective-permute-done.29 = f32[64,512]{1,0:T(8,128)S(1)} collective-permute-done((f32[64,512]{1,0:T(8,128)S(1)}, f32[64,512]{1,0:T(8,128)S(1)}, u32[]{:S(2)}, u32[]{:S(2)}) %collective-permute-start.29) | collective-permute-done | bytes 131104 | tf_op jit(solution)/shard_map/ppermute | solution.py:10
  101.0 1.3 %collective-permute-start.32 = (f32[64,512]{1,0:T(8,128)S(1)}, f32[64,512]{1,0:T(8,128)S(1)}, u32[]{:S(2)}, u32[]{:S(2)}) collective-permute-start(f32[64,512]{1,0:T(8,128)S(1)} %convolution_add_fusion.1), channel_id=1, source_target_pairs={{0,2},{1,3},{2,0},{3,1},{4,6},{5,7},{6,4},{7,5},{8,10},{9,11},{10,... | collective-permute-start | bytes 393224 | tf_op jit(solution)/shard_map/ppermute | solution.py:10
  102.5 4.1 %collective-permute-done.32 = f32[64,512]{1,0:T(8,128)S(1)} collective-permute-done((f32[64,512]{1,0:T(8,128)S(1)}, f32[64,512]{1,0:T(8,128)S(1)}, u32[]{:S(2)}, u32[]{:S(2)}) %collective-permute-start.32) | collective-permute-done | bytes 131104 | tf_op jit(solution)/shard_map/ppermute | solution.py:10
  106.7 0.7 bitcast_dynamic-update-slice_fusion
  (98 shorter events, 10.5 us)
Async XLA Ops:
  2.0 6.9 %copy-start.9 = (f32[64,2048]{1,0:T(8,128)}, f32[64,2048]{1,0:T(8,128)S(1)}, u32[]{:S(2)}) copy-start(f32[64,2048]{1,0:T(8,128)S(1)} %fusion.24) | copy-start | bytes 1572868
  2.9 18.2 %collective-permute-start = (f32[64,1024]{1,0:T(8,128)}, f32[64,1024]{1,0:T(8,128)}, u32[]{:S(2)}, u32[]{:S(2)}) collective-permute-start(f32[64,1024]{1,0:T(8,128)} %pad_maximum_fusion), channel_id=1, source_target_pairs={{0,1},{1,0},{2,3},{3,2},{4,5},{5,4},{6,7},{7,6},{8,9},{9,8},{10,11... | collective-permute-start | bytes 786440 | tf_op jit(solution)/shard_map/ppermute | solution.py:10
  22.8 6.7 %collective-permute-start.1 = (f32[32,512]{1,0:T(8,128)}, f32[32,512]{1,0:T(8,128)}, u32[]{:S(2)}, u32[]{:S(2)}) collective-permute-start(f32[32,512]{1,0:T(8,128)} %get-tuple-element.89), channel_id=1, source_target_pairs={{0,2},{1,3},{2,0},{3,1},{4,6},{5,7},{6,4},{7,5},{8,10},{9,11},{10,... | collective-permute-start | bytes 196616 | tf_op jit(solution)/shard_map/ppermute | solution.py:10
  25.3 5.5 %collective-permute-start.3 = (f32[32,512]{1,0:T(8,128)}, f32[32,512]{1,0:T(8,128)}, u32[]{:S(2)}, u32[]{:S(2)}) collective-permute-start(f32[32,512]{1,0:T(8,128)} %get-tuple-element.90), channel_id=1, source_target_pairs={{0,6},{1,7},{2,4},{3,5},{4,2},{5,3},{6,0},{7,1},{8,14},{9,15},{10,... | collective-permute-start | bytes 196616 | tf_op jit(solution)/shard_map/ppermute | solution.py:14
  27.4 4.6 %collective-permute-start.2 = (f32[32,512]{1,0:T(8,128)}, f32[32,512]{1,0:T(8,128)}, u32[]{:S(2)}, u32[]{:S(2)}) collective-permute-start(f32[32,512]{1,0:T(8,128)} %constant_dynamic-slice_fusion.4), channel_id=1, source_target_pairs={{0,4},{4,0},{8,12},{12,8},{16,20},{20,16},{24,28},{28,24},{1,5},{5... | collective-permute-start | bytes 196616 | tf_op jit(solution)/shard_map/ppermute | solution.py:12
  29.4 44.7 %copy-start.4 = (bf16[512,256]{1,0:T(8,128)(2,1)S(1)}, bf16[512,256]{1,0:T(8,128)(2,1)}, u32[]{:S(2)}) copy-start(bf16[512,256]{1,0:T(8,128)(2,1)} %get-tuple-element.38) | copy-start | bytes 786436
  29.4 46.5 %copy-start.3 = (bf16[512,256]{1,0:T(8,128)(2,1)S(1)}, bf16[512,256]{1,0:T(8,128)(2,1)}, u32[]{:S(2)}) copy-start(bf16[512,256]{1,0:T(8,128)(2,1)} %get-tuple-element.37) | copy-start | bytes 786436
  29.4 46.7 %copy-start.2 = (bf16[512,256]{1,0:T(8,128)(2,1)S(1)}, bf16[512,256]{1,0:T(8,128)(2,1)}, u32[]{:S(2)}) copy-start(bf16[512,256]{1,0:T(8,128)(2,1)} %get-tuple-element.39) | copy-start | bytes 786436
  29.4 50.6 %copy-start.11 = (f32[64,256]{1,0:T(8,128)S(1)}, f32[64,256]{1,0:T(8,128)}, u32[]{:S(2)}) copy-start(f32[64,256]{1,0:T(8,128)} %slice_bitcast_fusion.1) | copy-start | bytes 196612
  29.4 50.7 %copy-start.8 = (bf16[256,512]{1,0:T(8,128)(2,1)S(1)}, bf16[256,512]{1,0:T(8,128)(2,1)}, u32[]{:S(2)}) copy-start(bf16[256,512]{1,0:T(8,128)(2,1)} %get-tuple-element.44) | copy-start | bytes 786436
  29.4 50.9 %copy-start.7 = (bf16[256,512]{1,0:T(8,128)(2,1)S(1)}, bf16[256,512]{1,0:T(8,128)(2,1)}, u32[]{:S(2)}) copy-start(bf16[256,512]{1,0:T(8,128)(2,1)} %get-tuple-element.42) | copy-start | bytes 786436
  29.4 52.2 %copy-start.6 = (bf16[256,512]{1,0:T(8,128)(2,1)S(1)}, bf16[256,512]{1,0:T(8,128)(2,1)}, u32[]{:S(2)}) copy-start(bf16[256,512]{1,0:T(8,128)(2,1)} %get-tuple-element.43) | copy-start | bytes 786436
  29.4 54.9 %copy-start.5 = (bf16[256,512]{1,0:T(8,128)(2,1)S(1)}, bf16[256,512]{1,0:T(8,128)(2,1)}, u32[]{:S(2)}) copy-start(bf16[256,512]{1,0:T(8,128)(2,1)} %get-tuple-element.41) | copy-start | bytes 786436
  29.4 62.1 %copy-start.1 = (bf16[512,512]{1,0:T(8,128)(2,1)S(1)}, bf16[512,512]{1,0:T(8,128)(2,1)}, u32[]{:S(2)}) copy-start(bf16[512,512]{1,0:T(8,128)(2,1)} %get-tuple-element.48) | copy-start | bytes 1572868
  32.9 5.2 %collective-permute-start.4 = (f32[32,512]{1,0:T(8,128)S(1)}, f32[32,512]{1,0:T(8,128)S(1)}, u32[]{:S(2)}, u32[]{:S(2)}) collective-permute-start(f32[32,512]{1,0:T(8,128)S(1)} %add_add_fusion.2), channel_id=1, source_target_pairs={{0,16},{4,20},{8,24},{12,28},{16,0},{20,4},{24,8},{28,12},{1,17},{... | collective-permute-start | bytes 196616 | tf_op jit(solution)/shard_map/ppermute | solution.py:12
  38.1 4.4 %collective-permute-start.5 = (f32[32,512]{1,0:T(8,128)S(1)}, f32[32,512]{1,0:T(8,128)S(1)}, u32[]{:S(2)}, u32[]{:S(2)}) collective-permute-start(f32[32,512]{1,0:T(8,128)S(1)} %add.534), channel_id=1, source_target_pairs={{0,8},{4,12},{8,0},{12,4},{16,24},{20,28},{24,16},{28,20},{1,9},{5... | collective-permute-start | bytes 196616 | tf_op jit(solution)/shard_map/ppermute | solution.py:12
  39.8 4.3 %collective-permute-start.6 = (f32[32,512]{1,0:T(8,128)S(1)}, f32[32,512]{1,0:T(8,128)S(1)}, u32[]{:S(2)}, u32[]{:S(2)}) collective-permute-start(f32[32,512]{1,0:T(8,128)S(1)} %add.534), channel_id=1, source_target_pairs={{0,4},{4,0},{8,12},{12,8},{16,20},{20,16},{24,28},{28,24},{1,5},{5... | collective-permute-start | bytes 196616 | tf_op jit(solution)/shard_map/ppermute | solution.py:12
  40.7 5.2 %collective-permute-start.7 = (f32[32,512]{1,0:T(8,128)S(1)}, f32[32,512]{1,0:T(8,128)S(1)}, u32[]{:S(2)}, u32[]{:S(2)}) collective-permute-start(f32[32,512]{1,0:T(8,128)S(1)} %add.534), channel_id=1, source_target_pairs={{0,12},{4,8},{8,4},{12,0},{16,28},{20,24},{24,20},{28,16},{1,13},{... | collective-permute-start | bytes 196616 | tf_op jit(solution)/shard_map/ppermute | solution.py:12
  41.7 50.1 %copy-start = (bf16[512,512]{1,0:T(8,128)(2,1)S(1)}, bf16[512,512]{1,0:T(8,128)(2,1)}, u32[]{:S(2)}) copy-start(bf16[512,512]{1,0:T(8,128)(2,1)} %get-tuple-element.46) | copy-start | bytes 1572868
  47.0 7.6 %collective-permute-start.9 = (f32[64,128]{1,0:T(8,128)S(1)}, f32[64,128]{1,0:T(8,128)S(1)}, u32[]{:S(2)}, u32[]{:S(2)}) collective-permute-start(f32[64,128]{1,0:T(8,128)S(1)} %fusion.49), channel_id=1, source_target_pairs={{0,2},{1,3},{2,0},{3,1},{4,6},{5,7},{6,4},{7,5},{8,10},{9,11},{10,... | collective-permute-start | bytes 98312 | tf_op jit(solution)/shard_map/ppermute | solution.py:10
  49.5 5.1 %collective-permute-start.8 = (f32[64,128]{1,0:T(8,128)S(1)}, f32[64,128]{1,0:T(8,128)S(1)}, u32[]{:S(2)}, u32[]{:S(2)}) collective-permute-start(f32[64,128]{1,0:T(8,128)S(1)} %fusion.48), channel_id=1, source_target_pairs={{0,3},{1,2},{2,1},{3,0},{4,7},{5,6},{6,5},{7,4},{8,11},{9,10},{10,... | collective-permute-start | bytes 98312 | tf_op jit(solution)/shard_map/ppermute | solution.py:10
  50.6 4.0 %collective-permute-start.10 = (f32[64,128]{1,0:T(8,128)S(1)}, f32[64,128]{1,0:T(8,128)S(1)}, u32[]{:S(2)}, u32[]{:S(2)}) collective-permute-start(f32[64,128]{1,0:T(8,128)S(1)} %fusion.50), channel_id=1, source_target_pairs={{0,1},{1,0},{2,3},{3,2},{4,5},{5,4},{6,7},{7,6},{8,9},{9,8},{10,11... | collective-permute-start | bytes 98312 | tf_op jit(solution)/shard_map/ppermute | solution.py:10
  53.5 45.7 %copy-start.10 = (f32[64,512]{1,0:T(8,128)S(1)}, f32[64,512]{1,0:T(8,128)}, u32[]{:S(2)}) copy-start(f32[64,512]{1,0:T(8,128)} %slice_bitcast_fusion) | copy-start | bytes 393220
  56.4 1.7 %collective-permute-start.12 = (f32[64,512]{1,0:T(8,128)S(1)}, f32[64,512]{1,0:T(8,128)S(1)}, u32[]{:S(2)}, u32[]{:S(2)}) collective-permute-start(f32[64,512]{1,0:T(8,128)S(1)} %fusion.53), channel_id=1, source_target_pairs={{0,1},{1,0},{2,3},{3,2},{4,5},{5,4},{6,7},{7,6},{8,9},{9,8},{10,11... | collective-permute-start | bytes 393224 | tf_op jit(solution)/shard_map/ppermute | solution.py:10
  57.6 4.3 %collective-permute-start.11 = (f32[64,512]{1,0:T(8,128)S(1)}, f32[64,512]{1,0:T(8,128)S(1)}, u32[]{:S(2)}, u32[]{:S(2)}) collective-permute-start(f32[64,512]{1,0:T(8,128)S(1)} %fusion.52), channel_id=1, source_target_pairs={{0,1},{1,0},{2,3},{3,2},{4,5},{5,4},{6,7},{7,6},{8,9},{9,8},{10,11... | collective-permute-start | bytes 393224 | tf_op jit(solution)/shard_map/ppermute | solution.py:10
  59.2 6.2 %collective-permute-start.13 = (f32[32,512]{1,0:T(8,128)S(1)}, f32[32,512]{1,0:T(8,128)S(1)}, u32[]{:S(2)}, u32[]{:S(2)}) collective-permute-start(f32[32,512]{1,0:T(8,128)S(1)} %get-tuple-element.87), channel_id=1, source_target_pairs={{0,2},{1,3},{2,0},{3,1},{4,6},{5,7},{6,4},{7,5},{8,10},{9,11},{10,... | collective-permute-start | bytes 196616 | tf_op jit(solution)/shard_map/ppermute | solution.py:10
  60.7 5.2 %collective-permute-start.15 = (f32[32,512]{1,0:T(8,128)S(1)}, f32[32,512]{1,0:T(8,128)S(1)}, u32[]{:S(2)}, u32[]{:S(2)}) collective-permute-start(f32[32,512]{1,0:T(8,128)S(1)} %get-tuple-element.88), channel_id=1, source_target_pairs={{0,6},{1,7},{2,4},{3,5},{4,2},{5,3},{6,0},{7,1},{8,14},{9,15},{10,... | collective-permute-start | bytes 196616 | tf_op jit(solution)/shard_map/ppermute | solution.py:14
  62.9 4.3 %collective-permute-start.14 = (f32[32,512]{1,0:T(8,128)S(1)}, f32[32,512]{1,0:T(8,128)S(1)}, u32[]{:S(2)}, u32[]{:S(2)}) collective-permute-start(f32[32,512]{1,0:T(8,128)S(1)} %constant_dynamic-slice_fusion.1), channel_id=1, source_target_pairs={{0,4},{4,0},{8,12},{12,8},{16,20},{20,16},{24,28},{28,24},{1,5},{5... | collective-permute-start | bytes 196616 | tf_op jit(solution)/shard_map/ppermute | solution.py:12
  67.3 4.3 %collective-permute-start.16 = (f32[32,512]{1,0:T(8,128)S(1)}, f32[32,512]{1,0:T(8,128)S(1)}, u32[]{:S(2)}, u32[]{:S(2)}) collective-permute-start(f32[32,512]{1,0:T(8,128)S(1)} %add_add_fusion.1), channel_id=1, source_target_pairs={{0,8},{4,12},{8,0},{12,4},{16,24},{20,28},{24,16},{28,20},{1,9},{5... | collective-permute-start | bytes 196616 | tf_op jit(solution)/shard_map/ppermute | solution.py:12
  67.8 4.3 %collective-permute-start.17 = (f32[32,512]{1,0:T(8,128)S(1)}, f32[32,512]{1,0:T(8,128)S(1)}, u32[]{:S(2)}, u32[]{:S(2)}) collective-permute-start(f32[32,512]{1,0:T(8,128)S(1)} %add_add_fusion.1), channel_id=1, source_target_pairs={{0,4},{4,0},{8,12},{12,8},{16,20},{20,16},{24,28},{28,24},{1,5},{5... | collective-permute-start | bytes 196616 | tf_op jit(solution)/shard_map/ppermute | solution.py:12
  68.9 5.2 %collective-permute-start.18 = (f32[32,512]{1,0:T(8,128)S(1)}, f32[32,512]{1,0:T(8,128)S(1)}, u32[]{:S(2)}, u32[]{:S(2)}) collective-permute-start(f32[32,512]{1,0:T(8,128)S(1)} %add_add_fusion.1), channel_id=1, source_target_pairs={{0,12},{4,8},{8,4},{12,0},{16,28},{20,24},{24,20},{28,16},{1,13},{... | collective-permute-start | bytes 196616 | tf_op jit(solution)/shard_map/ppermute | solution.py:12
  74.3 4.3 %collective-permute-start.20 = (f32[64,256]{1,0:T(8,128)S(1)}, f32[64,256]{1,0:T(8,128)S(1)}, u32[]{:S(2)}, u32[]{:S(2)}) collective-permute-start(f32[64,256]{1,0:T(8,128)S(1)} %convolution_add_fusion.13), channel_id=1, source_target_pairs={{0,2},{1,3},{2,0},{3,1},{4,6},{5,7},{6,4},{7,5},{8,10},{9,11},{10,... | collective-permute-start | bytes 196616 | tf_op jit(solution)/shard_map/ppermute | solution.py:10
  76.0 4.0 %collective-permute-start.19 = (f32[64,256]{1,0:T(8,128)S(1)}, f32[64,256]{1,0:T(8,128)S(1)}, u32[]{:S(2)}, u32[]{:S(2)}) collective-permute-start(f32[64,256]{1,0:T(8,128)S(1)} %convolution_add_fusion.14), channel_id=1, source_target_pairs={{0,3},{1,2},{2,1},{3,0},{4,7},{5,6},{6,5},{7,4},{8,11},{9,10},{10,... | collective-permute-start | bytes 196616 | tf_op jit(solution)/shard_map/ppermute | solution.py:10
  76.3 3.7 %collective-permute-start.21 = (f32[64,256]{1,0:T(8,128)S(1)}, f32[64,256]{1,0:T(8,128)S(1)}, u32[]{:S(2)}, u32[]{:S(2)}) collective-permute-start(f32[64,256]{1,0:T(8,128)S(1)} %convolution_add_fusion.12), channel_id=1, source_target_pairs={{0,1},{1,0},{2,3},{3,2},{4,5},{5,4},{6,7},{7,6},{8,9},{9,8},{10,11... | collective-permute-start | bytes 196616 | tf_op jit(solution)/shard_map/ppermute | solution.py:10
  80.2 1.4 %collective-permute-start.23 = (f32[64,512]{1,0:T(8,128)S(1)}, f32[64,512]{1,0:T(8,128)S(1)}, u32[]{:S(2)}, u32[]{:S(2)}) collective-permute-start(f32[64,512]{1,0:T(8,128)S(1)} %fusion.55), channel_id=1, source_target_pairs={{0,1},{1,0},{2,3},{3,2},{4,5},{5,4},{6,7},{7,6},{8,9},{9,8},{10,11... | collective-permute-start | bytes 393224 | tf_op jit(solution)/shard_map/ppermute | solution.py:10
  80.5 3.8 %collective-permute-start.22 = (f32[64,512]{1,0:T(8,128)S(1)}, f32[64,512]{1,0:T(8,128)S(1)}, u32[]{:S(2)}, u32[]{:S(2)}) collective-permute-start(f32[64,512]{1,0:T(8,128)S(1)} %fusion.54), channel_id=1, source_target_pairs={{0,1},{1,0},{2,3},{3,2},{4,5},{5,4},{6,7},{7,6},{8,9},{9,8},{10,11... | collective-permute-start | bytes 393224 | tf_op jit(solution)/shard_map/ppermute | solution.py:10
  81.8 8.4 %collective-permute-start.24 = (f32[64,512]{1,0:T(8,128)S(1)}, f32[64,512]{1,0:T(8,128)S(1)}, u32[]{:S(2)}, u32[]{:S(2)}) collective-permute-start(f32[64,512]{1,0:T(8,128)S(1)} %convolution_add_fusion.9), channel_id=1, source_target_pairs={{0,2},{1,3},{2,0},{3,1},{4,6},{5,7},{6,4},{7,5},{8,10},{9,11},{10,... | collective-permute-start | bytes 393224 | tf_op jit(solution)/shard_map/ppermute | solution.py:10
  82.8 7.4 %collective-permute-start.26 = (f32[64,512]{1,0:T(8,128)S(1)}, f32[64,512]{1,0:T(8,128)S(1)}, u32[]{:S(2)}, u32[]{:S(2)}) collective-permute-start(f32[64,512]{1,0:T(8,128)S(1)} %convolution_add_fusion.9), channel_id=1, source_target_pairs={{0,6},{1,7},{2,4},{3,5},{4,2},{5,3},{6,0},{7,1},{8,14},{9,15},{10,... | collective-permute-start | bytes 393224 | tf_op jit(solution)/shard_map/ppermute | solution.py:14
  84.4 7.0 %collective-permute-start.25 = (f32[64,512]{1,0:T(8,128)S(1)}, f32[64,512]{1,0:T(8,128)S(1)}, u32[]{:S(2)}, u32[]{:S(2)}) collective-permute-start(f32[64,512]{1,0:T(8,128)S(1)} %convolution_add_fusion.10), channel_id=1, source_target_pairs={{0,4},{4,0},{8,12},{12,8},{16,20},{20,16},{24,28},{28,24},{1,5},{5... | collective-permute-start | bytes 393224 | tf_op jit(solution)/shard_map/ppermute | solution.py:12
  91.7 1.8 %collective-permute-start.28 = (f32[64,512]{1,0:T(8,128)S(1)}, f32[64,512]{1,0:T(8,128)S(1)}, u32[]{:S(2)}, u32[]{:S(2)}) collective-permute-start(f32[64,512]{1,0:T(8,128)S(1)} %convolution_add_fusion.3), channel_id=1, source_target_pairs={{0,1},{1,0},{2,3},{3,2},{4,5},{5,4},{6,7},{7,6},{8,9},{9,8},{10,11... | collective-permute-start | bytes 393224 | tf_op jit(solution)/shard_map/ppermute | solution.py:10
  92.0 2.9 %collective-permute-start.27 = (f32[64,512]{1,0:T(8,128)S(1)}, f32[64,512]{1,0:T(8,128)S(1)}, u32[]{:S(2)}, u32[]{:S(2)}) collective-permute-start(f32[64,512]{1,0:T(8,128)S(1)} %convolution_add_fusion.5), channel_id=1, source_target_pairs={{0,1},{1,0},{2,3},{3,2},{4,5},{5,4},{6,7},{7,6},{8,9},{9,8},{10,11... | collective-permute-start | bytes 393224 | tf_op jit(solution)/shard_map/ppermute | solution.py:10
  93.7 5.5 %collective-permute-start.29 = (f32[64,512]{1,0:T(8,128)S(1)}, f32[64,512]{1,0:T(8,128)S(1)}, u32[]{:S(2)}, u32[]{:S(2)}) collective-permute-start(f32[64,512]{1,0:T(8,128)S(1)} %fusion.3), channel_id=1, source_target_pairs={{0,2},{1,3},{2,0},{3,1},{4,6},{5,7},{6,4},{7,5},{8,10},{9,11},{10,... | collective-permute-start | bytes 393224 | tf_op jit(solution)/shard_map/ppermute | solution.py:10
  99.4 1.4 %collective-permute-start.31 = (f32[64,512]{1,0:T(8,128)S(1)}, f32[64,512]{1,0:T(8,128)S(1)}, u32[]{:S(2)}, u32[]{:S(2)}) collective-permute-start(f32[64,512]{1,0:T(8,128)S(1)} %fusion.57), channel_id=1, source_target_pairs={{0,1},{1,0},{2,3},{3,2},{4,5},{5,4},{6,7},{7,6},{8,9},{9,8},{10,11... | collective-permute-start | bytes 393224 | tf_op jit(solution)/shard_map/ppermute | solution.py:10
  99.7 2.6 %collective-permute-start.30 = (f32[64,512]{1,0:T(8,128)S(1)}, f32[64,512]{1,0:T(8,128)S(1)}, u32[]{:S(2)}, u32[]{:S(2)}) collective-permute-start(f32[64,512]{1,0:T(8,128)S(1)} %fusion.56), channel_id=1, source_target_pairs={{0,1},{1,0},{2,3},{3,2},{4,5},{5,4},{6,7},{7,6},{8,9},{9,8},{10,11... | collective-permute-start | bytes 393224 | tf_op jit(solution)/shard_map/ppermute | solution.py:10
  101.0 5.6 %collective-permute-start.32 = (f32[64,512]{1,0:T(8,128)S(1)}, f32[64,512]{1,0:T(8,128)S(1)}, u32[]{:S(2)}, u32[]{:S(2)}) collective-permute-start(f32[64,512]{1,0:T(8,128)S(1)} %convolution_add_fusion.1), channel_id=1, source_target_pairs={{0,2},{1,3},{2,0},{3,1},{4,6},{5,7},{6,4},{7,5},{8,10},{9,11},{10,... | collective-permute-start | bytes 393224 | tf_op jit(solution)/shard_map/ppermute | solution.py:10
